TPU v7x, 32 devices: a whole 2x2x4 slice. The times are simulated.
32 devices in a mesh: fsdp: 4 (over y, x), ctx: 8 (over z, core).
Axes of the slice: x: 2, y: 2, z: 4, core: 2. Of those that a mesh axis runs over, the one named last changes fastest.
Arguments:
- tokens: bfloat16 [8192, 768], P(('fsdp', 'ctx')), may hold values from -6 to 6
- frames: bfloat16 [12000, 768], P(('fsdp', 'ctx')), may hold values from -6 to 6
- document_starts: int32 [4, 2], P('fsdp'), may hold values from 0 to 1279, as said below
- cotangent: bfloat16 [8192, 768], P(('fsdp', 'ctx')), may hold values from -6 to 6
- gain_self: bfloat16 [768], P(('fsdp', 'ctx')), may hold values from 0.25 to 1.75
- gain_cross: bfloat16 [768], P(('fsdp', 'ctx')), may hold values from 0.25 to 1.75
- gain_feed: bfloat16 [768], P(('fsdp', 'ctx')), may hold values from 0.25 to 1.75
- gain_final: bfloat16 [768], P(('fsdp', 'ctx')), may hold values from 0.25 to 1.75
- self_query: bfloat16 [768, 768], P(('fsdp', 'ctx')), may hold values from -0.21875 to 0.21875
- self_key: bfloat16 [768, 768], P(('fsdp', 'ctx')), may hold values from -0.21875 to 0.21875
- self_value: bfloat16 [768, 768], P(('fsdp', 'ctx')), may hold values from -0.21875 to 0.21875
- self_output: bfloat16 [768, 768], P(('fsdp', 'ctx')), may hold values from -1.25 to 1.25
- cross_query: bfloat16 [768, 768], P(('fsdp', 'ctx')), may hold values from -0.21875 to 0.21875
- cross_key: bfloat16 [768, 768], P(('fsdp', 'ctx')), may hold values from -0.21875 to 0.21875
- cross_value: bfloat16 [768, 768], P(('fsdp', 'ctx')), may hold values from -0.21875 to 0.21875
- cross_output: bfloat16 [768, 768], P(('fsdp', 'ctx')), may hold values from -1.75 to 1.75
- feed_up: bfloat16 [768, 3072], P(('fsdp', 'ctx')), may hold values from -0.21875 to 0.21875
- feed_down: bfloat16 [3072, 768], P(('fsdp', 'ctx')), may hold values from -0.109375 to 0.109375
Outputs:
- layer_output: bfloat16 [8192, 768], P(('fsdp', 'ctx'))
- tokens_gradient: float32 [8192, 768], P(('fsdp', 'ctx'))
- frames_gradient: float32 [12000, 768], P(('fsdp', 'ctx'))
- gain_self_gradient: float32 [768], P(('fsdp', 'ctx'))
- gain_cross_gradient: float32 [768], P(('fsdp', 'ctx'))
- gain_feed_gradient: float32 [768], P(('fsdp', 'ctx'))
- gain_final_gradient: float32 [768], P(('fsdp', 'ctx'))
- self_query_gradient: float32 [768, 768], P(('fsdp', 'ctx'))
- self_key_gradient: float32 [768, 768], P(('fsdp', 'ctx'))
- self_value_gradient: float32 [768, 768], P(('fsdp', 'ctx'))
- self_output_gradient: float32 [768, 768], P(('fsdp', 'ctx'))
- cross_query_gradient: float32 [768, 768], P(('fsdp', 'ctx'))
- cross_key_gradient: float32 [768, 768], P(('fsdp', 'ctx'))
- cross_value_gradient: float32 [768, 768], P(('fsdp', 'ctx'))
- cross_output_gradient: float32 [768, 768], P(('fsdp', 'ctx'))
- feed_up_gradient: float32 [768, 3072], P(('fsdp', 'ctx'))
- feed_down_gradient: float32 [3072, 768], P(('fsdp', 'ctx'))
Inputs may be any that keep to these rules, and one draw needn't show every extreme that they name: `document_starts`: document k of a sequence starts at position k * 1024 plus an offset in 0 to 255. The first document's offset is 0 and the last document's is exactly 255.
All inputs are finite; a program needn't handle non-finite values.
Results may differ from a plain program's by a relative error of at most 0.02.
Values may be sent and summed in bfloat16 or wider, within the bound.
No kernel may reach another device: no remote copies, remote signals or barrier semaphores. Data moves between devices by JAX's collectives and lax.ppermute only.
A program may use at most 256 MiB of HBM per device.

v0:
```python
import jax
import jax.numpy as jnp
from jax import lax
from jax.sharding import PartitionSpec as P

D = 768
HEAD_DIM = 64
FF = 3072
FRAMES = 1500
SELF_REACH = 5
CROSS_BACK = 4
CROSS_FWD = 3


floor_score = -1e30


def from_behind(value, axis, steps):
    count = lax.axis_size(axis)
    first, last = (max(0, -steps), min(count, count - steps))
    return lax.ppermute(value, axis, [(source, source + steps) for source in range(first, last)])


def normalize(states, gain):
    center = states - jnp.mean(states, axis=-1, keepdims=True)
    spread = jnp.mean(center * center, axis=-1, keepdims=True)
    return center * lax.rsqrt(spread + 1e-05) * gain


def exact_gelu(values):
    return jax.nn.gelu(values, approximate=False)


def product(left, right):
    return jnp.dot(left, right, preferred_element_type=jnp.float32)


def product_left(left, right):
    return lax.dot_general(
        left, right, (((0,), (0,)), ((), ())), preferred_element_type=jnp.float32
    )


def product_right(left, right):
    return lax.dot_general(
        left, right, (((1,), (1,)), ((), ())), preferred_element_type=jnp.float32
    )


def flat_rows(matrix):
    return matrix.reshape(-1, 128)


def unflat(matrix, width):
    return matrix.reshape(-1, width)


def documents_of(places, starts):
    return jnp.sum((starts[None, :] <= places[:, None]).astype(jnp.int32), axis=1) - 1


def frame_documents(device, count):
    return jnp.floor_divide(device * count + jnp.arange(count, dtype=jnp.int32), FRAMES)


def group_columns():
    return 256


def split_heads(block, start, columns):
    part = lax.slice_in_dim(block, start, start + columns, axis=1)
    return part.reshape(block.shape[0], columns // HEAD_DIM, HEAD_DIM)


def head_scores(query_heads, key_heads):
    scores = jnp.einsum("qhd,khd->hqk", query_heads, key_heads, preferred_element_type=jnp.float32)
    return scores * HEAD_DIM ** (-0.5)


def piece_stats(operands):
    query_heads, key_heads, allowed = operands
    scores = jnp.where(allowed[None], head_scores(query_heads, key_heads), -jnp.inf)
    highest = jnp.maximum(jnp.max(scores, axis=2), floor_score)
    return (highest, jnp.sum(jnp.exp(scores - highest[:, :, None]), axis=2))


def piece_mix(operands):
    query_heads, key_heads, value_heads, allowed, log_total = operands
    scores = jnp.where(allowed[None], head_scores(query_heads, key_heads), -jnp.inf)
    weights = jnp.exp(scores - log_total[:, :, None]).astype(jnp.bfloat16)
    return jnp.einsum("hqk,khd->qhd", weights, value_heads, preferred_element_type=jnp.float32)


def piece_back(operands):
    query_heads, key_heads, value_heads, allowed, log_total, grad_heads, row_offset = operands
    scores = jnp.where(allowed[None], head_scores(query_heads, key_heads), -jnp.inf)
    probs = jnp.exp(scores - log_total[:, :, None])
    grad_probs = jnp.einsum(
        "qhd,khd->hqk", grad_heads, value_heads, preferred_element_type=jnp.float32
    )
    grad_scores = (probs * (grad_probs - row_offset[:, :, None])).astype(jnp.bfloat16)
    factor = HEAD_DIM ** (-0.5)
    grad_query = (
        jnp.einsum("hqk,khd->qhd", grad_scores, key_heads, preferred_element_type=jnp.float32)
        * factor
    )
    grad_key = (
        jnp.einsum("hqk,qhd->khd", grad_scores, query_heads, preferred_element_type=jnp.float32)
        * factor
    )
    grad_value = jnp.einsum(
        "hqk,qhd->khd", probs.astype(jnp.bfloat16), grad_heads, preferred_element_type=jnp.float32
    )
    return (grad_query, grad_key, grad_value)


def attention_forward(queries, pieces, masks, flags):
    rows = queries.shape[0]
    columns = group_columns()
    heads = columns // HEAD_DIM
    mixed_parts = []
    log_totals = []
    for start in range(0, queries.shape[1], columns):
        query_heads = split_heads(queries, start, columns)
        key_list = [split_heads(piece[0], start, columns) for piece in pieces]
        value_list = [split_heads(piece[1], start, columns) for piece in pieces]
        highest = jnp.full((heads, rows), floor_score, jnp.float32)
        totals = jnp.zeros((heads, rows), jnp.float32)
        for key_heads, allowed, flag in zip(key_list, masks, flags):
            piece_high, piece_total = piece_stats((query_heads, key_heads, allowed))
            new_high = jnp.maximum(highest, piece_high)
            totals = totals * jnp.exp(highest - new_high) + piece_total * jnp.exp(
                piece_high - new_high
            )
            highest = new_high
        log_total = highest + jnp.log(totals)
        empty_mix = jnp.zeros((rows, heads, HEAD_DIM), jnp.float32)
        mixed = empty_mix
        for key_heads, value_heads, allowed, flag in zip(key_list, value_list, masks, flags):
            mixed = mixed + piece_mix((query_heads, key_heads, value_heads, allowed, log_total))
        mixed_parts.append(mixed.reshape(rows, columns))
        log_totals.append(log_total)
    return (jnp.concatenate(mixed_parts, axis=1), log_totals)


def attention_backward(queries, pieces, masks, flags, mixed, log_totals, grad_mixed):
    rows = queries.shape[0]
    columns = group_columns()
    heads = columns // HEAD_DIM
    query_parts = []
    key_parts = [[] for piece in pieces]
    value_parts = [[] for piece in pieces]
    for group, start in enumerate(range(0, queries.shape[1], columns)):
        query_heads = split_heads(queries, start, columns)
        grad_heads = split_heads(grad_mixed, start, columns)
        row_offset = jnp.einsum(
            "qhd,qhd->hq", grad_heads.astype(jnp.float32), split_heads(mixed, start, columns)
        )
        grad_query = jnp.zeros((rows, heads, HEAD_DIM), jnp.float32)
        for number, (piece, allowed, flag) in enumerate(zip(pieces, masks, flags)):
            count = piece[0].shape[0]
            key_heads = split_heads(piece[0], start, columns)
            value_heads = split_heads(piece[1], start, columns)
            part_query, part_key, part_value = piece_back(
                (
                    query_heads,
                    key_heads,
                    value_heads,
                    allowed,
                    log_totals[group],
                    grad_heads,
                    row_offset,
                )
            )
            grad_query = grad_query + part_query
            key_parts[number].append(part_key.reshape(count, columns))
            value_parts[number].append(part_value.reshape(count, columns))
        query_parts.append(grad_query.reshape(rows, columns))
    return (
        jnp.concatenate(query_parts, axis=1),
        [jnp.concatenate(parts, axis=1) for parts in key_parts],
        [jnp.concatenate(parts, axis=1) for parts in value_parts],
    )


def shards(
    tokens,
    frames,
    document_starts,
    cotangent,
    gain_self,
    gain_cross,
    gain_feed,
    gain_final,
    self_query,
    self_key,
    self_value,
    self_output,
    cross_query,
    cross_key,
    cross_value,
    cross_output,
    feed_up,
    feed_down,
):
    (
        gain_self,
        gain_cross,
        gain_feed,
        gain_final,
        self_query,
        self_key,
        self_value,
        self_output,
        cross_query,
        cross_key,
        cross_value,
        cross_output,
        feed_up,
        feed_down,
    ) = (
        lax.all_gather(gain_self, ("fsdp", "ctx"), axis=0, tiled=True),
        lax.all_gather(gain_cross, ("fsdp", "ctx"), axis=0, tiled=True),
        lax.all_gather(gain_feed, ("fsdp", "ctx"), axis=0, tiled=True),
        lax.all_gather(gain_final, ("fsdp", "ctx"), axis=0, tiled=True),
        lax.all_gather(self_query, ("fsdp", "ctx"), axis=0, tiled=True),
        lax.all_gather(self_key, ("fsdp", "ctx"), axis=0, tiled=True),
        lax.all_gather(self_value, ("fsdp", "ctx"), axis=0, tiled=True),
        lax.all_gather(self_output, ("fsdp", "ctx"), axis=0, tiled=True),
        lax.all_gather(cross_query, ("fsdp", "ctx"), axis=0, tiled=True),
        lax.all_gather(cross_key, ("fsdp", "ctx"), axis=0, tiled=True),
        lax.all_gather(cross_value, ("fsdp", "ctx"), axis=0, tiled=True),
        lax.all_gather(cross_output, ("fsdp", "ctx"), axis=0, tiled=True),
        lax.all_gather(feed_up, ("fsdp", "ctx"), axis=0, tiled=True),
        lax.all_gather(feed_down, ("fsdp", "ctx"), axis=0, tiled=True),
    )
    rows = tokens.shape[0]
    frame_rows = frames.shape[0]
    starts = document_starts[0]
    device = lax.axis_index("ctx")
    places = device * rows + jnp.arange(rows, dtype=jnp.int32)
    token_docs = documents_of(places, starts)
    states = tokens.astype(jnp.float32)
    normed_self, back_self = jax.vjp(normalize, states, gain_self.astype(jnp.float32))
    normed_self = normed_self.astype(jnp.bfloat16)
    queries = product(normed_self, self_query).astype(jnp.bfloat16)
    keys = product(normed_self, self_key).astype(jnp.bfloat16)
    values = product(normed_self, self_value).astype(jnp.bfloat16)
    self_pieces = [(keys, values)]
    self_masks = [
        (token_docs[:, None] == token_docs[None, :]) & (places[None, :] <= places[:, None])
    ]
    for step in range(1, SELF_REACH + 1):
        self_pieces.append(from_behind((keys, values), "ctx", step))
        earlier = documents_of(places - step * rows, starts)
        self_masks.append(token_docs[:, None] == earlier[None, :])
    self_flags = [jnp.any(allowed) for allowed in self_masks]
    self_mixed, self_logs = attention_forward(queries, self_pieces, self_masks, self_flags)
    self_heads = self_mixed.astype(jnp.bfloat16)
    first_sum = states + product(self_heads, self_output)
    normed_cross, back_cross = jax.vjp(normalize, first_sum, gain_cross.astype(jnp.float32))
    normed_cross = normed_cross.astype(jnp.bfloat16)
    cross_queries = product(normed_cross, cross_query).astype(jnp.bfloat16)
    frame_keys = product(frames, cross_key).astype(jnp.bfloat16)
    frame_values = product(frames, cross_value).astype(jnp.bfloat16)
    shifts = [offset for offset in range(-CROSS_FWD, CROSS_BACK + 1) if offset != 0]
    cross_pieces = [(frame_keys, frame_values)]
    for offset in shifts:
        cross_pieces.append(from_behind((frame_keys, frame_values), "ctx", offset))
    cross_masks = [
        token_docs[:, None] == frame_documents(device - offset, frame_rows)[None, :]
        for offset in [0] + shifts
    ]
    cross_flags = [jnp.any(allowed) for allowed in cross_masks]
    cross_mixed, cross_logs = attention_forward(
        cross_queries, cross_pieces, cross_masks, cross_flags
    )
    cross_heads = cross_mixed.astype(jnp.bfloat16)
    second_sum = first_sum + product(cross_heads, cross_output)
    normed_feed, back_feed = jax.vjp(normalize, second_sum, gain_feed.astype(jnp.float32))
    normed_feed = normed_feed.astype(jnp.bfloat16)
    inner = product(normed_feed, feed_up)
    activated, back_gelu = jax.vjp(exact_gelu, inner)
    hidden = activated.astype(jnp.bfloat16)
    third_sum = second_sum + product(hidden, feed_down)
    result, back_final = jax.vjp(normalize, third_sum, gain_final.astype(jnp.float32))
    grad_third, grad_gain_final = back_final(cotangent.astype(jnp.float32))
    grad_feed_out = grad_third.astype(jnp.bfloat16)
    grad_feed_down = product_left(hidden, grad_feed_out)
    (grad_inner,) = back_gelu(product_right(grad_feed_out, feed_down))
    grad_inner = grad_inner.astype(jnp.bfloat16)
    grad_feed_up = product_left(normed_feed, grad_inner)
    grad_second_part, grad_gain_feed = back_feed(product_right(grad_inner, feed_up))
    grad_second = grad_third + grad_second_part
    grad_cross_out = grad_second.astype(jnp.bfloat16)
    grad_cross_output = product_left(cross_heads, grad_cross_out)
    grad_cross_heads = product_right(grad_cross_out, cross_output).astype(jnp.bfloat16)
    grad_cross_queries, cross_key_parts, cross_value_parts = attention_backward(
        cross_queries,
        cross_pieces,
        cross_masks,
        cross_flags,
        cross_mixed,
        cross_logs,
        grad_cross_heads,
    )
    grad_cross_queries = grad_cross_queries.astype(jnp.bfloat16)
    grad_cross_query = product_left(normed_cross, grad_cross_queries)
    grad_first_part, grad_gain_cross = back_cross(product_right(grad_cross_queries, cross_query))
    grad_first = grad_second + grad_first_part
    frame_key_total = cross_key_parts[0]
    frame_value_total = cross_value_parts[0]
    for number, offset in enumerate(shifts):
        back_key, back_value = (
            from_behind(cross_key_parts[number + 1].astype(jnp.bfloat16), "ctx", -offset).astype(
                jnp.float32
            ),
            from_behind(cross_value_parts[number + 1].astype(jnp.bfloat16), "ctx", -offset).astype(
                jnp.float32
            ),
        )
        frame_key_total = frame_key_total + back_key
        frame_value_total = frame_value_total + back_value
    frame_key_grad = frame_key_total.astype(jnp.bfloat16)
    frame_value_grad = frame_value_total.astype(jnp.bfloat16)
    grad_cross_key = product_left(frames, frame_key_grad)
    grad_cross_value = product_left(frames, frame_value_grad)
    frames_gradient = product_right(frame_key_grad, cross_key) + product_right(
        frame_value_grad, cross_value
    )
    grad_self_out = grad_first.astype(jnp.bfloat16)
    grad_self_output = product_left(self_heads, grad_self_out)
    grad_self_heads = product_right(grad_self_out, self_output).astype(jnp.bfloat16)
    grad_queries, self_key_parts, self_value_parts = attention_backward(
        queries, self_pieces, self_masks, self_flags, self_mixed, self_logs, grad_self_heads
    )
    key_total = self_key_parts[0]
    value_total = self_value_parts[0]
    for step in range(1, SELF_REACH + 1):
        back_key, back_value = (
            from_behind(self_key_parts[step].astype(jnp.bfloat16), "ctx", -step).astype(
                jnp.float32
            ),
            from_behind(self_value_parts[step].astype(jnp.bfloat16), "ctx", -step).astype(
                jnp.float32
            ),
        )
        key_total = key_total + back_key
        value_total = value_total + back_value
    grad_queries = grad_queries.astype(jnp.bfloat16)
    grad_keys = key_total.astype(jnp.bfloat16)
    grad_values = value_total.astype(jnp.bfloat16)
    grad_self_query = product_left(normed_self, grad_queries)
    grad_self_key = product_left(normed_self, grad_keys)
    grad_self_value = product_left(normed_self, grad_values)
    grad_normed_self = (
        product_right(grad_queries, self_query)
        + product_right(grad_keys, self_key)
        + product_right(grad_values, self_value)
    )
    grad_states_part, grad_gain_self = back_self(grad_normed_self)
    tokens_gradient = grad_first + grad_states_part
    weight_sums = (
        lax.psum_scatter(grad_gain_self, ("fsdp", "ctx"), scatter_dimension=0, tiled=True),
        lax.psum_scatter(grad_gain_cross, ("fsdp", "ctx"), scatter_dimension=0, tiled=True),
        lax.psum_scatter(grad_gain_feed, ("fsdp", "ctx"), scatter_dimension=0, tiled=True),
        lax.psum_scatter(grad_gain_final, ("fsdp", "ctx"), scatter_dimension=0, tiled=True),
        lax.psum_scatter(
            flat_rows(grad_self_query), ("fsdp", "ctx"), scatter_dimension=0, tiled=True
        ),
        lax.psum_scatter(
            flat_rows(grad_self_key), ("fsdp", "ctx"), scatter_dimension=0, tiled=True
        ),
        lax.psum_scatter(
            flat_rows(grad_self_value), ("fsdp", "ctx"), scatter_dimension=0, tiled=True
        ),
        lax.psum_scatter(
            flat_rows(grad_self_output), ("fsdp", "ctx"), scatter_dimension=0, tiled=True
        ),
        lax.psum_scatter(
            flat_rows(grad_cross_query), ("fsdp", "ctx"), scatter_dimension=0, tiled=True
        ),
        lax.psum_scatter(
            flat_rows(grad_cross_key), ("fsdp", "ctx"), scatter_dimension=0, tiled=True
        ),
        lax.psum_scatter(
            flat_rows(grad_cross_value), ("fsdp", "ctx"), scatter_dimension=0, tiled=True
        ),
        lax.psum_scatter(
            flat_rows(grad_cross_output), ("fsdp", "ctx"), scatter_dimension=0, tiled=True
        ),
        lax.psum_scatter(flat_rows(grad_feed_up), ("fsdp", "ctx"), scatter_dimension=0, tiled=True),
        lax.psum_scatter(
            flat_rows(grad_feed_down), ("fsdp", "ctx"), scatter_dimension=0, tiled=True
        ),
    )
    return (
        result.astype(jnp.bfloat16),
        tokens_gradient,
        frames_gradient,
        weight_sums[0],
        weight_sums[1],
        weight_sums[2],
        weight_sums[3],
        unflat(weight_sums[4], D),
        unflat(weight_sums[5], D),
        unflat(weight_sums[6], D),
        unflat(weight_sums[7], D),
        unflat(weight_sums[8], D),
        unflat(weight_sums[9], D),
        unflat(weight_sums[10], D),
        unflat(weight_sums[11], D),
        unflat(weight_sums[12], FF),
        unflat(weight_sums[13], D),
    )


def solution(mesh):
    in_specs = (
        P(("fsdp", "ctx"), None),
        P(("fsdp", "ctx"), None),
        P("fsdp", None),
        P(("fsdp", "ctx"), None),
        P(("fsdp", "ctx")),
        P(("fsdp", "ctx")),
        P(("fsdp", "ctx")),
        P(("fsdp", "ctx")),
        P(("fsdp", "ctx"), None),
        P(("fsdp", "ctx"), None),
        P(("fsdp", "ctx"), None),
        P(("fsdp", "ctx"), None),
        P(("fsdp", "ctx"), None),
        P(("fsdp", "ctx"), None),
        P(("fsdp", "ctx"), None),
        P(("fsdp", "ctx"), None),
        P(("fsdp", "ctx"), None),
        P(("fsdp", "ctx"), None),
    )
    out_specs = (
        P(("fsdp", "ctx"), None),
        P(("fsdp", "ctx"), None),
        P(("fsdp", "ctx"), None),
        P(("fsdp", "ctx")),
        P(("fsdp", "ctx")),
        P(("fsdp", "ctx")),
        P(("fsdp", "ctx")),
        P(("fsdp", "ctx"), None),
        P(("fsdp", "ctx"), None),
        P(("fsdp", "ctx"), None),
        P(("fsdp", "ctx"), None),
        P(("fsdp", "ctx"), None),
        P(("fsdp", "ctx"), None),
        P(("fsdp", "ctx"), None),
        P(("fsdp", "ctx"), None),
        P(("fsdp", "ctx"), None),
        P(("fsdp", "ctx"), None),
    )
    return jax.shard_map(shards, mesh=mesh, in_specs=in_specs, out_specs=out_specs, check_vma=False)
```

profile of v0, /device:TPU:0, one launch (start us, length us, event | category | flops | bytes accessed | tf_op | source)
XLA Modules:
  0.0 2021.4 jit_solution(2753573366372425311)
XLA Ops:
  17.5 42.2 %all-reduce.9 = (bf16[768]{0:T(1024)(128)(2,1)S(1)}, bf16[768]{0:T(1024)(128)(2,1)S(1)}, bf16[768]{0:T(1024)(128)(2,1)S(1)}, bf16[768]{0:T(1024)(128)(2,1)S(1)}) all-reduce(bf16[768]{0:T(1024)(128)(2,1)S(1)} %dynamic-update-slice, bf16[768]{0:T(1024)(128)(2,1)S(1)} %dynamic-update-slice.1, ...), channel_id=1, replica_groups=mesh['fsdp'=4,'ctx'=8] {'fsdp','ctx'}, use_global_device_ids=true, to_apply=%add | all-reduce | flops 3072 | bytes 12288
  84.6 51.0 %all-gather.11.cloned.1.call-done = bf16[768,768]{1,0:T(8,128)(2,1)} async-done(((bf16[24,768]{1,0:T(8,128)(2,1)}), bf16[768,768]{1,0:T(8,128)(2,1)}) %all-gather.11.cloned.1.call-update) | async-done | bytes 1179664 | tf_op jit(solution)/shard_map/all_gather | solution.py:228
  143.4 51.0 %all-gather.13.cloned.1.call-done = bf16[768,768]{1,0:T(8,128)(2,1)} async-done(((bf16[24,768]{1,0:T(8,128)(2,1)}), bf16[768,768]{1,0:T(8,128)(2,1)}) %all-gather.13.cloned.1.call-update) | async-done | bytes 1179664 | tf_op jit(solution)/shard_map/all_gather | solution.py:226
  202.8 47.6 %all-gather.23.cloned.1.call-done = bf16[768,768]{1,0:T(8,128)(2,1)} async-done(((bf16[24,768]{1,0:T(8,128)(2,1)}), bf16[768,768]{1,0:T(8,128)(2,1)}) %all-gather.23.cloned.1.call-update) | async-done | bytes 1179664 | tf_op jit(solution)/shard_map/all_gather | solution.py:231
  255.1 51.2 %all-gather.19.cloned.1.call-done = bf16[768,768]{1,0:T(8,128)(2,1)} async-done(((bf16[24,768]{1,0:T(8,128)(2,1)}), bf16[768,768]{1,0:T(8,128)(2,1)}) %all-gather.19.cloned.1.call-update) | async-done | bytes 1179664 | tf_op jit(solution)/shard_map/all_gather | solution.py:232
  371.3 5.5 collective-permute-start.15
  385.5 9.4 collective-permute-start.14
  402.5 18.6 collective-permute-start.13
  505.1 12.6 exponential_reduce_fusion.15
  532.6 8.3 collective-permute-start.22
  547.9 6.0 collective-permute-start.21
  650.0 8.4 collective-permute-done.17
  665.7 10.7 collective-permute-done.18
  730.0 11.7 multiply_convert_fusion
  741.7 4.6 fusion.568
  1038.3 9.7 collective-permute-start.36
  1069.8 30.8 %collective-permute-done.40 = bf16[375,768]{1,0:T(8,128)(2,1)} collective-permute-done((bf16[375,768]{1,0:T(8,128)(2,1)}, bf16[375,768]{1,0:T(8,128)(2,1)}, u32[]{:S(2)}, u32[]{:S(2)}) %collective-permute-start.40) | collective-permute-done | bytes 576032 | tf_op jit(solution)/shard_map/ppermute | solution.py:21
  1100.6 13.3 collective-permute-start.35
  1187.3 4.8 collective-permute-start.42
  1192.0 7.1 collective-permute-start.41
  1209.0 8.0 collective-permute-done.41
  1229.6 6.5 fusion.478
  1236.1 11.0 reshape.2352
  1248.2 6.5 fusion.475
  1254.7 10.8 reshape.2354
  1271.8 50.5 %all-reduce.8 = (f32[768]{0:T(1024)S(1)}, f32[768]{0:T(1024)S(1)}, f32[768]{0:T(1024)S(1)}, f32[768]{0:T(1024)S(1)}) all-reduce(f32[768]{0:T(1024)S(1)} %get-tuple-element.21, f32[768]{0:T(1024)S(1)} %get-tuple-element.19, f32[768]{0:T(1024)S(1)} %copy-done.557, ...), channel_id=2, replica_groups=mesh['fsdp'=4,'ctx'=8] {'fsdp','ctx'}, use_global_device_ids=true, to_apply=%region_107.108.clone | all-reduce | flops 3072 | bytes 24576
  1336.1 82.8 %reduce-scatter.13.cloned.1.call-done = f32[144,128]{1,0:T(8,128)} async-done(((f32[4608,128]{1,0:T(8,128)}), f32[144,128]{1,0:T(8,128)}) %reduce-scatter.13.cloned.1.call-update) | async-done | bytes 73744 | tf_op jit(solution)/shard_map/reduce_scatter | solution.py:371
  1420.4 102.3 %reduce-scatter.15.cloned.1.call-done = f32[144,128]{1,0:T(8,128)} async-done(((f32[4608,128]{1,0:T(8,128)}), f32[144,128]{1,0:T(8,128)}) %reduce-scatter.15.cloned.1.call-update) | async-done | bytes 73744 | tf_op jit(solution)/shard_map/reduce_scatter | solution.py:374
  1524.2 102.3 %reduce-scatter.21.cloned.1.call-done = f32[144,128]{1,0:T(8,128)} async-done(((f32[4608,128]{1,0:T(8,128)}), f32[144,128]{1,0:T(8,128)}) %reduce-scatter.21.cloned.1.call-update) | async-done | bytes 73744 | tf_op jit(solution)/shard_map/reduce_scatter | solution.py:383
  1628.0 102.2 %reduce-scatter.23.cloned.1.call-done = f32[144,128]{1,0:T(8,128)} async-done(((f32[4608,128]{1,0:T(8,128)}), f32[144,128]{1,0:T(8,128)}) %reduce-scatter.23.cloned.1.call-update) | async-done | bytes 73744 | tf_op jit(solution)/shard_map/reduce_scatter | solution.py:386
  1731.7 139.6 %reduce-scatter.27.cloned.1.call-done = f32[576,128]{1,0:T(8,128)} async-done(((f32[18432,128]{1,0:T(8,128)}), f32[576,128]{1,0:T(8,128)}) %reduce-scatter.27.cloned.1.call-update) | async-done | bytes 294928 | tf_op jit(solution)/shard_map/reduce_scatter | solution.py:392
  1873.1 139.5 %reduce-scatter.29.cloned.1.call-done = f32[576,128]{1,0:T(8,128)} async-done(((f32[18432,128]{1,0:T(8,128)}), f32[576,128]{1,0:T(8,128)}) %reduce-scatter.29.cloned.1.call-update) | async-done | bytes 294928 | tf_op jit(solution)/shard_map/reduce_scatter | solution.py:393
  (1918 shorter events, 835.1 us)
Async XLA Ops:
  7.9 127.6 %all-gather.11.cloned.1.call-start = ((), (), s32[]{:S(2)}) async-start(), calls=%async_computation.10 | async-start | bytes 1216512 | tf_op jit(solution)/shard_map/all_gather | solution.py:228
  8.7 185.8 %all-gather.13.cloned.1.call-start = ((), (), s32[]{:S(2)}) async-start(), calls=%async_computation.11 | async-start | bytes 1216512 | tf_op jit(solution)/shard_map/all_gather | solution.py:226
  9.4 241.0 %all-gather.23.cloned.1.call-start = ((), (), s32[]{:S(2)}) async-start(), calls=%async_computation.16 | async-start | bytes 1216512 | tf_op jit(solution)/shard_map/all_gather | solution.py:231
  10.0 296.3 %all-gather.19.cloned.1.call-start = ((), (), s32[]{:S(2)}) async-start(), calls=%async_computation.14 | async-start | bytes 1216512 | tf_op jit(solution)/shard_map/all_gather | solution.py:232
  10.6 484.9 %all-gather.17.cloned.1.call-start = ((), (), s32[]{:S(2)}) async-start(), calls=%async_computation.13 | async-start | bytes 1216512 | tf_op jit(solution)/shard_map/all_gather | solution.py:229
  11.2 486.5 %all-gather.21.cloned.1.call-start = ((), (), s32[]{:S(2)}) async-start(), calls=%async_computation.15 | async-start | bytes 1216512 | tf_op jit(solution)/shard_map/all_gather | solution.py:230
  11.9 714.7 %all-gather.25.cloned.1.call-start = ((), (), s32[]{:S(2)}) async-start(), calls=%async_computation.17 | async-start | bytes 1216512 | tf_op jit(solution)/shard_map/all_gather | solution.py:233
  12.7 717.3 %all-gather.27.cloned.1.call-start = ((), (), s32[]{:S(2)}) async-start(), calls=%async_computation.18 | async-start | bytes 4866048 | tf_op jit(solution)/shard_map/all_gather | solution.py:234
  13.4 728.3 %all-gather.29.cloned.1.call-start = ((), (), s32[]{:S(2)}) async-start(), calls=%async_computation.19 | async-start | bytes 4866048 | tf_op jit(solution)/shard_map/all_gather | solution.py:235
  14.0 1316.0 %reduce-scatter.11.cloned.1.call-start = ((), (), s32[]{:S(2)}) async-start(), calls=%async_computation.20 | async-start | bytes 2433024 | tf_op jit(solution)/shard_map/reduce_scatter | solution.py:368
  70.8 264.8 %collective-permute-start.4 = (bf16[256,768]{1,0:T(8,128)(2,1)}, bf16[256,768]{1,0:T(8,128)(2,1)}, u32[]{:S(2)}, u32[]{:S(2)}) collective-permute-start(bf16[256,768]{1,0:T(8,128)(2,1)} %convolution_convert_fusion.5), channel_id=1, source_target_pairs={{0,5},{1,6},{2,7},{8,13},{9,14},{10,15},{16,21},{17,22},{18,23},{2... | collective-permute-start | bytes 1179656 | tf_op jit(solution)/shard_map/ppermute | solution.py:21
  74.1 265.5 %collective-permute-start.3 = (bf16[256,768]{1,0:T(8,128)(2,1)}, bf16[256,768]{1,0:T(8,128)(2,1)}, u32[]{:S(2)}, u32[]{:S(2)}) collective-permute-start(bf16[256,768]{1,0:T(8,128)(2,1)} %convolution_convert_fusion.5), channel_id=1, source_target_pairs={{0,4},{1,5},{2,6},{3,7},{8,12},{9,13},{10,14},{11,15},{16,20},{17,... | collective-permute-start | bytes 1179656 | tf_op jit(solution)/shard_map/ppermute | solution.py:21
  76.2 268.6 %collective-permute-start.2 = (bf16[256,768]{1,0:T(8,128)(2,1)}, bf16[256,768]{1,0:T(8,128)(2,1)}, u32[]{:S(2)}, u32[]{:S(2)}) collective-permute-start(bf16[256,768]{1,0:T(8,128)(2,1)} %convolution_convert_fusion.5), channel_id=1, source_target_pairs={{0,3},{1,4},{2,5},{3,6},{4,7},{8,11},{9,12},{10,13},{11,14},{12,15... | collective-permute-start | bytes 1179656 | tf_op jit(solution)/shard_map/ppermute | solution.py:21
  79.8 269.8 %collective-permute-start.1 = (bf16[256,768]{1,0:T(8,128)(2,1)}, bf16[256,768]{1,0:T(8,128)(2,1)}, u32[]{:S(2)}, u32[]{:S(2)}) collective-permute-start(bf16[256,768]{1,0:T(8,128)(2,1)} %convolution_convert_fusion.5), channel_id=1, source_target_pairs={{0,2},{1,3},{2,4},{3,5},{4,6},{5,7},{8,10},{9,11},{10,12},{11,13},... | collective-permute-start | bytes 1179656 | tf_op jit(solution)/shard_map/ppermute | solution.py:21
  138.1 192.0 %collective-permute-start.9 = (bf16[256,768]{1,0:T(8,128)(2,1)}, bf16[256,768]{1,0:T(8,128)(2,1)}, u32[]{:S(2)}, u32[]{:S(2)}) collective-permute-start(bf16[256,768]{1,0:T(8,128)(2,1)} %convolution_convert_fusion.7), channel_id=1, source_target_pairs={{0,5},{1,6},{2,7},{8,13},{9,14},{10,15},{16,21},{17,22},{18,23},{2... | collective-permute-start | bytes 1179656 | tf_op jit(solution)/shard_map/ppermute | solution.py:21
  355.9 276.6 %collective-permute-start.23 = (bf16[375,768]{1,0:T(8,128)(2,1)}, bf16[375,768]{1,0:T(8,128)(2,1)}, u32[]{:S(2)}, u32[]{:S(2)}) collective-permute-start(bf16[375,768]{1,0:T(8,128)(2,1)} %convolution_convert_fusion.1), channel_id=1, source_target_pairs={{0,4},{1,5},{2,6},{3,7},{8,12},{9,13},{10,14},{11,15},{16,20},{17,... | collective-permute-start | bytes 1728008 | tf_op jit(solution)/shard_map/ppermute | solution.py:21
  363.4 155.1 %collective-permute-start.16 = (bf16[375,768]{1,0:T(8,128)(2,1)}, bf16[375,768]{1,0:T(8,128)(2,1)}, u32[]{:S(2)}, u32[]{:S(2)}) collective-permute-start(bf16[375,768]{1,0:T(8,128)(2,1)} %convolution_convert_fusion), channel_id=1, source_target_pairs={{0,4},{1,5},{2,6},{3,7},{8,12},{9,13},{10,14},{11,15},{16,20},{17,... | collective-permute-start | bytes 1728008 | tf_op jit(solution)/shard_map/ppermute | solution.py:21
  371.3 150.5 %collective-permute-start.15 = (bf16[375,768]{1,0:T(8,128)(2,1)}, bf16[375,768]{1,0:T(8,128)(2,1)}, u32[]{:S(2)}, u32[]{:S(2)}) collective-permute-start(bf16[375,768]{1,0:T(8,128)(2,1)} %convolution_convert_fusion), channel_id=1, source_target_pairs={{0,3},{1,4},{2,5},{3,6},{4,7},{8,11},{9,12},{10,13},{11,14},{12,15... | collective-permute-start | bytes 1728008 | tf_op jit(solution)/shard_map/ppermute | solution.py:21
  385.5 142.1 %collective-permute-start.14 = (bf16[375,768]{1,0:T(8,128)(2,1)}, bf16[375,768]{1,0:T(8,128)(2,1)}, u32[]{:S(2)}, u32[]{:S(2)}) collective-permute-start(bf16[375,768]{1,0:T(8,128)(2,1)} %convolution_convert_fusion), channel_id=1, source_target_pairs={{0,2},{1,3},{2,4},{3,5},{4,6},{5,7},{8,10},{9,11},{10,12},{11,13},... | collective-permute-start | bytes 1728008 | tf_op jit(solution)/shard_map/ppermute | solution.py:21
  402.5 130.0 %collective-permute-start.13 = (bf16[375,768]{1,0:T(8,128)(2,1)}, bf16[375,768]{1,0:T(8,128)(2,1)}, u32[]{:S(2)}, u32[]{:S(2)}) collective-permute-start(bf16[375,768]{1,0:T(8,128)(2,1)} %convolution_convert_fusion), channel_id=1, source_target_pairs={{0,1},{1,2},{2,3},{3,4},{4,5},{5,6},{6,7},{8,9},{9,10},{10,11},{11... | collective-permute-start | bytes 1728008 | tf_op jit(solution)/shard_map/ppermute | solution.py:21
  863.4 122.9 %collective-permute-start.28 = (bf16[256,768]{0,1:T(8,128)(2,1)}, bf16[256,768]{0,1:T(8,128)(2,1)}, u32[]{:S(2)}, u32[]{:S(2)}) collective-permute-start(bf16[256,768]{0,1:T(8,128)(2,1)} %pad_maximum_fusion.22), channel_id=1, source_target_pairs={{5,0},{6,1},{7,2},{13,8},{14,9},{15,10},{21,16},{22,17},{23,18},{2... | collective-permute-start | bytes 1179656 | tf_op jit(solution)/shard_map/ppermute | solution.py:21
  865.5 122.1 %collective-permute-start.27 = (bf16[256,768]{0,1:T(8,128)(2,1)}, bf16[256,768]{0,1:T(8,128)(2,1)}, u32[]{:S(2)}, u32[]{:S(2)}) collective-permute-start(bf16[256,768]{0,1:T(8,128)(2,1)} %pad_maximum_fusion.21), channel_id=1, source_target_pairs={{4,0},{5,1},{6,2},{7,3},{12,8},{13,9},{14,10},{15,11},{20,16},{21,... | collective-permute-start | bytes 1179656 | tf_op jit(solution)/shard_map/ppermute | solution.py:21
  876.8 454.7 %reduce-scatter.17.cloned.1.call-start = ((), (), s32[]{:S(2)}) async-start(), calls=%async_computation.23 | async-start | bytes 2433024 | tf_op jit(solution)/shard_map/reduce_scatter | solution.py:377
  878.7 110.2 %collective-permute-start.26 = (bf16[256,768]{0,1:T(8,128)(2,1)}, bf16[256,768]{0,1:T(8,128)(2,1)}, u32[]{:S(2)}, u32[]{:S(2)}) collective-permute-start(bf16[256,768]{0,1:T(8,128)(2,1)} %pad_maximum_fusion.20), channel_id=1, source_target_pairs={{3,0},{4,1},{5,2},{6,3},{7,4},{11,8},{12,9},{13,10},{14,11},{15,12... | collective-permute-start | bytes 1179656 | tf_op jit(solution)/shard_map/ppermute | solution.py:21
  899.2 433.8 %reduce-scatter.19.cloned.1.call-start = ((), (), s32[]{:S(2)}) async-start(), calls=%async_computation.24 | async-start | bytes 2433024 | tf_op jit(solution)/shard_map/reduce_scatter | solution.py:380
  922.2 412.4 %reduce-scatter.25.cloned.1.call-start = ((), (), s32[]{:S(2)}) async-start(), calls=%async_computation.27 | async-start | bytes 2433024 | tf_op jit(solution)/shard_map/reduce_scatter | solution.py:389
  967.8 451.0 %reduce-scatter.13.cloned.1.call-start = ((), (), s32[]{:S(2)}) async-start(), calls=%async_computation.21 | async-start | bytes 2433024 | tf_op jit(solution)/shard_map/reduce_scatter | solution.py:371
  1000.7 522.0 %reduce-scatter.15.cloned.1.call-start = ((), (), s32[]{:S(2)}) async-start(), calls=%async_computation.22 | async-start | bytes 2433024 | tf_op jit(solution)/shard_map/reduce_scatter | solution.py:374
  1055.8 570.6 %reduce-scatter.21.cloned.1.call-start = ((), (), s32[]{:S(2)}) async-start(), calls=%async_computation.25 | async-start | bytes 2433024 | tf_op jit(solution)/shard_map/reduce_scatter | solution.py:383
  1158.4 571.8 %reduce-scatter.23.cloned.1.call-start = ((), (), s32[]{:S(2)}) async-start(), calls=%async_computation.26 | async-start | bytes 2433024 | tf_op jit(solution)/shard_map/reduce_scatter | solution.py:386
  1228.5 642.9 %reduce-scatter.27.cloned.1.call-start = ((), (), s32[]{:S(2)}) async-start(), calls=%async_computation.28 | async-start | bytes 9732096 | tf_op jit(solution)/shard_map/reduce_scatter | solution.py:392
  1247.1 765.5 %reduce-scatter.29.cloned.1.call-start = ((), (), s32[]{:S(2)}) async-start(), calls=%async_computation.29 | async-start | bytes 9732096 | tf_op jit(solution)/shard_map/reduce_scatter | solution.py:393
  (599 other events, 5409.7 us)
Sparse Core Ops, SparseCore 0:
  11.0 57.1 all-gather.14
  71.2 64.2 all-gather.10
  138.6 55.8 all-gather.12
  197.4 52.9 all-gather.22
  253.3 52.9 all-gather.18
  309.2 60.8 all-gather.16
  373.1 61.3 all-gather.20
  437.5 67.1 all-gather.24
  507.7 75.1 all-gather.26
  585.8 61.8 all-gather.28
  876.9 111.4 reduce-scatter.10
  993.5 110.7 reduce-scatter.16
  1109.5 101.4 reduce-scatter.18
  1216.2 98.8 reduce-scatter.24
  1320.2 98.5 reduce-scatter.12
  1424.0 98.6 reduce-scatter.14
  1527.8 98.6 reduce-scatter.20
  1631.6 98.5 reduce-scatter.22
  1736.1 135.2 reduce-scatter.26
  1877.1 135.3 reduce-scatter.28
where the time goes:
time: 2040 us; the launch traced here: 2020 us
  waiting for transfers between devices  937 us (46%)
  local copies, waits for them, and re-layouts  369 us (18%)
  matrix products  342 us (17%)
  starting transfers between devices  160 us (8%)
  other arithmetic  101 us (5%)
  blocking collectives  92.7 us (5%)
    slice x128, local copies, waits for them, and re-layouts, split_heads(): part = lax.slice_in_dim(block, start, start + columns, axis=1)  158 us
    ppermute x48, starting transfers between devices, from_behind(): lax.ppermute(value, axis, [(source, source + steps) for source in range(f...  158 us
    reduce_scatter x1, waiting for transfers between devices, shards(): lax.psum_scatter(flat_rows(grad_feed_up), ('fsdp', 'ctx'), scatter_dimens...  140 us
    reduce_scatter x1, waiting for transfers between devices, shards(): lax.psum_scatter(flat_rows(grad_feed_down), ('fsdp', 'ctx'), scatter_dime...  139 us
    reduce_scatter x1, waiting for transfers between devices, shards(): lax.psum_scatter(flat_rows(grad_self_value), ('fsdp', 'ctx'), scatter_dim...  102 us
    reduce_scatter x1, waiting for transfers between devices, shards(): lax.psum_scatter(flat_rows(grad_cross_key), ('fsdp', 'ctx'), scatter_dime...  102 us
    reduce_scatter x1, waiting for transfers between devices, shards(): lax.psum_scatter(flat_rows(grad_cross_value), ('fsdp', 'ctx'), scatter_di...  102 us
    unnamed x2, blocking collectives  92.7 us
  transfers between devices with their start and end apart: 68, of which 15 were waited for; matrix products, arithmetic and copies ran while one was open for 32% of the time, Pallas kernels for 0%

commit v1 on v0

v1 whole, which is shorter than its diff:
```python
import functools

import jax
import jax.numpy as jnp
from jax import lax
from jax.experimental import pallas as pl
from jax.experimental.pallas import tpu as pltpu
from jax.sharding import Mesh, PartitionSpec as P

D = 768
HD = 64
FF = 3072
SPAN = 1024
MEM = 4
ROWS = 256
WIDE = (MEM + 1) * ROWS
HEADS = 3
FR = 375
FP = 384
KEYS = MEM * FP
NEG = -1e30
ALL = ("fsdp", "grp", "mem")
LINE = ("grp", "mem")
F32 = jnp.float32
BF = jnp.bfloat16


def normalize(states, gain):
    center = states - jnp.mean(states, axis=-1, keepdims=True)
    spread = jnp.mean(center * center, axis=-1, keepdims=True)
    return center * lax.rsqrt(spread + 1e-05) * gain


def exact_gelu(values):
    return jax.nn.gelu(values, approximate=False)


def product(left, right):
    return jnp.dot(left, right, preferred_element_type=F32)


def product_left(left, right):
    return lax.dot_general(left, right, (((0,), (0,)), ((), ())), preferred_element_type=F32)


def product_right(left, right):
    return lax.dot_general(left, right, (((1,), (1,)), ((), ())), preferred_element_type=F32)


def lanes(rows):
    return lax.broadcasted_iota(jnp.int32, (rows, 128), 1)


def head_lanes(head, rows):
    lane = lanes(rows)
    return (lane >= HD) if head == 1 else (lane < HD)


def only(head, window):
    return jnp.where(head_lanes(head, window.shape[0]), window, jnp.zeros_like(window))


def swap_halves(window):
    return pltpu.roll(window.astype(F32), HD, 1).astype(BF)


def marked(head, window, value):
    spare = 0 if head == 1 else HD
    return jnp.where(lanes(window.shape[0]) == spare, value, window)


def scaled(window):
    return (window.astype(F32) * 0.125).astype(BF)


def valid_rows(scal, first, count):
    row = first + lax.broadcasted_iota(jnp.int32, (count, 128), 0)
    return (row >= scal[4]) & (row < MEM * ROWS + scal[5])


def gather_rows(scal, pieces, tail, whole, step):
    for j in range(MEM):
        start = pl.multiple_of(scal[j] * step, step)
        whole[pl.ds(start, pieces[j].shape[0]), :] = pieces[j][...]
    if tail is not None:
        whole[pl.ds(MEM * step, tail.shape[0]), :] = tail[...]


def scatter_rows(scal, whole, pieces, tail, step):
    for j in range(MEM):
        start = pl.multiple_of(scal[j] * step, step)
        pieces[j][...] = whole[pl.ds(start, pieces[j].shape[0]), :].astype(BF)
    if tail is not None:
        tail[...] = whole[pl.ds(MEM * step, tail.shape[0]), :].astype(BF)


def self_prepare(scal, whole, qa, ka):
    hidden = lax.broadcasted_iota(jnp.int32, (WIDE, 128), 0) < scal[4]
    for head in range(HEADS):
        if head < 2:
            query, key = whole[:, 0:128], whole[:, 128:256]
        else:
            query = whole[:, 384:512]
            key = swap_halves(query)
        qa[head] = marked(head, scaled(query), jnp.asarray(NEG, BF))
        ka[head] = marked(head, only(head, key), jnp.where(hidden, 1.0, 0.0).astype(BF))


def forward_finish(scal, ot, out, outs, tail):
    ot[HEADS * HD :, :] = jnp.zeros((HD, WIDE), F32)
    for i in range(MEM + 1):
        block = ot[:, i * ROWS : (i + 1) * ROWS].T
        keep = valid_rows(scal, i * ROWS, ROWS)[:, 0:1]
        out[i * ROWS : (i + 1) * ROWS, :] = jnp.where(keep, block, 0.0).astype(BF)
    scatter_rows(scal, out, outs, tail, ROWS)


def self_forward_kernel(scal, p0, p1, p2, p3, tail, o0, o1, o2, o3, otail, ot, lse, whole, qa, ka, vt, out):
    gather_rows(scal, (p0, p1, p2, p3), tail, whole, ROWS)
    self_prepare(scal, whole, qa, ka)
    turned = whole[:, 256:384].astype(F32).T.astype(BF)
    vt[0] = turned[0:HD]
    vt[1] = turned[HD:128]
    vt[2] = whole[:, 512:640].astype(F32).T.astype(BF)[0:HD]
    causal = lax.broadcasted_iota(jnp.int32, (ROWS, ROWS), 0) <= lax.broadcasted_iota(
        jnp.int32, (ROWS, ROWS), 1
    )

    def one_head(head, carry):
        for i in range(MEM + 1):
            a, b = i * ROWS, (i + 1) * ROWS
            query = qa[head, a:b, :]
            near = jnp.where(causal, product_right(ka[head, a:b, :], query), NEG)
            top = jnp.max(near, axis=0, keepdims=True)
            if i:
                far = product_right(ka[head, 0:a, :], query)
                top = jnp.maximum(top, jnp.max(far, axis=0, keepdims=True))
                far = jnp.exp(far - top)
            near = jnp.exp(near - top)
            total = jnp.sum(near, axis=0, keepdims=True)
            if i:
                total = total + jnp.sum(far, axis=0, keepdims=True)
            scale = 1.0 / total
            mixed = product(vt[head, :, a:b], (near * scale).astype(BF))
            if i:
                mixed = mixed + product(vt[head, :, 0:a], (far * scale).astype(BF))
            ot[pl.ds(pl.multiple_of(head * HD, HD), HD), a:b] = mixed
            lse[head, 0:1, a:b] = top + jnp.log(total)
        return carry

    lax.fori_loop(0, HEADS, one_head, 0)
    forward_finish(scal, ot, out, (o0, o1, o2, o3), otail)


def grads_prepare(scal, grads, ot, dm, delta):
    for i in range(MEM + 1):
        a, b = i * ROWS, (i + 1) * ROWS
        keep = valid_rows(scal, a, ROWS)[:, 0:1]
        clean = jnp.where(keep, grads[a:b, :].astype(F32), 0.0)
        turned = clean.T * ot[:, a:b]
        clean = clean.astype(BF)
        for head in range(HEADS):
            window = clean[:, 0:128] if head < 2 else clean[:, 128:256]
            dm[head, a:b, :] = only(head, window)
            delta[head, 0:1, a:b] = jnp.sum(turned[head * HD : (head + 1) * HD], axis=0, keepdims=True)


def self_backward_kernel(
    scal, p0, p1, p2, p3, tail, g0, g1, g2, g3, gtail, ot, lse,
    d0, d1, d2, d3, dtail,
    whole, grads, qa, ka, qm, kt, vm, dm, delta, dqt, dk, dv, out,
):
    gather_rows(scal, (p0, p1, p2, p3), tail, whole, ROWS)
    gather_rows(scal, (g0, g1, g2, g3), gtail, grads, ROWS)
    self_prepare(scal, whole, qa, ka)
    grads_prepare(scal, grads, ot, dm, delta)
    turned = whole[:, 128:256].astype(F32).T.astype(BF)
    kt[0] = turned[0:HD]
    kt[1] = turned[HD:128]
    kt[2] = whole[:, 384:512].astype(F32).T.astype(BF)[HD:128]
    for head in range(HEADS):
        qm[head] = only(head, scaled(whole[:, 0:128] if head < 2 else whole[:, 384:512]))
        vm[head] = only(head, whole[:, 256:384] if head < 2 else whole[:, 512:640])
    dk[...] = jnp.zeros_like(dk)
    dv[...] = jnp.zeros_like(dv)
    dqt[HEADS * HD :, :] = jnp.zeros((HD, WIDE), F32)
    causal = lax.broadcasted_iota(jnp.int32, (ROWS, ROWS), 0) <= lax.broadcasted_iota(
        jnp.int32, (ROWS, ROWS), 1
    )

    def one_head(head, carry):
        side = jnp.where(head == 2, 1, 0)
        for i in range(MEM + 1):
            a, b = i * ROWS, (i + 1) * ROWS
            query, grad, own = qa[head, a:b, :], dm[head, a:b, :], qm[head, a:b, :]
            level, offset = lse[head, 0:1, a:b], delta[head, 0:1, a:b]
            change = jnp.zeros((HD, ROWS), F32)
            for low, high in ((a, b), (0, a)):
                if low == high:
                    continue
                scores = product_right(ka[head, low:high, :], query)
                if low == a:
                    scores = jnp.where(causal, scores, NEG)
                probs = jnp.exp(scores - level)
                slopes = product_right(vm[head, low:high, :], grad)
                slopes = (probs * (slopes - offset)).astype(BF)
                dv[side, low:high, :] += product(probs.astype(BF), grad)
                dk[side, low:high, :] += product(slopes, own)
                change = change + product(kt[head, :, low:high], slopes)
            dqt[pl.ds(pl.multiple_of(head * HD, HD), HD), a:b] = change * 0.125
        return carry

    lax.fori_loop(0, HEADS, one_head, 0)
    for i in range(MEM + 1):
        a, b = i * ROWS, (i + 1) * ROWS
        query = dqt[:, a:b].T
        out[a:b, 0:128] = query[:, 0:128].astype(BF)
        out[a:b, 128:256] = dk[0, a:b, :].astype(BF)
        out[a:b, 256:384] = dv[0, a:b, :].astype(BF)
        out[a:b, 384:512] = (query[:, 128:256] + pltpu.roll(dk[1, a:b, :], HD, 1)).astype(BF)
        out[a:b, 512:640] = dv[1, a:b, :].astype(BF)
    scatter_rows(scal, out, (d0, d1, d2, d3), dtail, ROWS)


def cross_prepare(whole, queries, qa, ka):
    spare = (lax.broadcasted_iota(jnp.int32, (KEYS, 128), 0) % FP) >= FR
    for head in range(HEADS):
        query = queries[:, 0:128] if head < 2 else queries[:, 128:256]
        key = whole[:, 0:128] if head < 2 else whole[:, 256:384]
        qa[head] = marked(head, scaled(query), jnp.asarray(NEG, BF))
        ka[head] = marked(head, only(head, key), jnp.where(spare, 1.0, 0.0).astype(BF))


def cross_forward_kernel(
    scal, q0, q1, q2, q3, qtail, f0, f1, f2, f3,
    o0, o1, o2, o3, otail, ot, lse,
    whole, queries, qa, ka, vt, out,
):
    whole[...] = jnp.zeros_like(whole)
    gather_rows(scal, (f0, f1, f2, f3), None, whole, FP)
    gather_rows(scal, (q0, q1, q2, q3), qtail, queries, ROWS)
    cross_prepare(whole, queries, qa, ka)
    turned = whole[:, 128:256].astype(F32).T.astype(BF)
    vt[0] = turned[0:HD]
    vt[1] = turned[HD:128]
    vt[2] = whole[:, 256:384].astype(F32).T.astype(BF)[HD:128]

    def one_head(head, carry):
        for i in range(MEM + 1):
            a, b = i * ROWS, (i + 1) * ROWS
            scores = product_right(ka[head], qa[head, a:b, :])
            top = jnp.max(scores, axis=0, keepdims=True)
            scores = jnp.exp(scores - top)
            total = jnp.sum(scores, axis=0, keepdims=True)
            mixed = product(vt[head], (scores * (1.0 / total)).astype(BF))
            ot[pl.ds(pl.multiple_of(head * HD, HD), HD), a:b] = mixed
            lse[head, 0:1, a:b] = top + jnp.log(total)
        return carry

    lax.fori_loop(0, HEADS, one_head, 0)
    forward_finish(scal, ot, out, (o0, o1, o2, o3), otail)


def cross_backward_kernel(
    scal, q0, q1, q2, q3, qtail, f0, f1, f2, f3, g0, g1, g2, g3, gtail, ot, lse,
    d0, d1, d2, d3, dtail, e0, e1, e2, e3,
    whole, queries, grads, qa, ka, qm, kt, vm, dm, delta, dqt, dk, dv, out, fout,
):
    whole[...] = jnp.zeros_like(whole)
    gather_rows(scal, (f0, f1, f2, f3), None, whole, FP)
    gather_rows(scal, (q0, q1, q2, q3), qtail, queries, ROWS)
    gather_rows(scal, (g0, g1, g2, g3), gtail, grads, ROWS)
    cross_prepare(whole, queries, qa, ka)
    grads_prepare(scal, grads, ot, dm, delta)
    turned = whole[:, 0:128].astype(F32).T.astype(BF)
    kt[0] = turned[0:HD]
    kt[1] = turned[HD:128]
    kt[2] = whole[:, 256:384].astype(F32).T.astype(BF)[0:HD]
    for head in range(HEADS):
        qm[head] = only(head, scaled(queries[:, 0:128] if head < 2 else queries[:, 128:256]))
        vm[head] = only(head, whole[:, 128:256] if head < 2 else swap_halves(whole[:, 256:384]))
    dk[...] = jnp.zeros_like(dk)
    dv[...] = jnp.zeros_like(dv)
    dqt[HEADS * HD :, :] = jnp.zeros((HD, WIDE), F32)

    def one_head(head, carry):
        side = jnp.where(head == 2, 1, 0)
        for i in range(MEM + 1):
            a, b = i * ROWS, (i + 1) * ROWS
            grad = dm[head, a:b, :]
            scores = product_right(ka[head], qa[head, a:b, :])
            probs = jnp.exp(scores - lse[head, 0:1, a:b])
            slopes = product_right(vm[head], grad)
            slopes = (probs * (slopes - delta[head, 0:1, a:b])).astype(BF)
            dv[side] += product(probs.astype(BF), grad)
            dk[side] += product(slopes, qm[head, a:b, :])
            change = product(kt[head], slopes)
            dqt[pl.ds(pl.multiple_of(head * HD, HD), HD), a:b] = change * 0.125
        return carry

    lax.fori_loop(0, HEADS, one_head, 0)
    for i in range(MEM + 1):
        a, b = i * ROWS, (i + 1) * ROWS
        out[a:b, :] = dqt[:, a:b].T.astype(BF)
    scatter_rows(scal, out, (d0, d1, d2, d3), dtail, ROWS)
    fout[:, 0:128] = dk[0].astype(BF)
    fout[:, 128:256] = dv[0].astype(BF)
    fout[:, 256:384] = (dk[1] + pltpu.roll(dv[1], HD, 1)).astype(BF)
    scatter_rows(scal, fout, (e0, e1, e2, e3), None, FP)


def shape(*dims, dtype=BF):
    return jax.ShapeDtypeStruct(dims, dtype)


def vmem(*dims, dtype=BF):
    return pltpu.VMEM(dims, dtype)


def call(kernel, scal, args, outs, scratch, flops, exps):
    full = pl.BlockSpec(memory_space=pltpu.VMEM)
    return pl.pallas_call(
        kernel,
        out_shape=outs,
        in_specs=[pl.BlockSpec(memory_space=pltpu.SMEM)] + [full] * len(args),
        out_specs=[full] * len(outs),
        scratch_shapes=scratch,
        cost_estimate=pl.CostEstimate(flops=flops, transcendentals=exps, bytes_accessed=4 << 20),
        compiler_params=pltpu.CompilerParams(vmem_limit_bytes=60 << 20),
    )(scal, *args)


def self_forward(scal, pieces):
    outs = [shape(ROWS, 256)] * 5 + [shape(256, WIDE, dtype=F32), shape(HEADS, 8, WIDE, dtype=F32)]
    scratch = [vmem(WIDE, 640), vmem(HEADS, WIDE, 128), vmem(HEADS, WIDE, 128), vmem(HEADS, HD, WIDE), vmem(WIDE, 256)]
    got = call(self_forward_kernel, scal, pieces, outs, scratch, 3 << 30, 3 << 20)
    return (got[:5], got[5:])


def self_backward(scal, pieces, grads, kept):
    outs = [shape(ROWS, 640)] * 5
    head = vmem(HEADS, WIDE, 128)
    scratch = [
        vmem(WIDE, 640), vmem(WIDE, 256), head, head, head, vmem(HEADS, HD, WIDE), head, head,
        vmem(HEADS, 8, WIDE, dtype=F32), vmem(256, WIDE, dtype=F32),
        vmem(2, WIDE, 128, dtype=F32), vmem(2, WIDE, 128, dtype=F32), vmem(WIDE, 640),
    ]
    return call(self_backward_kernel, scal, [*pieces, *grads, *kept], outs, scratch, 8 << 30, 3 << 20)


def cross_forward(scal, queries, pieces):
    outs = [shape(ROWS, 256)] * 5 + [shape(256, WIDE, dtype=F32), shape(HEADS, 8, WIDE, dtype=F32)]
    scratch = [
        vmem(KEYS, 384), vmem(WIDE, 256), vmem(HEADS, WIDE, 128), vmem(HEADS, KEYS, 128),
        vmem(HEADS, HD, KEYS), vmem(WIDE, 256),
    ]
    got = call(cross_forward_kernel, scal, [*queries, *pieces], outs, scratch, 6 << 30, 6 << 20)
    return (got[:5], got[5:])


def cross_backward(scal, queries, pieces, grads, kept):
    outs = [shape(ROWS, 256)] * 5 + [shape(FR, 384)] * 4
    head, keys = (vmem(HEADS, WIDE, 128), vmem(HEADS, KEYS, 128))
    scratch = [
        vmem(KEYS, 384), vmem(WIDE, 256), vmem(WIDE, 256), head, keys, head, vmem(HEADS, HD, KEYS), keys, head,
        vmem(HEADS, 8, WIDE, dtype=F32), vmem(256, WIDE, dtype=F32),
        vmem(2, KEYS, 128, dtype=F32), vmem(2, KEYS, 128, dtype=F32), vmem(WIDE, 256), vmem(KEYS, 384),
    ]
    got = call(cross_backward_kernel, scal, [*queries, *pieces, *grads, *kept], outs, scratch, 16 << 30, 6 << 20)
    return (got[:5], got[5:])


def swap(value, mask):
    if mask == 0:
        return value
    count = lax.axis_size("grp") * MEM
    return lax.ppermute(value, LINE, [(s, s ^ mask) for s in range(count)])


def to_previous(value):
    count = lax.axis_size("grp") * MEM
    return lax.ppermute(value, LINE, [(s, s - MEM) for s in range(MEM, count)])


def to_next(value):
    count = lax.axis_size("grp") * MEM
    return lax.ppermute(value, LINE, [(s, s + MEM) for s in range(count - MEM)])


def spread(member, rows, width):
    return [
        swap(lax.dynamic_slice_in_dim(rows, (member ^ j) * width, width, axis=1), j)
        for j in range(MEM)
    ]


def with_tail(member, pieces):
    return [*pieces, to_previous(lax.select_n(member, *pieces))]


def join(member, pieces):
    return jnp.concatenate(
        [lax.select_n(member, *[pieces[s ^ m] for m in range(MEM)]) for s in range(MEM)], axis=1
    )


def collect(member, pieces):
    late = to_next(pieces[4])
    whole = []
    for j in range(MEM):
        piece = pieces[j].astype(F32) + jnp.where(member == j, late.astype(F32), 0.0)
        whole.append(swap(piece.astype(BF), j))
    return join(member, whole)


def self_columns(query, key, value):
    parts = []
    for m in range(MEM):
        a = 192 * m
        for matrix in (query, key, value):
            parts.append(matrix[:, a : a + 128])
        parts += [query[:, a + 128 : a + 192], key[:, a + 128 : a + 192], value[:, a + 128 : a + 192]]
        parts.append(jnp.zeros((query.shape[0], 64), query.dtype))
    return jnp.concatenate(parts, axis=1)


def self_columns_back(matrix):
    parts = [[], [], []]
    for m in range(MEM):
        a = 640 * m
        for n in range(3):
            parts[n] += [matrix[:, a + 128 * n : a + 128 * n + 128], matrix[:, a + 384 + 64 * n : a + 448 + 64 * n]]
    return [jnp.concatenate(part, axis=1) for part in parts]


def query_columns(matrix):
    zero = jnp.zeros((matrix.shape[0], 64), matrix.dtype)
    parts = []
    for m in range(MEM):
        parts += [matrix[:, 192 * m : 192 * m + 192], zero]
    return jnp.concatenate(parts, axis=1)


def query_columns_back(matrix):
    return jnp.concatenate([matrix[:, 256 * m : 256 * m + 192] for m in range(MEM)], axis=1)


def frame_columns(key, value):
    parts = []
    for m in range(MEM):
        a = 192 * m
        parts += [key[:, a : a + 128], value[:, a : a + 128], key[:, a + 128 : a + 192], value[:, a + 128 : a + 192]]
    return jnp.concatenate(parts, axis=1)


def frame_columns_back(matrix):
    key, value = ([], [])
    for m in range(MEM):
        a = 384 * m
        key += [matrix[:, a : a + 128], matrix[:, a + 256 : a + 320]]
        value += [matrix[:, a + 128 : a + 256], matrix[:, a + 320 : a + 384]]
    return [jnp.concatenate(key, axis=1), jnp.concatenate(value, axis=1)]


def head_rows(matrix):
    zero = jnp.zeros((64, matrix.shape[1]), matrix.dtype)
    parts = []
    for m in range(MEM):
        parts += [matrix[192 * m : 192 * m + 192], zero]
    return jnp.concatenate(parts, axis=0)


def head_rows_back(matrix):
    return jnp.concatenate([matrix[256 * m : 256 * m + 192] for m in range(MEM)], axis=0)


def up_columns(matrix, devices):
    rows = matrix.shape[0]
    part = D // devices
    return matrix.reshape(rows, devices, 4, part).transpose(0, 2, 1, 3).reshape(rows, FF)


def up_columns_back(matrix, devices):
    rows = matrix.shape[0]
    part = D // devices
    return matrix.reshape(rows, 4, devices, part).transpose(0, 2, 1, 3).reshape(rows, FF)


def down_columns(matrix):
    part = matrix.shape[0] // 4
    return jnp.concatenate([matrix[c * part : (c + 1) * part] for c in range(4)], axis=1)


def down_columns_back(matrix):
    return jnp.concatenate([matrix[:, c * D : (c + 1) * D] for c in range(4)], axis=0)


def gather(matrix):
    return lax.all_gather(matrix, ALL, axis=0, tiled=True)


def scatter(matrix):
    return lax.psum_scatter(matrix, ALL, scatter_dimension=0, tiled=True).astype(F32)


def shards(
    tokens, frames, document_starts, cotangent,
    gain_self, gain_cross, gain_feed, gain_final,
    self_query, self_key, self_value, self_output,
    cross_query, cross_key, cross_value, cross_output,
    feed_up, feed_down,
):
    devices = lax.axis_size("fsdp") * lax.axis_size("grp") * MEM
    group, member = (lax.axis_index("grp"), lax.axis_index("mem"))
    groups = lax.axis_size("grp")
    starts = document_starts[0]
    inner = starts - SPAN * jnp.arange(groups, dtype=jnp.int32)
    late = jnp.concatenate([inner[1:], jnp.zeros((1,), jnp.int32)])
    scal = jnp.stack([
        member, member ^ 1, member ^ 2, member ^ 3,
        lax.dynamic_index_in_dim(inner, group, keepdims=False),
        lax.dynamic_index_in_dim(late, group, keepdims=False),
        member, member,
    ]).astype(jnp.int32)

    part = D // devices
    gains = jnp.stack([gain_self, gain_cross, gain_feed, gain_final], axis=1)
    gains = jnp.pad(gains, ((0, 0), (0, 124)))
    first = gather(jnp.concatenate([self_columns(self_query, self_key, self_value), gains], axis=1))
    second = gather(jnp.concatenate(
        [self_output, cross_output, query_columns(cross_query), frame_columns(cross_key, cross_value)], axis=1))
    third = gather(jnp.concatenate([up_columns(feed_up, devices), down_columns(feed_down)], axis=1))

    w_self = first[:, :2560]
    gain_rows = first[:, 2560:].T.astype(F32)
    w_so, w_co = (head_rows(second[:, :D]), head_rows(second[:, D : 2 * D]))
    w_cq, w_kv = (second[:, 1536:2560], second[:, 2560:])
    w_up = third[:, :FF]
    w_down = [third[:, FF + c * D : FF + (c + 1) * D] for c in range(4)]

    states = tokens.astype(F32)
    normed_self, back_self = jax.vjp(normalize, states, gain_rows[0])
    normed_self = normed_self.astype(BF)
    projected = product(normed_self, w_self).astype(BF)
    self_pieces = with_tail(member, spread(member, projected, 640))
    frame_rows = product(frames, w_kv).astype(BF)
    frame_pieces = spread(member, frame_rows, 384)

    mixed, self_kept = self_forward(scal, self_pieces)
    self_heads = collect(member, mixed)
    first_sum = states + product(self_heads, w_so)
    normed_cross, back_cross = jax.vjp(normalize, first_sum, gain_rows[1])
    normed_cross = normed_cross.astype(BF)
    cross_queries = product(normed_cross, w_cq).astype(BF)
    cross_pieces = with_tail(member, spread(member, cross_queries, 256))
    mixed, cross_kept = cross_forward(scal, cross_pieces, frame_pieces)
    cross_heads = collect(member, mixed)
    second_sum = first_sum + product(cross_heads, w_co)
    normed_feed, back_feed = jax.vjp(normalize, second_sum, gain_rows[2])
    normed_feed = normed_feed.astype(BF)
    inner_units = product(normed_feed, w_up)
    activated, back_gelu = jax.vjp(exact_gelu, inner_units)
    hidden = activated.astype(BF)
    third_sum = second_sum
    for c in range(4):
        third_sum = third_sum + product(hidden[:, c * D : (c + 1) * D], w_down[c])
    result, back_final = jax.vjp(normalize, third_sum, gain_rows[3])

    grad_third, grad_gain_final = back_final(cotangent.astype(F32))
    grad_feed_out = grad_third.astype(BF)
    grad_inner = jnp.concatenate([product_right(grad_feed_out, w_down[c]) for c in range(4)], axis=1)
    (grad_inner,) = back_gelu(grad_inner)
    grad_inner = grad_inner.astype(BF)
    grad_up = product_left(normed_feed, grad_inner).astype(BF)
    grad_down = [product_left(hidden[:, c * D : (c + 1) * D], grad_feed_out).astype(BF) for c in range(4)]
    sums_feed = scatter(jnp.concatenate([grad_up, *grad_down], axis=1))
    grad_second_part, grad_gain_feed = back_feed(product_right(grad_inner, w_up))
    grad_second = grad_third + grad_second_part

    grad_cross_out = grad_second.astype(BF)
    grad_cross_heads = product_right(grad_cross_out, w_co).astype(BF)
    grad_pieces = with_tail(member, spread(member, grad_cross_heads, 256))
    grad_co = head_rows_back(product_left(cross_heads, grad_cross_out)).astype(BF)
    query_pieces, frame_grads = cross_backward(scal, cross_pieces, frame_pieces, grad_pieces, cross_kept)
    grad_cross_queries = collect(member, query_pieces)
    frame_grad = join(member, [swap(frame_grads[j], j) for j in range(MEM)])
    grad_cq = product_left(normed_cross, grad_cross_queries).astype(BF)
    grad_first_part, grad_gain_cross = back_cross(product_right(grad_cross_queries, w_cq))
    grad_first = grad_second + grad_first_part

    grad_self_out = grad_first.astype(BF)
    grad_self_heads = product_right(grad_self_out, w_so).astype(BF)
    grad_pieces = with_tail(member, spread(member, grad_self_heads, 256))
    grad_so = head_rows_back(product_left(self_heads, grad_self_out)).astype(BF)
    grad_kv = product_left(frames, frame_grad).astype(BF)
    frames_gradient = product_right(frame_grad, w_kv)
    sums_cross = scatter(jnp.concatenate([grad_so, grad_co, grad_cq, grad_kv], axis=1))
    grad_projected = collect(member, self_backward(scal, self_pieces, grad_pieces, self_kept))
    grad_qkv = product_left(normed_self, grad_projected).astype(BF)
    grad_states_part, grad_gain_self = back_self(product_right(grad_projected, w_self))
    tokens_gradient = grad_first + grad_states_part
    grad_gains = jnp.stack([grad_gain_self, grad_gain_cross, grad_gain_feed, grad_gain_final])
    grad_gains = jnp.pad(grad_gains, ((0, 124), (0, 0))).T.astype(BF)
    sums_self = scatter(jnp.concatenate([grad_qkv, grad_gains], axis=1))

    gains_out = sums_self[:, 2560:2564].T
    query, key, value = self_columns_back(sums_self[:, :2560])
    cross_k, cross_v = frame_columns_back(sums_cross[:, 2560:])
    return (
        result.astype(BF),
        tokens_gradient,
        frames_gradient,
        gains_out[0],
        gains_out[1],
        gains_out[2],
        gains_out[3],
        query,
        key,
        value,
        sums_cross[:, :D],
        query_columns_back(sums_cross[:, 1536:2560]),
        cross_k,
        cross_v,
        sums_cross[:, D : 2 * D],
        up_columns_back(sums_feed[:, :FF], devices),
        down_columns_back(sums_feed[:, FF:]),
    )


def solution(mesh):
    fsdp, ctx = (mesh.shape["fsdp"], mesh.shape["ctx"])
    fine = Mesh(mesh.devices.reshape(fsdp, ctx // MEM, MEM), ALL)
    rows, flat = (P(ALL, None), P(ALL))
    in_specs = (rows, rows, P("fsdp", None), rows) + (flat,) * 4 + (rows,) * 10
    out_specs = (rows,) * 3 + (flat,) * 4 + (rows,) * 10
    return jax.shard_map(shards, mesh=fine, in_specs=in_specs, out_specs=out_specs, check_vma=False)
```

time: 2040 us -> 806 us (0.40)
  waiting for transfers between devices: 937 us -> 504 us
  local copies, waits for them, and re-layouts: 369 us -> 70 us
  matrix products: 342 us -> 55.6 us
  starting transfers between devices: 160 us -> 47.3 us
  blocking collectives: 92.7 us -> 0 us
  Pallas kernels: 0 us -> 69.2 us
  other arithmetic: 101 us -> 36.1 us
    reduce_scatter x10 -> x1, waiting for transfers between devices: 669 us -> 134 us  [scatter(): lax.psum_scatter(matrix, ALL, scatter_dimension=0, tiled=True).astype(F32)]
    dot_general x262 -> x10, matrix products: 302 us -> 20.2 us  [product(): return jnp.dot(left, right, preferred_element_type=F32)]
    unnamed x20 -> x8, waiting for transfers between devices: 6.41 us -> 158 us
    all_gather x10 -> x3, waiting for transfers between devices: 204 us -> 55.1 us  [gather(): return lax.all_gather(matrix, ALL, axis=0, tiled=True)]
    slice x128 -> x40, local copies, waits for them, and re-layouts: 158 us -> 12.8 us  [the longest x2 1.78 us: self_columns(): parts.append(matrix[:, a:a + 128])]
    reshape x68 -> x8, local copies, waits for them, and re-layouts: 145 us -> 8.49 us  [the longest x2 5.1 us: up_columns_back(): matrix.reshape(rows, 4, devices, part).transpose(0, 2, 1, 3)]
    ppermute x48 -> x38, starting transfers between devices: 158 us -> 46.7 us  [the longest x30 31.3 us: swap(): return lax.ppermute(value, LINE, [(s, s ^ mask) for s in range(count)])]
    ppermute x48 -> x38, waiting for transfers between devices: 58 us -> 157 us  [the longest x30 81.8 us: swap(): return lax.ppermute(value, LINE, [(s, s ^ mask) for s in range(count)])]
  transfers between devices with their start and end apart: 68 -> 44, of which waited for: 15 -> 30; matrix products, arithmetic and copies ran while one was open for 32% -> 12% of each run, Pallas kernels for 0% -> 4%
where the time goes in v1:
time: 806 us; the launch traced here: 798 us
  waiting for transfers between devices  504 us (63%)
  local copies, waits for them, and re-layouts  70 us (9%)
  Pallas kernels  69.2 us (9%)
  matrix products  55.6 us (7%)
  starting transfers between devices  47.3 us (6%)
  other arithmetic  36.1 us (4%)
  between operations  15.7 us (2%)
    unnamed x8, waiting for transfers between devices  158 us
    reduce_scatter x1, waiting for transfers between devices, scatter(): lax.psum_scatter(matrix, ALL, scatter_dimension=0, tiled=True).astype(F32)  134 us
    ppermute x30, waiting for transfers between devices, swap(): return lax.ppermute(value, LINE, [(s, s ^ mask) for s in range(count)])  81.8 us
    pallas_call x4, Pallas kernels, call(): pl.pallas_call(kernel, out_shape=outs, in_specs=[pl.BlockSpec(memory_spac...  69.2 us
    all_gather x3, waiting for transfers between devices, gather(): return lax.all_gather(matrix, ALL, axis=0, tiled=True)  55.1 us
    ppermute x4, waiting for transfers between devices, to_previous(): return lax.ppermute(value, LINE, [(s, s - MEM) for s in range(MEM, count)])  51.8 us
    ppermute x30, starting transfers between devices, swap(): return lax.ppermute(value, LINE, [(s, s ^ mask) for s in range(count)])  31.3 us
    unnamed x171, local copies, waits for them, and re-layouts  27.5 us
  transfers between devices with their start and end apart: 44, of which 30 were waited for; matrix products, arithmetic and copies ran while one was open for 12% of the time, Pallas kernels for 4%

profile of v1, /device:TPU:0, one launch (start us, length us, event | category | flops | bytes accessed | tf_op | source)
XLA Modules:
  0.0 797.6 jit_solution(11281261427741794013)
XLA Ops:
  21.7 55.1 %all-gather.4.cloned.1.call-done = bf16[768,2688]{1,0:T(8,128)(2,1)} async-done(((bf16[24,2688]{1,0:T(8,128)(2,1)}), bf16[768,2688]{1,0:T(8,128)(2,1)}) %all-gather.4.cloned.1.call-update) | async-done | bytes 4128784 | tf_op jit(solution)/shard_map/all_gather | solution.py:499
  85.1 10.5 %collective-permute-done.1.p2 = bf16[256,640]{1,0:T(8,128)(2,1)S(1)} collective-permute-done((bf16[256,640]{1,0:T(8,128)(2,1)}, bf16[256,640]{1,0:T(8,128)(2,1)S(1)}, u32[]{:S(2)}, u32[]{:S(2)}) %collective-permute-start.1) | collective-permute-done | bytes 327712 | tf_op jit(solution)/shard_map/ppermute | solution.py:377
  95.5 8.0 collective-permute-done.2.p3
  109.6 22.2 %collective-permute-done.3.tail = bf16[256,640]{1,0:T(8,128)(2,1)S(1)} collective-permute-done((bf16[256,640]{1,0:T(8,128)(2,1)}, bf16[256,640]{1,0:T(8,128)(2,1)S(1)}, u32[]{:S(2)}, u32[]{:S(2)}) %collective-permute-start.3) | collective-permute-done | bytes 327712 | tf_op jit(solution)/shard_map/ppermute | solution.py:382
  132.6 11.2 %shard_map.305 = (bf16[256,256]{1,0:T(8,128)(2,1)}, bf16[256,256]{1,0:T(8,128)(2,1)}, bf16[256,256]{1,0:T(8,128)(2,1)}, bf16[256,256]{1,0:T(8,128)(2,1)}, bf16[2...) custom-call(s32[8]{0:T(128)} %stack.50.scal, bf16[256,640]{1,0:T(8,128)(2,1)} %get-tuple-element.180.p0, ...), custom_call_target="tpu_custom_call" | custom-call | flops 3221225472 | bytes 4194304 | tf_op jit(solution)/shard_map/pallas_call | solution.py:322
  145.7 5.6 collective-permute-done.4
  154.3 4.5 collective-permute-done.7
  178.5 5.4 collective-permute-done.10.q3
  185.9 8.5 %collective-permute-done.11.qtail = bf16[256,256]{1,0:T(8,128)(2,1)S(1)} collective-permute-done((bf16[256,256]{1,0:T(8,128)(2,1)S(1)}, bf16[256,256]{1,0:T(8,128)(2,1)S(1)}, u32[]{:S(2)}, u32[]{:S(2)}) %collective-permute-start.11) | collective-permute-done | bytes 131104 | tf_op jit(solution)/shard_map/ppermute | solution.py:382
  195.3 10.0 %collective-permute-done.14.f3 = bf16[375,384]{1,0:T(8,128)(2,1)S(1)} collective-permute-done((bf16[375,384]{1,0:T(8,128)(2,1)S(1)}, bf16[375,384]{1,0:T(8,128)(2,1)S(1)}, u32[]{:S(2)}, u32[]{:S(2)}) %collective-permute-start.14) | collective-permute-done | bytes 288032 | tf_op jit(solution)/shard_map/ppermute | solution.py:377
  206.0 21.5 %shard_map.306 = (bf16[256,256]{1,0:T(8,128)(2,1)}, bf16[256,256]{1,0:T(8,128)(2,1)}, bf16[256,256]{1,0:T(8,128)(2,1)}, bf16[256,256]{1,0:T(8,128)(2,1)}, bf16[2...) custom-call(s32[8]{0:T(128)} %stack.50.scal, bf16[256,256]{1,0:T(8,128)(2,1)} %get-tuple-element.176.q0, ...), custom_call_target="tpu_custom_call" | custom-call | flops 6442450944 | bytes 4194304 | tf_op jit(solution)/shard_map/pallas_call | solution.py:322
  227.5 5.0 collective-permute-start.15
  232.5 6.3 collective-permute-done.15
  239.9 9.0 %collective-permute-start.18 = (bf16[256,256]{1,0:T(8,128)(2,1)S(1)}, bf16[256,256]{1,0:T(8,128)(2,1)S(1)}, u32[]{:S(2)}, u32[]{:S(2)}) collective-permute-start(bf16[256,256]{1,0:T(8,128)(2,1)S(1)} %get-tuple-element.262), channel_id=1, source_target_pairs={{0,3},{1,2},{2,1},{3,0},{4,7},{5,6},{6,5},{7,4},{8,11},{9,10},{10,... | collective-permute-start | bytes 393224 | tf_op jit(solution)/shard_map/ppermute | solution.py:377
  249.8 4.5 collective-permute-done.18
  260.7 10.2 %multiply_convert_fusion = (bf16[256,3072]{1,0:T(8,128)(2,1)S(1)}, f32[256,3072]{1,0:T(8,128)S(1)}, f32[256,3072]{1,0:T(8,128)S(1)}) fusion(bf16[768,6144]{1,0:T(8,128)(2,1)} %all-gather.8.cloned.1.call-done, f32[256,768]{1,0:T(8,128)S(1)} %get-tuple-element.341, f32[768]{0:T(1024)S(1)} %get-tuple-element.150, f32[256]{0:T(256)S(1)} %fusion.101, ...), kind=kOutput, calls=%fused_computation.18 | convolution fusion | flops 1259864064 | bytes 13374464 | tf_op jit(solution)/shard_map/dot_general | solution.py:39
  284.4 4.2 collective-permute-done.20.g2
  292.0 11.0 %collective-permute-done.22.gtail = bf16[256,256]{1,0:T(8,128)(2,1)S(1)} collective-permute-done((bf16[256,256]{1,0:T(8,128)(2,1)S(1)}, bf16[256,256]{1,0:T(8,128)(2,1)S(1)}, u32[]{:S(2)}, u32[]{:S(2)}) %collective-permute-start.22) | collective-permute-done | bytes 131104 | tf_op jit(solution)/shard_map/ppermute | solution.py:382
  303.6 21.7 %shard_map.307 = (bf16[256,256]{1,0:T(8,128)(2,1)}, bf16[256,256]{1,0:T(8,128)(2,1)}, bf16[256,256]{1,0:T(8,128)(2,1)}, bf16[256,256]{1,0:T(8,128)(2,1)}, bf16[2...) custom-call(s32[8]{0:T(128)} %stack.50.scal, ...), custom_call_target="tpu_custom_call" | custom-call | flops 17179869184 | bytes 4194304 | tf_op jit(solution)/shard_map/pallas_call | solution.py:322
  347.7 4.2 collective-permute-done.28.g2
  354.2 10.1 %collective-permute-done.30.gtail = bf16[256,256]{1,0:T(8,128)(2,1)S(1)} collective-permute-done((bf16[256,256]{1,0:T(8,128)(2,1)S(1)}, bf16[256,256]{1,0:T(8,128)(2,1)S(1)}, u32[]{:S(2)}, u32[]{:S(2)}) %collective-permute-start.30) | collective-permute-done | bytes 131104 | tf_op jit(solution)/shard_map/ppermute | solution.py:382
  364.9 14.8 %shard_map.308 = (bf16[256,640]{1,0:T(8,128)(2,1)}, bf16[256,640]{1,0:T(8,128)(2,1)}, bf16[256,640]{1,0:T(8,128)(2,1)}, bf16[256,640]{1,0:T(8,128)(2,1)}, bf16[256,640]{1,0:T(8,128)(2,1)}) custom-call(s32[8]{0:T(128)} %stack.50.scal, bf16[256,640]{1,0:T(8,128)(2,1)} %get-tuple-element.180.p0, bf16[256,640]{1,0:T(8,128)(2,1)} %copy-done.26, ...), custom_call_target="tpu_custom_call" | custom-call | flops 8589934592 | bytes 4194304 | tf_op jit(solution)/shard_map/pallas_call | solution.py:322
  381.1 7.9 collective-permute-done.31
  395.6 5.2 collective-permute-done.34
  400.8 8.3 %collective-permute-done.33 = bf16[256,640]{1,0:T(8,128)(2,1)S(1)} collective-permute-done((bf16[256,640]{1,0:T(8,128)(2,1)S(1)}, bf16[256,640]{1,0:T(8,128)(2,1)S(1)}, u32[]{:S(2)}, u32[]{:S(2)}) %collective-permute-start.33) | collective-permute-done | bytes 327712 | tf_op jit(solution)/shard_map/ppermute | solution.py:377
  416.5 4.4 pad_maximum_fusion.1
  449.7 8.7 %copy.192 = bf16[768,4096]{1,0:T(8,128)(2,1)} copy(bf16[768,4096]{0,1:T(8,128)(2,1)} %pad_maximum_fusion) | data formatting | bytes 12582912
  459.1 5.4 fusion
  477.2 43.8 %reduce-scatter.12.cloned.1.call-done = bf16[24,2688]{1,0:T(8,128)(2,1)} async-done(((bf16[768,2688]{1,0:T(8,128)(2,1)}), bf16[24,2688]{1,0:T(8,128)(2,1)}) %reduce-scatter.12.cloned.1.call-update) | async-done | bytes 129040
  526.6 113.9 %reduce-scatter.10.cloned.1.call-done = bf16[24,4096]{1,0:T(8,128)(2,1)} async-done(((bf16[768,4096]{1,0:T(8,128)(2,1)}), bf16[24,4096]{1,0:T(8,128)(2,1)}) %reduce-scatter.10.cloned.1.call-update) | async-done | bytes 196624
  647.2 134.2 %reduce-scatter.8.cloned.1.call-done = bf16[24,6144]{1,0:T(8,128)(2,1)} async-done(((bf16[768,6144]{1,0:T(8,128)(2,1)}), bf16[24,6144]{1,0:T(8,128)(2,1)}) %reduce-scatter.8.cloned.1.call-update) | async-done | bytes 294928 | tf_op jit(solution)/shard_map/reduce_scatter | solution.py:503
  785.9 4.0 reshape.169
  (402 shorter events, 182.8 us)
Async XLA Ops:
  7.2 69.6 %all-gather.4.cloned.1.call-start = ((), (), s32[]{:S(2)}) async-start(), calls=%async_computation.3 | async-start | bytes 4257792 | tf_op jit(solution)/shard_map/all_gather | solution.py:499
  12.4 149.9 %all-gather.6.cloned.1.call-start = ((), (), s32[]{:S(2)}) async-start(), calls=%async_computation.4 | async-start | bytes 6488064 | tf_op jit(solution)/shard_map/all_gather | solution.py:499
  16.8 243.9 %all-gather.8.cloned.1.call-start = ((), (), s32[]{:S(2)}) async-start(), calls=%async_computation.5 | async-start | bytes 9732096 | tf_op jit(solution)/shard_map/all_gather | solution.py:499
  21.2 499.8 %reduce-scatter.12.cloned.1.call-start = ((), (), s32[]{:S(2)}) async-start(), calls=%async_computation.8 | async-start | bytes 4257792
  82.9 12.6 %collective-permute-start.1 = (bf16[256,640]{1,0:T(8,128)(2,1)}, bf16[256,640]{1,0:T(8,128)(2,1)S(1)}, u32[]{:S(2)}, u32[]{:S(2)}) collective-permute-start(bf16[256,640]{1,0:T(8,128)(2,1)} %get-tuple-element.202), channel_id=1, source_target_pairs={{0,2},{1,3},{2,0},{3,1},{4,6},{5,7},{6,4},{7,5},{8,10},{9,11},{10,... | collective-permute-start | bytes 983048 | tf_op jit(solution)/shard_map/ppermute | solution.py:377
  84.3 19.2 %collective-permute-start.2 = (bf16[256,640]{1,0:T(8,128)(2,1)}, bf16[256,640]{1,0:T(8,128)(2,1)S(1)}, u32[]{:S(2)}, u32[]{:S(2)}) collective-permute-start(bf16[256,640]{1,0:T(8,128)(2,1)} %get-tuple-element.201), channel_id=1, source_target_pairs={{0,3},{1,2},{2,1},{3,0},{4,7},{5,6},{6,5},{7,4},{8,11},{9,10},{10,... | collective-permute-start | bytes 983048 | tf_op jit(solution)/shard_map/ppermute | solution.py:377
  84.5 19.0 %collective-permute-start = (bf16[256,640]{1,0:T(8,128)(2,1)}, bf16[256,640]{1,0:T(8,128)(2,1)S(1)}, u32[]{:S(2)}, u32[]{:S(2)}) collective-permute-start(bf16[256,640]{1,0:T(8,128)(2,1)} %get-tuple-element.200), channel_id=1, source_target_pairs={{0,1},{1,0},{2,3},{3,2},{4,5},{5,4},{6,7},{7,6},{8,9},{9,8},{10,11... | collective-permute-start | bytes 983048 | tf_op jit(solution)/shard_map/ppermute | solution.py:377
  104.5 27.3 %collective-permute-start.3 = (bf16[256,640]{1,0:T(8,128)(2,1)}, bf16[256,640]{1,0:T(8,128)(2,1)S(1)}, u32[]{:S(2)}, u32[]{:S(2)}) collective-permute-start(bf16[256,640]{1,0:T(8,128)(2,1)} %get-tuple-element.179), channel_id=1, source_target_pairs={{4,0},{5,1},{6,2},{7,3},{12,8},{13,9},{14,10},{15,11},{20,16},{21,... | collective-permute-start | bytes 983048 | tf_op jit(solution)/shard_map/ppermute | solution.py:382
  152.5 8.7 %collective-permute-start.6 = (bf16[256,256]{1,0:T(8,128)(2,1)S(1)}, bf16[256,256]{1,0:T(8,128)(2,1)S(1)}, u32[]{:S(2)}, u32[]{:S(2)}) collective-permute-start(bf16[256,256]{1,0:T(8,128)(2,1)S(1)} %get-tuple-element.267), channel_id=1, source_target_pairs={{0,2},{1,3},{2,0},{3,1},{4,6},{5,7},{6,4},{7,5},{8,10},{9,11},{10,... | collective-permute-start | bytes 393224 | tf_op jit(solution)/shard_map/ppermute | solution.py:377
  170.8 7.7 collective-permute-start.9
  172.8 11.1 %collective-permute-start.10 = (bf16[256,256]{1,0:T(8,128)(2,1)S(1)}, bf16[256,256]{1,0:T(8,128)(2,1)S(1)}, u32[]{:S(2)}, u32[]{:S(2)}) collective-permute-start(bf16[256,256]{1,0:T(8,128)(2,1)S(1)} %get-tuple-element.247), channel_id=1, source_target_pairs={{0,3},{1,2},{2,1},{3,0},{4,7},{5,6},{6,5},{7,4},{8,11},{9,10},{10,... | collective-permute-start | bytes 393224 | tf_op jit(solution)/shard_map/ppermute | solution.py:377
  172.8 11.1 %collective-permute-start.8 = (bf16[256,256]{1,0:T(8,128)(2,1)S(1)}, bf16[256,256]{1,0:T(8,128)(2,1)S(1)}, u32[]{:S(2)}, u32[]{:S(2)}) collective-permute-start(bf16[256,256]{1,0:T(8,128)(2,1)S(1)} %get-tuple-element.246), channel_id=1, source_target_pairs={{0,1},{1,0},{2,3},{3,2},{4,5},{5,4},{6,7},{7,6},{8,9},{9,8},{10,11... | collective-permute-start | bytes 393224 | tf_op jit(solution)/shard_map/ppermute | solution.py:377
  174.9 19.5 %collective-permute-start.12 = (bf16[375,384]{1,0:T(8,128)(2,1)S(1)}, bf16[375,384]{1,0:T(8,128)(2,1)S(1)}, u32[]{:S(2)}, u32[]{:S(2)}) collective-permute-start(bf16[375,384]{1,0:T(8,128)(2,1)S(1)} %get-tuple-element.209), channel_id=1, source_target_pairs={{0,1},{1,0},{2,3},{3,2},{4,5},{5,4},{6,7},{7,6},{8,9},{9,8},{10,11... | collective-permute-start | bytes 864008 | tf_op jit(solution)/shard_map/ppermute | solution.py:377
  175.2 20.1 %collective-permute-start.13 = (bf16[375,384]{1,0:T(8,128)(2,1)S(1)}, bf16[375,384]{1,0:T(8,128)(2,1)S(1)}, u32[]{:S(2)}, u32[]{:S(2)}) collective-permute-start(bf16[375,384]{1,0:T(8,128)(2,1)S(1)} %get-tuple-element.208), channel_id=1, source_target_pairs={{0,2},{1,3},{2,0},{3,1},{4,6},{5,7},{6,4},{7,5},{8,10},{9,11},{10,... | collective-permute-start | bytes 864008 | tf_op jit(solution)/shard_map/ppermute | solution.py:377
  178.5 26.8 %collective-permute-start.14 = (bf16[375,384]{1,0:T(8,128)(2,1)S(1)}, bf16[375,384]{1,0:T(8,128)(2,1)S(1)}, u32[]{:S(2)}, u32[]{:S(2)}) collective-permute-start(bf16[375,384]{1,0:T(8,128)(2,1)S(1)} %get-tuple-element.207), channel_id=1, source_target_pairs={{0,3},{1,2},{2,1},{3,0},{4,7},{5,6},{6,5},{7,4},{8,11},{9,10},{10,... | collective-permute-start | bytes 864008 | tf_op jit(solution)/shard_map/ppermute | solution.py:377
  184.7 9.8 %collective-permute-start.11 = (bf16[256,256]{1,0:T(8,128)(2,1)S(1)}, bf16[256,256]{1,0:T(8,128)(2,1)S(1)}, u32[]{:S(2)}, u32[]{:S(2)}) collective-permute-start(bf16[256,256]{1,0:T(8,128)(2,1)S(1)} %get-tuple-element.175), channel_id=1, source_target_pairs={{4,0},{5,1},{6,2},{7,3},{12,8},{13,9},{14,10},{15,11},{20,16},{21,... | collective-permute-start | bytes 393224 | tf_op jit(solution)/shard_map/ppermute | solution.py:382
  227.5 11.3 %collective-permute-start.15 = (bf16[256,256]{1,0:T(8,128)(2,1)}, bf16[256,256]{1,0:T(8,128)(2,1)S(1)}, u32[]{:S(2)}, u32[]{:S(2)}) collective-permute-start(bf16[256,256]{1,0:T(8,128)(2,1)} %get-tuple-element.51), channel_id=1, source_target_pairs={{0,4},{1,5},{2,6},{3,7},{8,12},{9,13},{10,14},{11,15},{16,20},{17,... | collective-permute-start | bytes 393224 | tf_op jit(solution)/shard_map/ppermute | solution.py:387
  239.9 14.3 %collective-permute-start.18 = (bf16[256,256]{1,0:T(8,128)(2,1)S(1)}, bf16[256,256]{1,0:T(8,128)(2,1)S(1)}, u32[]{:S(2)}, u32[]{:S(2)}) collective-permute-start(bf16[256,256]{1,0:T(8,128)(2,1)S(1)} %get-tuple-element.262), channel_id=1, source_target_pairs={{0,3},{1,2},{2,1},{3,0},{4,7},{5,6},{6,5},{7,4},{8,11},{9,10},{10,... | collective-permute-start | bytes 393224 | tf_op jit(solution)/shard_map/ppermute | solution.py:377
  249.0 8.1 %collective-permute-start.17 = (bf16[256,256]{1,0:T(8,128)(2,1)S(1)}, bf16[256,256]{1,0:T(8,128)(2,1)S(1)}, u32[]{:S(2)}, u32[]{:S(2)}) collective-permute-start(bf16[256,256]{1,0:T(8,128)(2,1)S(1)} %get-tuple-element.264), channel_id=1, source_target_pairs={{0,2},{1,3},{2,0},{3,1},{4,6},{5,7},{6,4},{7,5},{8,10},{9,11},{10,... | collective-permute-start | bytes 393224 | tf_op jit(solution)/shard_map/ppermute | solution.py:377
  249.0 8.1 %collective-permute-start.16 = (bf16[256,256]{1,0:T(8,128)(2,1)S(1)}, bf16[256,256]{1,0:T(8,128)(2,1)S(1)}, u32[]{:S(2)}, u32[]{:S(2)}) collective-permute-start(bf16[256,256]{1,0:T(8,128)(2,1)S(1)} %get-tuple-element.263), channel_id=1, source_target_pairs={{0,1},{1,0},{2,3},{3,2},{4,5},{5,4},{6,7},{7,6},{8,9},{9,8},{10,11... | collective-permute-start | bytes 393224 | tf_op jit(solution)/shard_map/ppermute | solution.py:377
  290.5 12.5 %collective-permute-start.22 = (bf16[256,256]{1,0:T(8,128)(2,1)S(1)}, bf16[256,256]{1,0:T(8,128)(2,1)S(1)}, u32[]{:S(2)}, u32[]{:S(2)}) collective-permute-start(bf16[256,256]{1,0:T(8,128)(2,1)S(1)} %get-tuple-element.165), channel_id=1, source_target_pairs={{4,0},{5,1},{6,2},{7,3},{12,8},{13,9},{14,10},{15,11},{20,16},{21,... | collective-permute-start | bytes 393224 | tf_op jit(solution)/shard_map/ppermute | solution.py:382
  331.4 8.6 %collective-permute-start.25 = (bf16[256,256]{1,0:T(8,128)(2,1)S(1)}, bf16[256,256]{1,0:T(8,128)(2,1)S(1)}, u32[]{:S(2)}, u32[]{:S(2)}) collective-permute-start(bf16[256,256]{1,0:T(8,128)(2,1)S(1)} %get-tuple-element.261), channel_id=1, source_target_pairs={{0,2},{1,3},{2,0},{3,1},{4,6},{5,7},{6,4},{7,5},{8,10},{9,11},{10,... | collective-permute-start | bytes 393224 | tf_op jit(solution)/shard_map/ppermute | solution.py:377
  352.7 11.6 %collective-permute-start.30 = (bf16[256,256]{1,0:T(8,128)(2,1)S(1)}, bf16[256,256]{1,0:T(8,128)(2,1)S(1)}, u32[]{:S(2)}, u32[]{:S(2)}) collective-permute-start(bf16[256,256]{1,0:T(8,128)(2,1)S(1)} %get-tuple-element.159), channel_id=1, source_target_pairs={{4,0},{5,1},{6,2},{7,3},{12,8},{13,9},{14,10},{15,11},{20,16},{21,... | collective-permute-start | bytes 393224 | tf_op jit(solution)/shard_map/ppermute | solution.py:382
  379.6 9.4 %collective-permute-start.31 = (bf16[256,640]{1,0:T(8,128)(2,1)}, bf16[256,640]{1,0:T(8,128)(2,1)S(1)}, u32[]{:S(2)}, u32[]{:S(2)}) collective-permute-start(bf16[256,640]{1,0:T(8,128)(2,1)} %get-tuple-element.65), channel_id=1, source_target_pairs={{0,4},{1,5},{2,6},{3,7},{8,12},{9,13},{10,14},{11,15},{16,20},{17,... | collective-permute-start | bytes 983048 | tf_op jit(solution)/shard_map/ppermute | solution.py:387
  390.5 10.3 %collective-permute-start.34 = (bf16[256,640]{1,0:T(8,128)(2,1)S(1)}, bf16[256,640]{1,0:T(8,128)(2,1)S(1)}, u32[]{:S(2)}, u32[]{:S(2)}) collective-permute-start(bf16[256,640]{1,0:T(8,128)(2,1)S(1)} %get-tuple-element.252), channel_id=1, source_target_pairs={{0,3},{1,2},{2,1},{3,0},{4,7},{5,6},{6,5},{7,4},{8,11},{9,10},{10,... | collective-permute-start | bytes 983048 | tf_op jit(solution)/shard_map/ppermute | solution.py:377
  393.8 15.3 %collective-permute-start.33 = (bf16[256,640]{1,0:T(8,128)(2,1)S(1)}, bf16[256,640]{1,0:T(8,128)(2,1)S(1)}, u32[]{:S(2)}, u32[]{:S(2)}) collective-permute-start(bf16[256,640]{1,0:T(8,128)(2,1)S(1)} %get-tuple-element.254), channel_id=1, source_target_pairs={{0,2},{1,3},{2,0},{3,1},{4,6},{5,7},{6,4},{7,5},{8,10},{9,11},{10,... | collective-permute-start | bytes 983048 | tf_op jit(solution)/shard_map/ppermute | solution.py:377
  395.6 13.6 %collective-permute-start.32 = (bf16[256,640]{1,0:T(8,128)(2,1)S(1)}, bf16[256,640]{1,0:T(8,128)(2,1)S(1)}, u32[]{:S(2)}, u32[]{:S(2)}) collective-permute-start(bf16[256,640]{1,0:T(8,128)(2,1)S(1)} %get-tuple-element.253), channel_id=1, source_target_pairs={{0,1},{1,0},{2,3},{3,2},{4,5},{5,4},{6,7},{7,6},{8,9},{9,8},{10,11... | collective-permute-start | bytes 983048 | tf_op jit(solution)/shard_map/ppermute | solution.py:377
  420.9 219.5 %reduce-scatter.10.cloned.1.call-start = ((), (), s32[]{:S(2)}) async-start(), calls=%async_computation.7 | async-start | bytes 6488064
  427.1 13.1 %collective-permute-start.36 = (bf16[375,384]{1,0:T(8,128)(2,1)}, bf16[375,384]{1,0:T(8,128)(2,1)}, u32[]{:S(2)}, u32[]{:S(2)}) collective-permute-start(bf16[375,384]{1,0:T(8,128)(2,1)} %get-tuple-element.71), channel_id=1, source_target_pairs={{0,2},{1,3},{2,0},{3,1},{4,6},{5,7},{6,4},{7,5},{8,10},{9,11},{10,... | collective-permute-start | bytes 864008 | tf_op jit(solution)/shard_map/ppermute | solution.py:377
  428.4 13.9 %collective-permute-start.37 = (bf16[375,384]{1,0:T(8,128)(2,1)}, bf16[375,384]{1,0:T(8,128)(2,1)}, u32[]{:S(2)}, u32[]{:S(2)}) collective-permute-start(bf16[375,384]{1,0:T(8,128)(2,1)} %get-tuple-element.72), channel_id=1, source_target_pairs={{0,3},{1,2},{2,1},{3,0},{4,7},{5,6},{6,5},{7,4},{8,11},{9,10},{10,... | collective-permute-start | bytes 864008 | tf_op jit(solution)/shard_map/ppermute | solution.py:377
  428.9 13.3 %collective-permute-start.35 = (bf16[375,384]{1,0:T(8,128)(2,1)}, bf16[375,384]{1,0:T(8,128)(2,1)}, u32[]{:S(2)}, u32[]{:S(2)}) collective-permute-start(bf16[375,384]{1,0:T(8,128)(2,1)} %get-tuple-element.70), channel_id=1, source_target_pairs={{0,1},{1,0},{2,3},{3,2},{4,5},{5,4},{6,7},{7,6},{8,9},{9,8},{10,11... | collective-permute-start | bytes 864008 | tf_op jit(solution)/shard_map/ppermute | solution.py:377
  458.4 323.0 %reduce-scatter.8.cloned.1.call-start = ((), (), s32[]{:S(2)}) async-start(), calls=%async_computation.6 | async-start | bytes 9732096 | tf_op jit(solution)/shard_map/reduce_scatter | solution.py:503
  (88 other events, 1603.7 us)
Sparse Core Ops, SparseCore 0:
  12.5 64.1 all-gather.3
  80.3 77.6 all-gather.5
  161.7 92.8 all-gather.7
  421.1 99.8 reduce-scatter.11
  526.5 113.9 reduce-scatter.9
  646.2 135.1 reduce-scatter.7

commit v2 on v1

--- a/solution.py
+++ b/solution.py
@@ -499,8 +499,25 @@
     return lax.all_gather(matrix, ALL, axis=0, tiled=True)
 
 
-def scatter(matrix):
-    return lax.psum_scatter(matrix, ALL, scatter_dimension=0, tiled=True).astype(F32)
+def halve(matrix, turned):
+    devices = lax.axis_size("fsdp") * lax.axis_size("grp") * MEM
+    bits = devices.bit_length() - 1
+    outer = [bits - 1, bits - 2] if turned else [bits - 2, bits - 1]
+    order = [0, *outer, *range(1, bits - 2)]
+    here = lax.axis_index(ALL)
+    value = matrix.reshape([2] * bits + [matrix.shape[0] // devices, matrix.shape[1]])
+    left = list(range(bits - 1, -1, -1))
+    for bit in order:
+        axis = left.index(bit)
+        mine = (here >> bit) & 1
+        away = lax.dynamic_index_in_dim(value, 1 - mine, axis, keepdims=False)
+        kept = lax.dynamic_index_in_dim(value, mine, axis, keepdims=False)
+        came = lax.ppermute(away, ALL, [(s, s ^ (1 << bit)) for s in range(devices)])
+        value = kept.astype(F32) + came.astype(F32)
+        if bit != order[-1]:
+            value = value.astype(BF)
+        left.remove(bit)
+    return value
 
 
 def shards(
@@ -573,7 +590,8 @@
     grad_inner = grad_inner.astype(BF)
     grad_up = product_left(normed_feed, grad_inner).astype(BF)
     grad_down = [product_left(hidden[:, c * D : (c + 1) * D], grad_feed_out).astype(BF) for c in range(4)]
-    sums_feed = scatter(jnp.concatenate([grad_up, *grad_down], axis=1))
+    sums_up = halve(grad_up, False)
+    sums_down = halve(jnp.concatenate(grad_down, axis=1), True)
     grad_second_part, grad_gain_feed = back_feed(product_right(grad_inner, w_up))
     grad_second = grad_third + grad_second_part
 
@@ -594,18 +612,20 @@
     grad_so = head_rows_back(product_left(self_heads, grad_self_out)).astype(BF)
     grad_kv = product_left(frames, frame_grad).astype(BF)
     frames_gradient = product_right(frame_grad, w_kv)
-    sums_cross = scatter(jnp.concatenate([grad_so, grad_co, grad_cq, grad_kv], axis=1))
+    sums_out = halve(jnp.concatenate([grad_so, grad_co, grad_cq], axis=1), False)
+    sums_kv = halve(grad_kv, True)
     grad_projected = collect(member, self_backward(scal, self_pieces, grad_pieces, self_kept))
     grad_qkv = product_left(normed_self, grad_projected).astype(BF)
     grad_states_part, grad_gain_self = back_self(product_right(grad_projected, w_self))
     tokens_gradient = grad_first + grad_states_part
     grad_gains = jnp.stack([grad_gain_self, grad_gain_cross, grad_gain_feed, grad_gain_final])
     grad_gains = jnp.pad(grad_gains, ((0, 124), (0, 0))).T.astype(BF)
-    sums_self = scatter(jnp.concatenate([grad_qkv, grad_gains], axis=1))
-
-    gains_out = sums_self[:, 2560:2564].T
-    query, key, value = self_columns_back(sums_self[:, :2560])
-    cross_k, cross_v = frame_columns_back(sums_cross[:, 2560:])
+    sums_self = halve(grad_qkv[:, :1280], False)
+    sums_rest = halve(jnp.concatenate([grad_qkv[:, 1280:], grad_gains], axis=1), True)
+
+    gains_out = sums_rest[:, 1280:1284].T
+    query, key, value = self_columns_back(jnp.concatenate([sums_self, sums_rest[:, :1280]], axis=1))
+    cross_k, cross_v = frame_columns_back(sums_kv)
     return (
         result.astype(BF),
         tokens_gradient,
@@ -617,13 +637,13 @@
         query,
         key,
         value,
-        sums_cross[:, :D],
-        query_columns_back(sums_cross[:, 1536:2560]),
+        sums_out[:, :D],
+        query_columns_back(sums_out[:, 1536:]),
         cross_k,
         cross_v,
-        sums_cross[:, D : 2 * D],
-        up_columns_back(sums_feed[:, :FF], devices),
-        down_columns_back(sums_feed[:, FF:]),
+        sums_out[:, D : 2 * D],
+        up_columns_back(sums_up, devices),
+        down_columns_back(sums_down),
     )
 
 

time: 806 us -> 629 us (0.78)
  waiting for transfers between devices: 504 us -> 253 us
  starting transfers between devices: 47.3 us -> 88.7 us
  other arithmetic: 36.1 us -> 68.9 us
  matrix products: 55.6 us -> 44.6 us
  local copies, waits for them, and re-layouts: 70 us -> 79.6 us
    unnamed x8 -> x3, waiting for transfers between devices: 158 us -> 0.05 us
    reduce_scatter x1 -> x0, waiting for transfers between devices: 134 us -> none  [scatter(): lax.psum_scatter(matrix, ALL, scatter_dimension=0, tiled=True).astype(F32)]
    ppermute x0 -> x30, waiting for transfers between devices: none -> 75.3 us  [halve(): came = lax.ppermute(away, ALL, [(s, s ^ 1 << bit) for s in range(devices)])]
    ppermute x0 -> x30, starting transfers between devices: none -> 42.5 us  [halve(): came = lax.ppermute(away, ALL, [(s, s ^ 1 << bit) for s in range(devices)])]
    ppermute x30, waiting for transfers between devices: 81.8 us -> 60.5 us  [swap(): return lax.ppermute(value, LINE, [(s, s ^ mask) for s in range(count)])]
    convert_element_type x1 -> x24, other arithmetic: 0.92 us -> 19.3 us  [halve(): value = value.astype(BF)]
    concatenate x4 -> x3, other arithmetic: 9.85 us -> 27.9 us  [the longest x1 25.3 us: shards(): jnp.concatenate([grad_so, grad_co, grad_cq], axis=1)]
    unnamed x171 -> x173, local copies, waits for them, and re-layouts: 27.5 us -> 16.1 us
  transfers between devices with their start and end apart: 44 -> 71, of which waited for: 30 -> 37; matrix products, arithmetic and copies ran while one was open for 12% -> 24% of each run, Pallas kernels for 4% -> 8%
where the time goes in v2:
time: 629 us; the launch traced here: 620 us
  waiting for transfers between devices  253 us (40%)
  starting transfers between devices  88.7 us (14%)
  local copies, waits for them, and re-layouts  79.6 us (13%)
  Pallas kernels  69.6 us (11%)
  other arithmetic  68.9 us (11%)
  matrix products  44.6 us (7%)
  between operations  16 us (3%)
    ppermute x30, waiting for transfers between devices, halve(): came = lax.ppermute(away, ALL, [(s, s ^ 1 << bit) for s in range(devices)])  75.3 us
    pallas_call x4, Pallas kernels, call(): pl.pallas_call(kernel, out_shape=outs, in_specs=[pl.BlockSpec(memory_spac...  69.6 us
    ppermute x30, waiting for transfers between devices, swap(): return lax.ppermute(value, LINE, [(s, s ^ mask) for s in range(count)])  60.5 us
    all_gather x3, waiting for transfers between devices, gather(): return lax.all_gather(matrix, ALL, axis=0, tiled=True)  55.2 us
    ppermute x4, waiting for transfers between devices, to_previous(): return lax.ppermute(value, LINE, [(s, s - MEM) for s in range(MEM, count)])  46.6 us
    ppermute x30, starting transfers between devices, halve(): came = lax.ppermute(away, ALL, [(s, s ^ 1 << bit) for s in range(devices)])  42.5 us
    ppermute x30, starting transfers between devices, swap(): return lax.ppermute(value, LINE, [(s, s ^ mask) for s in range(count)])  30.5 us
    concatenate x1, other arithmetic, shards(): jnp.concatenate([grad_so, grad_co, grad_cq], axis=1)  25.3 us
  transfers between devices with their start and end apart: 71, of which 37 were waited for; matrix products, arithmetic and copies ran while one was open for 24% of the time, Pallas kernels for 8%

profile of v2, /device:TPU:0, one launch (start us, length us, event | category | flops | bytes accessed | tf_op | source)
XLA Modules:
  0.0 620.4 jit_solution(2207094238551714509)
XLA Ops:
  21.6 55.1 %all-gather.4.cloned.1.call-done = bf16[768,2688]{1,0:T(8,128)(2,1)} async-done(((bf16[24,2688]{1,0:T(8,128)(2,1)}), bf16[768,2688]{1,0:T(8,128)(2,1)}) %all-gather.4.cloned.1.call-update) | async-done | bytes 4128784 | tf_op jit(solution)/shard_map/all_gather | solution.py:499
  85.0 10.5 %collective-permute-done.1.p2 = bf16[256,640]{1,0:T(8,128)(2,1)S(1)} collective-permute-done((bf16[256,640]{1,0:T(8,128)(2,1)}, bf16[256,640]{1,0:T(8,128)(2,1)S(1)}, u32[]{:S(2)}, u32[]{:S(2)}) %collective-permute-start.1) | collective-permute-done | bytes 327712 | tf_op jit(solution)/shard_map/ppermute | solution.py:377
  95.5 8.0 %collective-permute-done.2.p3 = bf16[256,640]{1,0:T(8,128)(2,1)S(1)} collective-permute-done((bf16[256,640]{1,0:T(8,128)(2,1)}, bf16[256,640]{1,0:T(8,128)(2,1)S(1)}, u32[]{:S(2)}, u32[]{:S(2)}) %collective-permute-start.2) | collective-permute-done | bytes 327712 | tf_op jit(solution)/shard_map/ppermute | solution.py:377
  109.6 22.2 %collective-permute-done.3.tail = bf16[256,640]{1,0:T(8,128)(2,1)S(1)} collective-permute-done((bf16[256,640]{1,0:T(8,128)(2,1)}, bf16[256,640]{1,0:T(8,128)(2,1)S(1)}, u32[]{:S(2)}, u32[]{:S(2)}) %collective-permute-start.3) | collective-permute-done | bytes 327712 | tf_op jit(solution)/shard_map/ppermute | solution.py:382
  132.6 11.2 %shard_map.305 = (bf16[256,256]{1,0:T(8,128)(2,1)}, bf16[256,256]{1,0:T(8,128)(2,1)}, bf16[256,256]{1,0:T(8,128)(2,1)}, bf16[256,256]{1,0:T(8,128)(2,1)}, bf16[2...) custom-call(s32[8]{0:T(128)} %stack.50.scal, bf16[256,640]{1,0:T(8,128)(2,1)} %get-tuple-element.112.p0, ...), custom_call_target="tpu_custom_call" | custom-call | flops 3221225472 | bytes 4194304 | tf_op jit(solution)/shard_map/pallas_call | solution.py:322
  145.8 5.4 collective-permute-done.4
  154.3 4.4 collective-permute-done.7
  178.4 5.4 collective-permute-done.10.q3
  185.9 8.5 %collective-permute-done.11.qtail = bf16[256,256]{1,0:T(8,128)(2,1)S(1)} collective-permute-done((bf16[256,256]{1,0:T(8,128)(2,1)S(1)}, bf16[256,256]{1,0:T(8,128)(2,1)S(1)}, u32[]{:S(2)}, u32[]{:S(2)}) %collective-permute-start.11) | collective-permute-done | bytes 131104 | tf_op jit(solution)/shard_map/ppermute | solution.py:382
  195.3 10.0 %collective-permute-done.14.f3 = bf16[375,384]{1,0:T(8,128)(2,1)S(1)} collective-permute-done((bf16[375,384]{1,0:T(8,128)(2,1)S(1)}, bf16[375,384]{1,0:T(8,128)(2,1)S(1)}, u32[]{:S(2)}, u32[]{:S(2)}) %collective-permute-start.14) | collective-permute-done | bytes 288032 | tf_op jit(solution)/shard_map/ppermute | solution.py:377
  206.1 21.5 %shard_map.306 = (bf16[256,256]{1,0:T(8,128)(2,1)}, bf16[256,256]{1,0:T(8,128)(2,1)}, bf16[256,256]{1,0:T(8,128)(2,1)}, bf16[256,256]{1,0:T(8,128)(2,1)}, bf16[2...) custom-call(s32[8]{0:T(128)} %stack.50.scal, bf16[256,256]{1,0:T(8,128)(2,1)} %get-tuple-element.108.q0, ...), custom_call_target="tpu_custom_call" | custom-call | flops 6442450944 | bytes 4194304 | tf_op jit(solution)/shard_map/pallas_call | solution.py:322
  227.6 5.1 collective-permute-start.15
  232.7 6.1 collective-permute-done.15
  239.9 9.0 %collective-permute-start.18 = (bf16[256,256]{1,0:T(8,128)(2,1)S(1)}, bf16[256,256]{1,0:T(8,128)(2,1)S(1)}, u32[]{:S(2)}, u32[]{:S(2)}) collective-permute-start(bf16[256,256]{1,0:T(8,128)(2,1)S(1)} %get-tuple-element.218), channel_id=1, source_target_pairs={{0,3},{1,2},{2,1},{3,0},{4,7},{5,6},{6,5},{7,4},{8,11},{9,10},{10,... | collective-permute-start | bytes 393224 | tf_op jit(solution)/shard_map/ppermute | solution.py:377
  249.8 4.5 collective-permute-done.18
  260.7 9.7 %multiply_convert_fusion = (bf16[256,3072]{1,0:T(8,128)(2,1)S(1)}, f32[256,3072]{1,0:T(8,128)S(1)}, f32[256,3072]{1,0:T(8,128)S(1)}) fusion(bf16[768,6144]{1,0:T(8,128)(2,1)} %all-gather.8.cloned.1.call-done, f32[256,768]{1,0:T(8,128)S(1)} %get-tuple-element.285, f32[768]{0:T(1024)S(1)} %get-tuple-element.82, f32[256]{0:T(256)S(1)} %fusion.119, ...), kind=kOutput, calls=%fused_computation.23 | convolution fusion | flops 1259864064 | bytes 13374464 | tf_op jit(solution)/shard_map/dot_general | solution.py:39
  292.9 6.6 %copy.148 = bf16[768,3072]{1,0:T(8,128)(2,1)} copy(bf16[768,3072]{0,1:T(8,128)(2,1)} %pad_maximum_fusion) | data formatting | bytes 9437184 | tf_op jit(solution)/shard_map/concatenate | solution.py:594
  305.8 7.3 %collective-permute-done.22.gtail = bf16[256,256]{1,0:T(8,128)(2,1)S(1)} collective-permute-done((bf16[256,256]{1,0:T(8,128)(2,1)S(1)}, bf16[256,256]{1,0:T(8,128)(2,1)S(1)}, u32[]{:S(2)}, u32[]{:S(2)}) %collective-permute-start.22) | collective-permute-done | bytes 131104 | tf_op jit(solution)/shard_map/ppermute | solution.py:382
  313.8 22.2 %shard_map.307 = (bf16[256,256]{1,0:T(8,128)(2,1)}, bf16[256,256]{1,0:T(8,128)(2,1)}, bf16[256,256]{1,0:T(8,128)(2,1)}, bf16[256,256]{1,0:T(8,128)(2,1)}, bf16[2...) custom-call(s32[8]{0:T(128)} %stack.50.scal, ...), custom_call_target="tpu_custom_call" | custom-call | flops 17179869184 | bytes 4194304 | tf_op jit(solution)/shard_map/pallas_call | solution.py:322
  357.1 25.3 %pad_maximum_fusion.1 = bf16[768,2560]{1,0:T(8,128)(2,1)S(1)} fusion(bf16[768,1024]{1,0:T(8,128)(2,1)S(1)} %convolution_convert_fusion.5, bf16[192,768]{1,0:T(8,128)(2,1)S(1)} %get-tuple-element.138, bf16[192,768]{1,0:T(8,128)(2,1)S(1)} %get-tuple-element.139, bf16[192,768]{1,0:T(8,128)(2,1)S(1)} %get-tuple-element.140, ...), kind=kLoop, calls=%fused_computation.12 | loop fusion | flops 35389440 | bytes 7864320 | tf_op jit(solution)/shard_map/concatenate | solution.py:615
  390.5 8.5 %collective-permute-done.30.gtail = bf16[256,256]{1,0:T(8,128)(2,1)S(1)} collective-permute-done((bf16[256,256]{1,0:T(8,128)(2,1)S(1)}, bf16[256,256]{1,0:T(8,128)(2,1)S(1)}, u32[]{:S(2)}, u32[]{:S(2)}) %collective-permute-start.30) | collective-permute-done | bytes 131104 | tf_op jit(solution)/shard_map/ppermute | solution.py:382
  399.7 14.7 %shard_map.308 = (bf16[256,640]{1,0:T(8,128)(2,1)}, bf16[256,640]{1,0:T(8,128)(2,1)}, bf16[256,640]{1,0:T(8,128)(2,1)}, bf16[256,640]{1,0:T(8,128)(2,1)}, bf16[256,640]{1,0:T(8,128)(2,1)}) custom-call(s32[8]{0:T(128)} %stack.50.scal, bf16[256,640]{1,0:T(8,128)(2,1)} %get-tuple-element.112.p0, bf16[256,640]{1,0:T(8,128)(2,1)} %copy-done.34, ...), custom_call_target="tpu_custom_call" | custom-call | flops 8589934592 | bytes 4194304 | tf_op jit(solution)/shard_map/pallas_call | solution.py:322
  428.3 3.8 fusion.20
  436.5 5.4 collective-permute-done.33
  458.5 11.4 %collective-permute-done.54 = bf16[2,2,2,24,1536]{4,3,1,2,0:T(8,128)(2,1)S(1)} collective-permute-done((bf16[2,2,2,24,1536]{4,3,1,2,0:T(8,128)(2,1)S(1)}, bf16[2,2,2,24,1536]{4,3,1,2,0:T(8,128)(2,1)S(1)}, u32[]{:S(2)}, u32[]{:S(2)}) %collective-permute-start.54) | collective-permute-done | bytes 589856 | tf_op jit(solution)/shard_map/ppermute | solution.py:515
  503.6 12.5 %collective-permute-done.44 = bf16[2,2,2,24,1280]{4,3,1,2,0:T(8,128)(2,1)} collective-permute-done((bf16[2,2,2,24,1280]{4,3,1,2,0:T(8,128)(2,1)}, bf16[2,2,2,24,1280]{4,3,1,2,0:T(8,128)(2,1)}, u32[]{:S(2)}, u32[]{:S(2)}) %collective-permute-start.44) | collective-permute-done | bytes 491552 | tf_op jit(solution)/shard_map/ppermute | solution.py:515
  533.2 9.1 %collective-permute-done.40 = bf16[2,2,24,1408]{3,2,0,1:T(8,128)(2,1)S(1)} collective-permute-done((bf16[2,2,24,1408]{3,2,0,1:T(8,128)(2,1)S(1)}, bf16[2,2,24,1408]{3,2,0,1:T(8,128)(2,1)S(1)}, u32[]{:S(2)}, u32[]{:S(2)}) %collective-permute-start.40) | collective-permute-done | bytes 270368 | tf_op jit(solution)/shard_map/ppermute | solution.py:515
  565.0 3.7 collective-permute-done.50
  571.5 7.2 %collective-permute-done.60 = bf16[2,2,24,3072]{3,2,0,1:T(8,128)(2,1)S(1)} collective-permute-done((bf16[2,2,24,3072]{3,2,0,1:T(8,128)(2,1)S(1)}, bf16[2,2,24,3072]{3,2,0,1:T(8,128)(2,1)S(1)}, u32[]{:S(2)}, u32[]{:S(2)}) %collective-permute-start.60) | collective-permute-done | bytes 589856 | tf_op jit(solution)/shard_map/ppermute | solution.py:515
  581.8 8.9 %collective-permute-done.52 = bf16[24,2560]{1,0:T(8,128)(2,1)S(1)} collective-permute-done((bf16[24,2560]{1,0:T(8,128)(2,1)S(1)}, bf16[24,2560]{1,0:T(8,128)(2,1)S(1)}, u32[]{:S(2)}, u32[]{:S(2)}) %collective-permute-start.52) | collective-permute-done | bytes 122912 | tf_op jit(solution)/shard_map/ppermute | solution.py:515
  596.9 8.2 %collective-permute-done.62 = bf16[24,3072]{1,0:T(8,128)(2,1)S(1)} collective-permute-done((bf16[24,3072]{1,0:T(8,128)(2,1)S(1)}, bf16[24,3072]{1,0:T(8,128)(2,1)S(1)}, u32[]{:S(2)}, u32[]{:S(2)}) %collective-permute-start.62) | collective-permute-done | bytes 147488 | tf_op jit(solution)/shard_map/ppermute | solution.py:515
  608.7 4.0 reshape.252
  (499 shorter events, 248.9 us)
Async XLA Ops:
  7.2 69.5 %all-gather.4.cloned.1.call-start = ((), (), s32[]{:S(2)}) async-start(), calls=%async_computation | async-start | bytes 4257792 | tf_op jit(solution)/shard_map/all_gather | solution.py:499
  12.4 149.9 %all-gather.6.cloned.1.call-start = ((), (), s32[]{:S(2)}) async-start(), calls=%async_computation.1 | async-start | bytes 6488064 | tf_op jit(solution)/shard_map/all_gather | solution.py:499
  16.7 244.0 %all-gather.8.cloned.1.call-start = ((), (), s32[]{:S(2)}) async-start(), calls=%async_computation.2 | async-start | bytes 9732096 | tf_op jit(solution)/shard_map/all_gather | solution.py:499
  84.2 19.2 %collective-permute-start.2 = (bf16[256,640]{1,0:T(8,128)(2,1)}, bf16[256,640]{1,0:T(8,128)(2,1)S(1)}, u32[]{:S(2)}, u32[]{:S(2)}) collective-permute-start(bf16[256,640]{1,0:T(8,128)(2,1)} %get-tuple-element.145), channel_id=1, source_target_pairs={{0,3},{1,2},{2,1},{3,0},{4,7},{5,6},{6,5},{7,4},{8,11},{9,10},{10,... | collective-permute-start | bytes 983048 | tf_op jit(solution)/shard_map/ppermute | solution.py:377
  84.5 19.0 %collective-permute-start = (bf16[256,640]{1,0:T(8,128)(2,1)}, bf16[256,640]{1,0:T(8,128)(2,1)S(1)}, u32[]{:S(2)}, u32[]{:S(2)}) collective-permute-start(bf16[256,640]{1,0:T(8,128)(2,1)} %get-tuple-element.144), channel_id=1, source_target_pairs={{0,1},{1,0},{2,3},{3,2},{4,5},{5,4},{6,7},{7,6},{8,9},{9,8},{10,11... | collective-permute-start | bytes 983048 | tf_op jit(solution)/shard_map/ppermute | solution.py:377
  104.5 27.3 %collective-permute-start.3 = (bf16[256,640]{1,0:T(8,128)(2,1)}, bf16[256,640]{1,0:T(8,128)(2,1)S(1)}, u32[]{:S(2)}, u32[]{:S(2)}) collective-permute-start(bf16[256,640]{1,0:T(8,128)(2,1)} %get-tuple-element.111), channel_id=1, source_target_pairs={{4,0},{5,1},{6,2},{7,3},{12,8},{13,9},{14,10},{15,11},{20,16},{21,... | collective-permute-start | bytes 983048 | tf_op jit(solution)/shard_map/ppermute | solution.py:382
  174.9 19.5 %collective-permute-start.12 = (bf16[375,384]{1,0:T(8,128)(2,1)S(1)}, bf16[375,384]{1,0:T(8,128)(2,1)S(1)}, u32[]{:S(2)}, u32[]{:S(2)}) collective-permute-start(bf16[375,384]{1,0:T(8,128)(2,1)S(1)} %get-tuple-element.153), channel_id=1, source_target_pairs={{0,1},{1,0},{2,3},{3,2},{4,5},{5,4},{6,7},{7,6},{8,9},{9,8},{10,11... | collective-permute-start | bytes 864008 | tf_op jit(solution)/shard_map/ppermute | solution.py:377
  175.2 20.1 %collective-permute-start.13 = (bf16[375,384]{1,0:T(8,128)(2,1)S(1)}, bf16[375,384]{1,0:T(8,128)(2,1)S(1)}, u32[]{:S(2)}, u32[]{:S(2)}) collective-permute-start(bf16[375,384]{1,0:T(8,128)(2,1)S(1)} %get-tuple-element.152), channel_id=1, source_target_pairs={{0,2},{1,3},{2,0},{3,1},{4,6},{5,7},{6,4},{7,5},{8,10},{9,11},{10,... | collective-permute-start | bytes 864008 | tf_op jit(solution)/shard_map/ppermute | solution.py:377
  178.4 26.9 %collective-permute-start.14 = (bf16[375,384]{1,0:T(8,128)(2,1)S(1)}, bf16[375,384]{1,0:T(8,128)(2,1)S(1)}, u32[]{:S(2)}, u32[]{:S(2)}) collective-permute-start(bf16[375,384]{1,0:T(8,128)(2,1)S(1)} %get-tuple-element.151), channel_id=1, source_target_pairs={{0,3},{1,2},{2,1},{3,0},{4,7},{5,6},{6,5},{7,4},{8,11},{9,10},{10,... | collective-permute-start | bytes 864008 | tf_op jit(solution)/shard_map/ppermute | solution.py:377
  344.7 43.5 %collective-permute-start.36 = (bf16[375,384]{1,0:T(8,128)(2,1)S(1)}, bf16[375,384]{1,0:T(8,128)(2,1)S(1)}, u32[]{:S(2)}, u32[]{:S(2)}) collective-permute-start(bf16[375,384]{1,0:T(8,128)(2,1)S(1)} %copy-done.72), channel_id=1, source_target_pairs={{0,2},{1,3},{2,0},{3,1},{4,6},{5,7},{6,4},{7,5},{8,10},{9,11},{10,... | collective-permute-start | bytes 864008 | tf_op jit(solution)/shard_map/ppermute | solution.py:377
  346.4 43.0 %collective-permute-start.37 = (bf16[375,384]{1,0:T(8,128)(2,1)S(1)}, bf16[375,384]{1,0:T(8,128)(2,1)S(1)}, u32[]{:S(2)}, u32[]{:S(2)}) collective-permute-start(bf16[375,384]{1,0:T(8,128)(2,1)S(1)} %copy-done.71), channel_id=1, source_target_pairs={{0,3},{1,2},{2,1},{3,0},{4,7},{5,6},{6,5},{7,4},{8,11},{9,10},{10,... | collective-permute-start | bytes 864008 | tf_op jit(solution)/shard_map/ppermute | solution.py:377
  346.5 42.9 %collective-permute-start.35 = (bf16[375,384]{1,0:T(8,128)(2,1)S(1)}, bf16[375,384]{1,0:T(8,128)(2,1)S(1)}, u32[]{:S(2)}, u32[]{:S(2)}) collective-permute-start(bf16[375,384]{1,0:T(8,128)(2,1)S(1)} %copy-done.70), channel_id=1, source_target_pairs={{0,1},{1,0},{2,3},{3,2},{4,5},{5,4},{6,7},{7,6},{8,9},{9,8},{10,11... | collective-permute-start | bytes 864008 | tf_op jit(solution)/shard_map/ppermute | solution.py:377
  356.1 26.3 %collective-permute-start.28 = (bf16[256,256]{1,0:T(8,128)(2,1)S(1)}, bf16[256,256]{1,0:T(8,128)(2,1)S(1)}, u32[]{:S(2)}, u32[]{:S(2)}) collective-permute-start(bf16[256,256]{1,0:T(8,128)(2,1)S(1)} %get-tuple-element.158), channel_id=1, source_target_pairs={{0,2},{1,3},{2,0},{3,1},{4,6},{5,7},{6,4},{7,5},{8,10},{9,11},{10,... | collective-permute-start | bytes 393224 | tf_op jit(solution)/shard_map/ppermute | solution.py:377
  356.2 30.7 %collective-permute-start.29 = (bf16[256,256]{1,0:T(8,128)(2,1)S(1)}, bf16[256,256]{1,0:T(8,128)(2,1)S(1)}, u32[]{:S(2)}, u32[]{:S(2)}) collective-permute-start(bf16[256,256]{1,0:T(8,128)(2,1)S(1)} %get-tuple-element.157), channel_id=1, source_target_pairs={{0,3},{1,2},{2,1},{3,0},{4,7},{5,6},{6,5},{7,4},{8,11},{9,10},{10,... | collective-permute-start | bytes 393224 | tf_op jit(solution)/shard_map/ppermute | solution.py:377
  386.9 83.3 %collective-permute-start.58 = (bf16[2,2,2,2,24,3072]{5,4,2,3,0,1:T(8,128)(2,1)}, bf16[2,2,2,2,24,3072]{5,4,2,3,0,1:T(8,128)(2,1)}, u32[]{:S(2)}, u32[]{:S(2)}) collective-permute-start(bf16[2,2,2,2,24,3072]{5,4,2,3,0,1:T(8,128)(2,1)} %bitcast.212), channel_id=1, source_target_pairs={{0,1},{1,0},{2,3},{3,2},{4,5},{5,4},{6,7},{7,6},{8,9},{9,8},{10,11... | collective-permute-start | bytes 7077896 | tf_op jit(solution)/shard_map/ppermute | solution.py:515
  386.9 88.9 %collective-permute-start.63 = (bf16[2,2,2,2,24,3072]{5,4,3,2,1,0:T(8,128)(2,1)}, bf16[2,2,2,2,24,3072]{5,4,3,2,1,0:T(8,128)(2,1)}, u32[]{:S(2)}, u32[]{:S(2)}) collective-permute-start(bf16[2,2,2,2,24,3072]{5,4,3,2,1,0:T(8,128)(2,1)} %dynamic-slice_bitcast_fusion), channel_id=1, source_target_pairs={{0,1},{1,0},{2,3},{3,2},{4,5},{5,4},{6,7},{7,6},{8,9},{9,8},{10,11... | collective-permute-start | bytes 7077896 | tf_op jit(solution)/shard_map/ppermute | solution.py:515
  426.6 15.3 %collective-permute-start.33 = (bf16[256,640]{1,0:T(8,128)(2,1)S(1)}, bf16[256,640]{1,0:T(8,128)(2,1)S(1)}, u32[]{:S(2)}, u32[]{:S(2)}) collective-permute-start(bf16[256,640]{1,0:T(8,128)(2,1)S(1)} %get-tuple-element.176), channel_id=1, source_target_pairs={{0,2},{1,3},{2,0},{3,1},{4,6},{5,7},{6,4},{7,5},{8,10},{9,11},{10,... | collective-permute-start | bytes 983048 | tf_op jit(solution)/shard_map/ppermute | solution.py:377
  433.7 49.0 %collective-permute-start.48 = (bf16[2,2,2,2,24,2560]{5,4,2,3,0,1:T(8,128)(2,1)}, bf16[2,2,2,2,24,2560]{5,4,2,3,0,1:T(8,128)(2,1)}, u32[]{:S(2)}, u32[]{:S(2)}) collective-permute-start(bf16[2,2,2,2,24,2560]{5,4,2,3,0,1:T(8,128)(2,1)} %bitcast.213), channel_id=1, source_target_pairs={{0,1},{1,0},{2,3},{3,2},{4,5},{5,4},{6,7},{7,6},{8,9},{9,8},{10,11... | collective-permute-start | bytes 5898248 | tf_op jit(solution)/shard_map/ppermute | solution.py:515
  451.5 36.6 %collective-permute-start.38 = (bf16[2,2,2,2,24,1408]{5,4,2,3,1,0:T(8,128)(2,1)S(1)}, bf16[2,2,2,2,24,1408]{5,4,2,3,1,0:T(8,128)(2,1)S(1)}, u32[]{:S(2)}, u32[]{:S(2)}) collective-permute-start(bf16[2,2,2,2,24,1408]{5,4,2,3,1,0:T(8,128)(2,1)S(1)} %bitcast.228), channel_id=1, source_target_pairs={{0,1},{1,0},{2,3},{3,2},{4,5},{5,4},{6,7},{7,6},{8,9},{9,8},{10,11... | collective-permute-start | bytes 3244040 | tf_op jit(solution)/shard_map/ppermute | solution.py:515
  454.2 15.8 %collective-permute-start.54 = (bf16[2,2,2,24,1536]{4,3,1,2,0:T(8,128)(2,1)S(1)}, bf16[2,2,2,24,1536]{4,3,1,2,0:T(8,128)(2,1)S(1)}, u32[]{:S(2)}, u32[]{:S(2)}) collective-permute-start(bf16[2,2,2,24,1536]{4,3,1,2,0:T(8,128)(2,1)S(1)} %dynamic-slice_bitcast_fusion.6), channel_id=1, source_target_pairs={{0,16},{1,17},{2,18},{3,19},{4,20},{5,21},{6,22},{7,23},{8,24},{9,... | collective-permute-start | bytes 1769480 | tf_op jit(solution)/shard_map/ppermute | solution.py:515
  470.2 17.3 %collective-permute-start.55 = (bf16[2,2,24,1536]{3,2,0,1:T(8,128)(2,1)S(1)}, bf16[2,2,24,1536]{3,2,0,1:T(8,128)(2,1)S(1)}, u32[]{:S(2)}, u32[]{:S(2)}) collective-permute-start(bf16[2,2,24,1536]{3,2,0,1:T(8,128)(2,1)S(1)} %dynamic-slice_bitcast_fusion.12), channel_id=1, source_target_pairs={{0,8},{1,9},{2,10},{3,11},{4,12},{5,13},{6,14},{7,15},{8,0},{9,1},... | collective-permute-start | bytes 884744 | tf_op jit(solution)/shard_map/ppermute | solution.py:515
  475.8 83.2 %collective-permute-start.59 = (bf16[2,2,2,24,3072]{4,3,1,2,0:T(8,128)(2,1)}, bf16[2,2,2,24,3072]{4,3,1,2,0:T(8,128)(2,1)}, u32[]{:S(2)}, u32[]{:S(2)}) collective-permute-start(bf16[2,2,2,24,3072]{4,3,1,2,0:T(8,128)(2,1)} %dynamic-slice_bitcast_fusion.2), channel_id=1, source_target_pairs={{0,8},{1,9},{2,10},{3,11},{4,12},{5,13},{6,14},{7,15},{8,0},{9,1},... | collective-permute-start | bytes 3538952 | tf_op jit(solution)/shard_map/ppermute | solution.py:515
  479.8 81.6 %collective-permute-start.64 = (bf16[2,2,2,24,3072]{4,3,2,1,0:T(8,128)(2,1)}, bf16[2,2,2,24,3072]{4,3,2,1,0:T(8,128)(2,1)}, u32[]{:S(2)}, u32[]{:S(2)}) collective-permute-start(bf16[2,2,2,24,3072]{4,3,2,1,0:T(8,128)(2,1)} %dynamic-slice_bitcast_fusion.1), channel_id=1, source_target_pairs={{0,16},{1,17},{2,18},{3,19},{4,20},{5,21},{6,22},{7,23},{8,24},{9,... | collective-permute-start | bytes 3538952 | tf_op jit(solution)/shard_map/ppermute | solution.py:515
  482.7 33.3 %collective-permute-start.44 = (bf16[2,2,2,24,1280]{4,3,1,2,0:T(8,128)(2,1)}, bf16[2,2,2,24,1280]{4,3,1,2,0:T(8,128)(2,1)}, u32[]{:S(2)}, u32[]{:S(2)}) collective-permute-start(bf16[2,2,2,24,1280]{4,3,1,2,0:T(8,128)(2,1)} %dynamic-slice_bitcast_fusion.9), channel_id=1, source_target_pairs={{0,8},{1,9},{2,10},{3,11},{4,12},{5,13},{6,14},{7,15},{8,0},{9,1},... | collective-permute-start | bytes 1474568 | tf_op jit(solution)/shard_map/ppermute | solution.py:515
  487.4 63.6 %collective-permute-start.49 = (bf16[2,2,2,24,2560]{4,3,1,2,0:T(8,128)(2,1)}, bf16[2,2,2,24,2560]{4,3,1,2,0:T(8,128)(2,1)}, u32[]{:S(2)}, u32[]{:S(2)}) collective-permute-start(bf16[2,2,2,24,2560]{4,3,1,2,0:T(8,128)(2,1)} %dynamic-slice_bitcast_fusion.3), channel_id=1, source_target_pairs={{0,8},{1,9},{2,10},{3,11},{4,12},{5,13},{6,14},{7,15},{8,0},{9,1},... | collective-permute-start | bytes 2949128 | tf_op jit(solution)/shard_map/ppermute | solution.py:515
  499.1 20.7 %collective-permute-start.39 = (bf16[2,2,2,24,1408]{4,3,1,2,0:T(8,128)(2,1)}, bf16[2,2,2,24,1408]{4,3,1,2,0:T(8,128)(2,1)S(1)}, u32[]{:S(2)}, u32[]{:S(2)}) collective-permute-start(bf16[2,2,2,24,1408]{4,3,1,2,0:T(8,128)(2,1)} %dynamic-slice_bitcast_fusion.7), channel_id=1, source_target_pairs={{0,16},{1,17},{2,18},{3,19},{4,20},{5,21},{6,22},{7,23},{8,24},{9,... | collective-permute-start | bytes 1622024 | tf_op jit(solution)/shard_map/ppermute | solution.py:515
  526.6 15.8 %collective-permute-start.40 = (bf16[2,2,24,1408]{3,2,0,1:T(8,128)(2,1)S(1)}, bf16[2,2,24,1408]{3,2,0,1:T(8,128)(2,1)S(1)}, u32[]{:S(2)}, u32[]{:S(2)}) collective-permute-start(bf16[2,2,24,1408]{3,2,0,1:T(8,128)(2,1)S(1)} %dynamic-slice_bitcast_fusion.17), channel_id=1, source_target_pairs={{0,8},{1,9},{2,10},{3,11},{4,12},{5,13},{6,14},{7,15},{8,0},{9,1},... | collective-permute-start | bytes 811016 | tf_op jit(solution)/shard_map/ppermute | solution.py:515
  554.3 14.4 %collective-permute-start.50 = (bf16[2,2,24,2560]{3,2,0,1:T(8,128)(2,1)}, bf16[2,2,24,2560]{3,2,0,1:T(8,128)(2,1)}, u32[]{:S(2)}, u32[]{:S(2)}) collective-permute-start(bf16[2,2,24,2560]{3,2,0,1:T(8,128)(2,1)} %dynamic-slice_bitcast_fusion.8), channel_id=1, source_target_pairs={{0,16},{1,17},{2,18},{3,19},{4,20},{5,21},{6,22},{7,23},{8,24},{9,... | collective-permute-start | bytes 1474568 | tf_op jit(solution)/shard_map/ppermute | solution.py:515
  561.1 17.7 %collective-permute-start.60 = (bf16[2,2,24,3072]{3,2,0,1:T(8,128)(2,1)S(1)}, bf16[2,2,24,3072]{3,2,0,1:T(8,128)(2,1)S(1)}, u32[]{:S(2)}, u32[]{:S(2)}) collective-permute-start(bf16[2,2,24,3072]{3,2,0,1:T(8,128)(2,1)S(1)} %dynamic-slice_bitcast_fusion.5), channel_id=1, source_target_pairs={{0,16},{1,17},{2,18},{3,19},{4,20},{5,21},{6,22},{7,23},{8,24},{9,... | collective-permute-start | bytes 1769480 | tf_op jit(solution)/shard_map/ppermute | solution.py:515
  563.2 17.5 %collective-permute-start.65 = (bf16[2,2,24,3072]{3,2,1,0:T(8,128)(2,1)S(1)}, bf16[2,2,24,3072]{3,2,1,0:T(8,128)(2,1)S(1)}, u32[]{:S(2)}, u32[]{:S(2)}) collective-permute-start(bf16[2,2,24,3072]{3,2,1,0:T(8,128)(2,1)S(1)} %dynamic-slice_bitcast_fusion.4), channel_id=1, source_target_pairs={{0,8},{1,9},{2,10},{3,11},{4,12},{5,13},{6,14},{7,15},{8,0},{9,1},... | collective-permute-start | bytes 1769480 | tf_op jit(solution)/shard_map/ppermute | solution.py:515
  581.3 14.8 %collective-permute-start.66 = (bf16[2,24,3072]{2,1,0:T(8,128)(2,1)S(1)}, bf16[2,24,3072]{2,1,0:T(8,128)(2,1)S(1)}, u32[]{:S(2)}, u32[]{:S(2)}) collective-permute-start(bf16[2,24,3072]{2,1,0:T(8,128)(2,1)S(1)} %dynamic-slice_bitcast_fusion.10), channel_id=1, source_target_pairs={{0,2},{1,3},{2,0},{3,1},{4,6},{5,7},{6,4},{7,5},{8,10},{9,11},{10,... | collective-permute-start | bytes 884744 | tf_op jit(solution)/shard_map/ppermute | solution.py:515
  596.2 16.4 %collective-permute-start.67 = (bf16[24,3072]{1,0:T(8,128)(2,1)S(1)}, bf16[24,3072]{1,0:T(8,128)(2,1)S(1)}, u32[]{:S(2)}, u32[]{:S(2)}) collective-permute-start(bf16[24,3072]{1,0:T(8,128)(2,1)S(1)} %dynamic-slice_bitcast_fusion.20), channel_id=1, source_target_pairs={{0,4},{1,5},{2,6},{3,7},{4,0},{5,1},{6,2},{7,3},{8,12},{9,13},{10,... | collective-permute-start | bytes 442376 | tf_op jit(solution)/shard_map/ppermute | solution.py:515
  (118 other events, 1232.4 us)
Sparse Core Ops, SparseCore 0:
  12.5 64.1 all-gather.3
  80.3 77.6 all-gather.5
  161.6 92.8 all-gather.7

commit v3 on v1

--- a/solution.py
+++ b/solution.py
@@ -86,6 +86,10 @@
         whole[pl.ds(MEM * step, tail.shape[0]), :] = tail[...]
 
 
+def parts_of(ref):
+    return [ref.at[j * ROWS : (j + 1) * ROWS] for j in range(MEM + 1)]
+
+
 def scatter_rows(scal, whole, pieces, tail, step):
     for j in range(MEM):
         start = pl.multiple_of(scal[j] * step, step)
@@ -115,8 +119,9 @@
     scatter_rows(scal, out, outs, tail, ROWS)
 
 
-def self_forward_kernel(scal, p0, p1, p2, p3, tail, o0, o1, o2, o3, otail, ot, lse, whole, qa, ka, vt, out):
-    gather_rows(scal, (p0, p1, p2, p3), tail, whole, ROWS)
+def self_forward_kernel(scal, rows, o0, o1, o2, o3, otail, ot, lse, whole, qa, ka, vt, out):
+    *pieces, tail = parts_of(rows)
+    gather_rows(scal, pieces, tail, whole, ROWS)
     self_prepare(scal, whole, qa, ka)
     turned = whole[:, 256:384].astype(F32).T.astype(BF)
     vt[0] = turned[0:HD]
@@ -166,11 +171,11 @@
 
 
 def self_backward_kernel(
-    scal, p0, p1, p2, p3, tail, g0, g1, g2, g3, gtail, ot, lse,
-    d0, d1, d2, d3, dtail,
+    scal, rows, g0, g1, g2, g3, gtail, ot, lse, drows,
     whole, grads, qa, ka, qm, kt, vm, dm, delta, dqt, dk, dv, out,
 ):
-    gather_rows(scal, (p0, p1, p2, p3), tail, whole, ROWS)
+    *pieces, tail = parts_of(rows)
+    gather_rows(scal, pieces, tail, whole, ROWS)
     gather_rows(scal, (g0, g1, g2, g3), gtail, grads, ROWS)
     self_prepare(scal, whole, qa, ka)
     grads_prepare(scal, grads, ot, dm, delta)
@@ -219,7 +224,8 @@
         out[a:b, 256:384] = dv[0, a:b, :].astype(BF)
         out[a:b, 384:512] = (query[:, 128:256] + pltpu.roll(dk[1, a:b, :], HD, 1)).astype(BF)
         out[a:b, 512:640] = dv[1, a:b, :].astype(BF)
-    scatter_rows(scal, out, (d0, d1, d2, d3), dtail, ROWS)
+    *pieces, tail = parts_of(drows)
+    scatter_rows(scal, out, pieces, tail, ROWS)
 
 
 def cross_prepare(whole, queries, qa, ka):
@@ -237,7 +243,8 @@
     whole, queries, qa, ka, vt, out,
 ):
     whole[...] = jnp.zeros_like(whole)
-    gather_rows(scal, (f0, f1, f2, f3), None, whole, FP)
+    for j, piece in enumerate((f0, f1, f2, f3)):
+        whole[j * FP : j * FP + FR, :] = piece[...]
     gather_rows(scal, (q0, q1, q2, q3), qtail, queries, ROWS)
     cross_prepare(whole, queries, qa, ka)
     turned = whole[:, 128:256].astype(F32).T.astype(BF)
@@ -267,7 +274,8 @@
     whole, queries, grads, qa, ka, qm, kt, vm, dm, delta, dqt, dk, dv, out, fout,
 ):
     whole[...] = jnp.zeros_like(whole)
-    gather_rows(scal, (f0, f1, f2, f3), None, whole, FP)
+    for j, piece in enumerate((f0, f1, f2, f3)):
+        whole[j * FP : j * FP + FR, :] = piece[...]
     gather_rows(scal, (q0, q1, q2, q3), qtail, queries, ROWS)
     gather_rows(scal, (g0, g1, g2, g3), gtail, grads, ROWS)
     cross_prepare(whole, queries, qa, ka)
@@ -306,7 +314,8 @@
     fout[:, 0:128] = dk[0].astype(BF)
     fout[:, 128:256] = dv[0].astype(BF)
     fout[:, 256:384] = (dk[1] + pltpu.roll(dv[1], HD, 1)).astype(BF)
-    scatter_rows(scal, fout, (e0, e1, e2, e3), None, FP)
+    for j, piece in enumerate((e0, e1, e2, e3)):
+        piece[...] = fout[j * FP : j * FP + FR, :]
 
 
 def shape(*dims, dtype=BF):
@@ -330,35 +339,35 @@
     )(scal, *args)
 
 
-def self_forward(scal, pieces):
+def self_forward(scal, rows):
     outs = [shape(ROWS, 256)] * 5 + [shape(256, WIDE, dtype=F32), shape(HEADS, 8, WIDE, dtype=F32)]
     scratch = [vmem(WIDE, 640), vmem(HEADS, WIDE, 128), vmem(HEADS, WIDE, 128), vmem(HEADS, HD, WIDE), vmem(WIDE, 256)]
-    got = call(self_forward_kernel, scal, pieces, outs, scratch, 3 << 30, 3 << 20)
+    got = call(self_forward_kernel, scal, [rows], outs, scratch, 3 << 30, 3 << 20)
     return (got[:5], got[5:])
 
 
-def self_backward(scal, pieces, grads, kept):
-    outs = [shape(ROWS, 640)] * 5
+def self_backward(scal, rows, grads, kept):
+    outs = [shape(WIDE, 640)]
     head = vmem(HEADS, WIDE, 128)
     scratch = [
         vmem(WIDE, 640), vmem(WIDE, 256), head, head, head, vmem(HEADS, HD, WIDE), head, head,
         vmem(HEADS, 8, WIDE, dtype=F32), vmem(256, WIDE, dtype=F32),
         vmem(2, WIDE, 128, dtype=F32), vmem(2, WIDE, 128, dtype=F32), vmem(WIDE, 640),
     ]
-    return call(self_backward_kernel, scal, [*pieces, *grads, *kept], outs, scratch, 8 << 30, 3 << 20)
-
-
-def cross_forward(scal, queries, pieces):
+    return call(self_backward_kernel, scal, [rows, *grads, *kept], outs, scratch, 8 << 30, 3 << 20)[0]
+
+
+def cross_forward(scal, queries, frames):
     outs = [shape(ROWS, 256)] * 5 + [shape(256, WIDE, dtype=F32), shape(HEADS, 8, WIDE, dtype=F32)]
     scratch = [
         vmem(KEYS, 384), vmem(WIDE, 256), vmem(HEADS, WIDE, 128), vmem(HEADS, KEYS, 128),
         vmem(HEADS, HD, KEYS), vmem(WIDE, 256),
     ]
-    got = call(cross_forward_kernel, scal, [*queries, *pieces], outs, scratch, 6 << 30, 6 << 20)
+    got = call(cross_forward_kernel, scal, [*queries, *frames], outs, scratch, 6 << 30, 6 << 20)
     return (got[:5], got[5:])
 
 
-def cross_backward(scal, queries, pieces, grads, kept):
+def cross_backward(scal, queries, frames, grads, kept):
     outs = [shape(ROWS, 256)] * 5 + [shape(FR, 384)] * 4
     head, keys = (vmem(HEADS, WIDE, 128), vmem(HEADS, KEYS, 128))
     scratch = [
@@ -366,7 +375,7 @@
         vmem(HEADS, 8, WIDE, dtype=F32), vmem(256, WIDE, dtype=F32),
         vmem(2, KEYS, 128, dtype=F32), vmem(2, KEYS, 128, dtype=F32), vmem(WIDE, 256), vmem(KEYS, 384),
     ]
-    got = call(cross_backward_kernel, scal, [*queries, *pieces, *grads, *kept], outs, scratch, 16 << 30, 6 << 20)
+    got = call(cross_backward_kernel, scal, [*queries, *frames, *grads, *kept], outs, scratch, 16 << 30, 6 << 20)
     return (got[:5], got[5:])
 
 
@@ -396,6 +405,30 @@
 
 def with_tail(member, pieces):
     return [*pieces, to_previous(lax.select_n(member, *pieces))]
+
+
+def token_tail(member, pieces):
+    count = lax.axis_size("grp") * MEM
+    even = lax.ppermute(
+        lax.select_n(member, *pieces), LINE, [(s, s - MEM) for s in range(MEM, count, 2)]
+    )
+    odd = lax.ppermute(even, LINE, [(s, s + 1) for s in range(0, count, 2)])
+    return jnp.where(member % 2 == 0, even, odd)
+
+
+def total_rows(member, partial):
+    core = member % 2
+    half = ROWS // 2
+    tail = partial[MEM * ROWS :].reshape(2, half, D)
+    late = swap(lax.dynamic_index_in_dim(tail, 1 - core, keepdims=False).astype(BF), 1).astype(F32)
+    late = to_next((late + lax.dynamic_index_in_dim(tail, core, keepdims=False)).astype(BF)).astype(F32)
+    late = jnp.concatenate([jnp.where(core == c, late, 0.0) for c in range(2)], axis=0)
+    pieces = [
+        partial[j * ROWS : (j + 1) * ROWS] + jnp.where(member == j, late, 0.0) for j in range(MEM)
+    ]
+    other = swap(jnp.concatenate([pieces[1], pieces[3]], axis=0).astype(BF), 1).astype(F32)
+    far = (pieces[2] + other[ROWS:]).astype(BF)
+    return pieces[0] + other[:ROWS] + swap(far, 2).astype(F32)
 
 
 def join(member, pieces):
@@ -413,14 +446,14 @@
     return join(member, whole)
 
 
-def self_columns(query, key, value):
+def self_columns(query, key, value, gains):
     parts = []
     for m in range(MEM):
         a = 192 * m
         for matrix in (query, key, value):
             parts.append(matrix[:, a : a + 128])
         parts += [query[:, a + 128 : a + 192], key[:, a + 128 : a + 192], value[:, a + 128 : a + 192]]
-        parts.append(jnp.zeros((query.shape[0], 64), query.dtype))
+        parts += [gains, jnp.zeros((query.shape[0], 60), query.dtype)]
     return jnp.concatenate(parts, axis=1)
 
 
@@ -474,33 +507,89 @@
     return jnp.concatenate([matrix[256 * m : 256 * m + 192] for m in range(MEM)], axis=0)
 
 
-def up_columns(matrix, devices):
-    rows = matrix.shape[0]
-    part = D // devices
-    return matrix.reshape(rows, devices, 4, part).transpose(0, 2, 1, 3).reshape(rows, FF)
-
-
-def up_columns_back(matrix, devices):
-    rows = matrix.shape[0]
-    part = D // devices
-    return matrix.reshape(rows, 4, devices, part).transpose(0, 2, 1, 3).reshape(rows, FF)
-
-
-def down_columns(matrix):
-    part = matrix.shape[0] // 4
-    return jnp.concatenate([matrix[c * part : (c + 1) * part] for c in range(4)], axis=1)
-
-
-def down_columns_back(matrix):
-    return jnp.concatenate([matrix[:, c * D : (c + 1) * D] for c in range(4)], axis=0)
+def column_blocks(matrix):
+    return [matrix[:, c * D : (c + 1) * D] for c in range(FF // D)]
 
 
 def gather(matrix):
     return lax.all_gather(matrix, ALL, axis=0, tiled=True)
 
 
-def scatter(matrix):
-    return lax.psum_scatter(matrix, ALL, scatter_dimension=0, tiled=True).astype(F32)
+class Halving:
+    def __init__(self, matrix, turned, own=False):
+        self.devices = lax.axis_size("fsdp") * lax.axis_size("grp") * MEM
+        bits = self.devices.bit_length() - 1
+        outer = [bits - 1, bits - 2] if turned else [bits - 2, bits - 1]
+        self.order = ([] if own else [0]) + outer + list(range(2 if own else 1, bits - 2))
+        self.here = lax.axis_index(ALL)
+        self.left = list(range(bits - 1, -1, -1))
+        self.value = matrix.reshape([2] * bits + [matrix.shape[0] // self.devices, matrix.shape[1]])
+        self.own = own
+        self.split()
+
+    def split(self):
+        self.bit = self.order.pop(0)
+        axis = self.left.index(self.bit)
+        self.left.remove(self.bit)
+        mine = (self.here >> self.bit) & 1
+        self.away = lax.dynamic_index_in_dim(self.value, 1 - mine, axis, keepdims=False)
+        self.kept = lax.dynamic_index_in_dim(self.value, mine, axis, keepdims=False)
+
+    def send(self):
+        self.came = lax.ppermute(self.away, ALL, [(s, s ^ (1 << self.bit)) for s in range(self.devices)])
+
+    def add(self):
+        self.value = self.kept.astype(F32) + self.came.astype(F32)
+        if self.order or self.own:
+            self.value = self.value.astype(BF)
+        self.came = None
+        if self.order:
+            self.split()
+
+    def on(self):
+        if self.order:
+            self.add()
+            self.send()
+
+    def finish(self):
+        while self.order:
+            self.on()
+        self.add()
+        return self.value
+
+
+def tie(value, chains, name):
+    got = lax.optimization_barrier((value, [getattr(chain, name) for chain in chains]))
+    for chain, array in zip(chains, got[1]):
+        setattr(chain, name, array)
+    return got[0]
+
+
+def gather_own(member, shard, width):
+    devices = lax.axis_size("fsdp") * lax.axis_size("grp") * MEM
+    here = lax.axis_index(ALL)
+    pieces = spread(member, shard, width)
+    value = jnp.stack([lax.select_n(member, *[pieces[s ^ m] for m in range(MEM)]) for s in range(MEM)])
+    for bit in range(2, devices.bit_length() - 1):
+        mine = ((here >> bit) & 1) == 0
+        came = lax.ppermute(value, ALL, [(s, s ^ (1 << bit)) for s in range(devices)])
+        value = jnp.concatenate([jnp.where(mine, value, came), jnp.where(mine, came, value)])
+    return value.reshape(devices * shard.shape[0], width)
+
+
+def own_sets(member, value):
+    value = value.reshape(MEM, *value.shape[2:])
+    pieces = [
+        swap(lax.dynamic_index_in_dim(value, member ^ j, keepdims=False), j) for j in range(MEM)
+    ]
+    return [lax.select_n(member, *[pieces[s ^ m] for m in range(MEM)]).astype(F32) for s in range(MEM)]
+
+
+def moments(states):
+    center = states - jnp.mean(states, axis=-1, keepdims=True)
+    spread_ = jnp.mean(center * center, axis=-1, keepdims=True)
+    rate = lax.rsqrt(spread_ + 1e-05)
+    return (center * rate, rate)
 
 
 def shards(
@@ -523,37 +612,42 @@
         member, member,
     ]).astype(jnp.int32)
 
-    part = D // devices
     gains = jnp.stack([gain_self, gain_cross, gain_feed, gain_final], axis=1)
-    gains = jnp.pad(gains, ((0, 0), (0, 124)))
-    first = gather(jnp.concatenate([self_columns(self_query, self_key, self_value), gains], axis=1))
+    w_own = gather_own(member, self_columns(self_query, self_key, self_value, gains), 640)
+    two = swap(tokens, 2)
+    other = swap(jnp.concatenate([tokens, two], axis=0), 1)
+    near_tokens = [tokens, other[:ROWS], two, other[ROWS:]]
+    near_tokens = jnp.concatenate([*near_tokens, token_tail(member, near_tokens)], axis=0)
+    held_frames, two = lax.optimization_barrier((frames, two))
+    two = swap(held_frames, 2)
+    near_frames = [frames, swap(frames, 1), two, swap(two, 1)]
+    scal, near_frames = lax.optimization_barrier((scal, near_frames))
     second = gather(jnp.concatenate(
         [self_output, cross_output, query_columns(cross_query), frame_columns(cross_key, cross_value)], axis=1))
-    third = gather(jnp.concatenate([up_columns(feed_up, devices), down_columns(feed_down)], axis=1))
-
-    w_self = first[:, :2560]
-    gain_rows = first[:, 2560:].T.astype(F32)
+    third = gather(jnp.concatenate([*column_blocks(feed_up), feed_down], axis=0))
+    third = third.reshape(devices, 2 * FF // devices, D)
+    part = D // devices
+
+    gain_rows = w_own[:, 512:].T[64:68].astype(F32)
     w_so, w_co = (head_rows(second[:, :D]), head_rows(second[:, D : 2 * D]))
     w_cq, w_kv = (second[:, 1536:2560], second[:, 2560:])
-    w_up = third[:, :FF]
-    w_down = [third[:, FF + c * D : FF + (c + 1) * D] for c in range(4)]
+    w_up = jnp.concatenate([third[:, c * part : (c + 1) * part].reshape(D, D) for c in range(4)], axis=1)
+    w_down = third[:, 4 * part :].reshape(FF, D)
 
     states = tokens.astype(F32)
-    normed_self, back_self = jax.vjp(normalize, states, gain_rows[0])
-    normed_self = normed_self.astype(BF)
-    projected = product(normed_self, w_self).astype(BF)
-    self_pieces = with_tail(member, spread(member, projected, 640))
-    frame_rows = product(frames, w_kv).astype(BF)
-    frame_pieces = spread(member, frame_rows, 384)
-
-    mixed, self_kept = self_forward(scal, self_pieces)
+    unit, _ = moments(near_tokens.astype(F32))
+    normed_self = (unit * gain_rows[0]).astype(BF)
+    self_rows = product(normed_self, w_own).astype(BF)
+    mixed, self_kept = self_forward(scal, self_rows)
+    own_kv = lax.dynamic_slice_in_dim(w_kv, member * 384, 384, axis=1)
+    frame_rows = [product(piece, own_kv).astype(BF) for piece in near_frames]
     self_heads = collect(member, mixed)
     first_sum = states + product(self_heads, w_so)
     normed_cross, back_cross = jax.vjp(normalize, first_sum, gain_rows[1])
     normed_cross = normed_cross.astype(BF)
     cross_queries = product(normed_cross, w_cq).astype(BF)
     cross_pieces = with_tail(member, spread(member, cross_queries, 256))
-    mixed, cross_kept = cross_forward(scal, cross_pieces, frame_pieces)
+    mixed, cross_kept = cross_forward(scal, cross_pieces, frame_rows)
     cross_heads = collect(member, mixed)
     second_sum = first_sum + product(cross_heads, w_co)
     normed_feed, back_feed = jax.vjp(normalize, second_sum, gain_rows[2])
@@ -561,29 +655,37 @@
     inner_units = product(normed_feed, w_up)
     activated, back_gelu = jax.vjp(exact_gelu, inner_units)
     hidden = activated.astype(BF)
-    third_sum = second_sum
-    for c in range(4):
-        third_sum = third_sum + product(hidden[:, c * D : (c + 1) * D], w_down[c])
+    third_sum = second_sum + product(hidden, w_down)
     result, back_final = jax.vjp(normalize, third_sum, gain_rows[3])
 
     grad_third, grad_gain_final = back_final(cotangent.astype(F32))
     grad_feed_out = grad_third.astype(BF)
-    grad_inner = jnp.concatenate([product_right(grad_feed_out, w_down[c]) for c in range(4)], axis=1)
-    (grad_inner,) = back_gelu(grad_inner)
+    (grad_inner,) = back_gelu(product_right(grad_feed_out, w_down))
     grad_inner = grad_inner.astype(BF)
     grad_up = product_left(normed_feed, grad_inner).astype(BF)
-    grad_down = [product_left(hidden[:, c * D : (c + 1) * D], grad_feed_out).astype(BF) for c in range(4)]
-    sums_feed = scatter(jnp.concatenate([grad_up, *grad_down], axis=1))
+    grad_down = product_left(hidden, grad_feed_out).astype(BF)
+    feed = [Halving(grad_up, False), Halving(grad_down, True)]
+    for chain in feed:
+        chain.send()
     grad_second_part, grad_gain_feed = back_feed(product_right(grad_inner, w_up))
     grad_second = grad_third + grad_second_part
 
     grad_cross_out = grad_second.astype(BF)
     grad_cross_heads = product_right(grad_cross_out, w_co).astype(BF)
     grad_pieces = with_tail(member, spread(member, grad_cross_heads, 256))
-    grad_co = head_rows_back(product_left(cross_heads, grad_cross_out)).astype(BF)
-    query_pieces, frame_grads = cross_backward(scal, cross_pieces, frame_pieces, grad_pieces, cross_kept)
+    for chain in feed:
+        chain.add()
+    held = tie(scal, feed, "away")
+    for chain in feed:
+        chain.send()
+    query_pieces, frame_grads = cross_backward(held, cross_pieces, frame_rows, grad_pieces, cross_kept)
+    query_pieces = tie(query_pieces, feed, "came")
+    for chain in feed:
+        chain.on()
     grad_cross_queries = collect(member, query_pieces)
-    frame_grad = join(member, [swap(frame_grads[j], j) for j in range(MEM)])
+    grad_cross_queries = tie(grad_cross_queries, feed, "came")
+    for chain in feed:
+        chain.on()
     grad_cq = product_left(normed_cross, grad_cross_queries).astype(BF)
     grad_first_part, grad_gain_cross = back_cross(product_right(grad_cross_queries, w_cq))
     grad_first = grad_second + grad_first_part
@@ -591,21 +693,50 @@
     grad_self_out = grad_first.astype(BF)
     grad_self_heads = product_right(grad_self_out, w_so).astype(BF)
     grad_pieces = with_tail(member, spread(member, grad_self_heads, 256))
+    grad_co = head_rows_back(product_left(cross_heads, grad_cross_out)).astype(BF)
     grad_so = head_rows_back(product_left(self_heads, grad_self_out)).astype(BF)
-    grad_kv = product_left(frames, frame_grad).astype(BF)
+    grad_kv = sum(product_left(near_frames[j], frame_grads[j]) for j in range(MEM)).astype(BF)
+    rest = [
+        Halving(jnp.concatenate([grad_so, grad_cq[:, :512]], axis=1), False),
+        Halving(jnp.concatenate([grad_co, grad_cq[:, 512:]], axis=1), True),
+        Halving(grad_kv, True, True),
+    ]
+    held = tie(scal, rest, "away")
+    for chain in rest:
+        chain.send()
+    for chain in feed:
+        chain.add()
+    held = tie(held, feed, "away")
+    for chain in feed:
+        chain.send()
+    grad_rows = self_backward(held, self_rows, grad_pieces, self_kept)
+    grad_rows = tie(grad_rows, [*rest, *feed], "came")
+    for chain in rest:
+        chain.on()
+    grad_normed = product_right(grad_rows, w_own)
+    grad_gain_self = jnp.sum(grad_normed * unit, axis=0)
+    grad_gains = jnp.stack([grad_gain_self, grad_gain_cross, grad_gain_feed, grad_gain_final])
+    grad_gains = jnp.pad(grad_gains, ((64, 60), (0, 0))).T
+    grad_qkv = product_left(normed_self, grad_rows)
+    grad_qkv = jnp.concatenate([grad_qkv[:, :512], grad_qkv[:, 512:] + grad_gains], axis=1).astype(BF)
+    own = Halving(grad_qkv, False, True)
+    own.send()
+    total = total_rows(member, grad_normed)
+    _, back_self = jax.vjp(normalize, states, gain_rows[0])
+    tokens_gradient = grad_first + back_self(total)[0]
+    frame_grad = join(member, [swap(frame_grads[j], j) for j in range(MEM)])
     frames_gradient = product_right(frame_grad, w_kv)
-    sums_cross = scatter(jnp.concatenate([grad_so, grad_co, grad_cq, grad_kv], axis=1))
-    grad_projected = collect(member, self_backward(scal, self_pieces, grad_pieces, self_kept))
-    grad_qkv = product_left(normed_self, grad_projected).astype(BF)
-    grad_states_part, grad_gain_self = back_self(product_right(grad_projected, w_self))
-    tokens_gradient = grad_first + grad_states_part
-    grad_gains = jnp.stack([grad_gain_self, grad_gain_cross, grad_gain_feed, grad_gain_final])
-    grad_gains = jnp.pad(grad_gains, ((0, 124), (0, 0))).T.astype(BF)
-    sums_self = scatter(jnp.concatenate([grad_qkv, grad_gains], axis=1))
-
-    gains_out = sums_self[:, 2560:2564].T
-    query, key, value = self_columns_back(sums_self[:, :2560])
-    cross_k, cross_v = frame_columns_back(sums_cross[:, 2560:])
+
+    sums_up, sums_down = [chain.finish() for chain in feed]
+    for _ in range(8):
+        for chain in (*rest, own):
+            chain.on()
+    sums_out, sums_mix, kv = [chain.finish() for chain in rest]
+    sets = own_sets(member, jnp.concatenate([own.finish(), kv], axis=-1))
+    gains_out = sum(part[:, 576:580] for part in sets).T
+    query, key, value = self_columns_back(jnp.concatenate([part[:, :640] for part in sets], axis=1))
+    cross_k, cross_v = frame_columns_back(jnp.concatenate([part[:, 640:] for part in sets], axis=1))
+    grad_cq = jnp.concatenate([sums_out[:, D:], sums_mix[:, D:]], axis=1)
     return (
         result.astype(BF),
         tokens_gradient,
@@ -617,13 +748,13 @@
         query,
         key,
         value,
-        sums_cross[:, :D],
-        query_columns_back(sums_cross[:, 1536:2560]),
+        sums_out[:, :D],
+        query_columns_back(grad_cq),
         cross_k,
         cross_v,
-        sums_cross[:, D : 2 * D],
-        up_columns_back(sums_feed[:, :FF], devices),
-        down_columns_back(sums_feed[:, FF:]),
+        sums_mix[:, :D],
+        sums_up,
+        sums_down,
     )
 
 

time: 806 us -> 518 us (0.64)
  waiting for transfers between devices: 504 us -> 170 us
  starting transfers between devices: 47.3 us -> 92.7 us
  other arithmetic: 36.1 us -> 45.2 us
    unnamed x8 -> x2, waiting for transfers between devices: 158 us -> 0.03 us
    reduce_scatter x1 -> x0, waiting for transfers between devices: 134 us -> none  [scatter(): lax.psum_scatter(matrix, ALL, scatter_dimension=0, tiled=True).astype(F32)]
    ppermute x0 -> x31, waiting for transfers between devices: none -> 78.7 us  [the longest x26 47.5 us: send(): lax.ppermute(self.away, ALL, [(s, s ^ 1 << self.bit) for s in range(self....]
    all_gather x3 -> x2, waiting for transfers between devices: 55.1 us -> 0.02 us  [gather(): return lax.all_gather(matrix, ALL, axis=0, tiled=True)]
    ppermute x0 -> x31, starting transfers between devices: none -> 49.3 us  [the longest x26 40 us: send(): lax.ppermute(self.away, ALL, [(s, s ^ 1 << self.bit) for s in range(self....]
    ppermute x30 -> x35, waiting for transfers between devices: 81.8 us -> 43.6 us  [swap(): return lax.ppermute(value, LINE, [(s, s ^ mask) for s in range(count)])]
    ppermute x4 -> x3, waiting for transfers between devices: 51.8 us -> 33.7 us  [to_previous(): return lax.ppermute(value, LINE, [(s, s - MEM) for s in range(MEM, count)])]
    convert_element_type x4 -> x27, other arithmetic: 3.36 us -> 12.9 us  [the longest x22 9.53 us: add(): self.value = self.value.astype(BF)]
  transfers between devices with their start and end apart: 44 -> 75, of which waited for: 30 -> 37; matrix products, arithmetic and copies ran while one was open for 12% -> 20% of each run, Pallas kernels for 4% -> 9%
where the time goes in v3:
time: 518 us; the launch traced here: 510 us
  waiting for transfers between devices  170 us (33%)
  starting transfers between devices  92.7 us (18%)
  Pallas kernels  68.4 us (13%)
  local copies, waits for them, and re-layouts  63.9 us (12%)
  matrix products  52.7 us (10%)
  other arithmetic  45.2 us (9%)
  between operations  16.6 us (3%)
    pallas_call x4, Pallas kernels, call(): pl.pallas_call(kernel, out_shape=outs, in_specs=[pl.BlockSpec(memory_spac...  68.4 us
    ppermute x26, waiting for transfers between devices, send(): lax.ppermute(self.away, ALL, [(s, s ^ 1 << self.bit) for s in range(self....  47.5 us
    ppermute x35, waiting for transfers between devices, swap(): return lax.ppermute(value, LINE, [(s, s ^ mask) for s in range(count)])  43.6 us
    ppermute x26, starting transfers between devices, send(): lax.ppermute(self.away, ALL, [(s, s ^ 1 << self.bit) for s in range(self....  40 us
    ppermute x3, waiting for transfers between devices, to_previous(): return lax.ppermute(value, LINE, [(s, s - MEM) for s in range(MEM, count)])  33.7 us
    ppermute x35, starting transfers between devices, swap(): return lax.ppermute(value, LINE, [(s, s ^ mask) for s in range(count)])  31.3 us
    dot_general x10, matrix products, product(): return jnp.dot(left, right, preferred_element_type=F32)  23.9 us
    unnamed x200, local copies, waits for them, and re-layouts  23.5 us
  transfers between devices with their start and end apart: 75, of which 37 were waited for; matrix products, arithmetic and copies ran while one was open for 20% of the time, Pallas kernels for 9%

profile of v3, /device:TPU:0, one launch (start us, length us, event | category | flops | bytes accessed | tf_op | source)
XLA Modules:
  0.0 509.5 jit_solution(4259255258106144051)
XLA Ops:
  23.0 3.1 collective-permute-start.8
  32.8 9.5 %collective-permute-done.10 = bf16[4,24,640]{2,1,0:T(8,128)(2,1)S(1)} collective-permute-done((bf16[4,24,640]{2,1,0:T(8,128)(2,1)S(1)}, bf16[4,24,640]{2,1,0:T(8,128)(2,1)S(1)}, u32[]{:S(2)}, u32[]{:S(2)}) %collective-permute-start.10) | collective-permute-done | bytes 122912 | tf_op jit(solution)/shard_map/ppermute | solution.py:575
  49.2 5.3 %collective-permute-done.11 = bf16[8,24,640]{2,1,0:T(8,128)(2,1)} collective-permute-done((bf16[8,24,640]{2,1,0:T(8,128)(2,1)}, bf16[8,24,640]{2,1,0:T(8,128)(2,1)}, u32[]{:S(2)}, u32[]{:S(2)}) %collective-permute-start.11) | collective-permute-done | bytes 245792 | tf_op jit(solution)/shard_map/ppermute | solution.py:575
  66.2 5.2 %collective-permute-done.2 = bf16[375,768]{1,0:T(8,128)(2,1)} collective-permute-done((bf16[375,768]{1,0:T(8,128)(2,1)}, bf16[375,768]{1,0:T(8,128)(2,1)}, u32[]{:S(2)}, u32[]{:S(2)}) %collective-permute-start.2) | collective-permute-done | bytes 576032 | tf_op jit(solution)/shard_map/ppermute | solution.py:386
  71.4 4.3 collective-permute-done.12
  77.1 12.1 %collective-permute-done.5 = bf16[256,768]{1,0:T(8,128)(2,1)S(1)} collective-permute-done((bf16[256,768]{1,0:T(8,128)(2,1)}, bf16[256,768]{1,0:T(8,128)(2,1)S(1)}, u32[]{:S(2)}, u32[]{:S(2)}) %collective-permute-start.5) | collective-permute-done | bytes 393248 | tf_op jit(solution)/shard_map/ppermute | solution.py:412
  98.5 11.2 %shard_map.305 = (bf16[256,256]{1,0:T(8,128)(2,1)}, bf16[256,256]{1,0:T(8,128)(2,1)}, bf16[256,256]{1,0:T(8,128)(2,1)}, bf16[256,256]{1,0:T(8,128)(2,1)}, bf16[2...) custom-call(s32[8]{0:T(128)} %stack.60.scal, bf16[1280,640]{1,0:T(8,128)(2,1)} %convolution_convert_fusion.2.rows), custom_call_target="tpu_custom_call" | custom-call | flops 3221225472 | bytes 4194304 | tf_op jit(solution)/shard_map/pallas_call | solution.py:331
  111.2 4.6 collective-permute-done.13
  119.8 3.8 collective-permute-done.16
  135.3 4.5 collective-permute-start.17
  152.7 17.6 %collective-permute-done.20.qtail = bf16[256,256]{1,0:T(8,128)(2,1)S(1)} collective-permute-done((bf16[256,256]{1,0:T(8,128)(2,1)S(1)}, bf16[256,256]{1,0:T(8,128)(2,1)S(1)}, u32[]{:S(2)}, u32[]{:S(2)}) %collective-permute-start.20) | collective-permute-done | bytes 131104 | tf_op jit(solution)/shard_map/ppermute | solution.py:391
  171.0 21.0 %shard_map.306 = (bf16[256,256]{1,0:T(8,128)(2,1)}, bf16[256,256]{1,0:T(8,128)(2,1)}, bf16[256,256]{1,0:T(8,128)(2,1)}, bf16[256,256]{1,0:T(8,128)(2,1)}, bf16[2...) custom-call(s32[8]{0:T(128)} %stack.60.scal, bf16[256,256]{1,0:T(8,128)(2,1)} %get-tuple-element.161.q0, ...), custom_call_target="tpu_custom_call" | custom-call | flops 6442450944 | bytes 4194304 | tf_op jit(solution)/shard_map/pallas_call | solution.py:331
  193.6 3.7 collective-permute-done.21
  214.2 7.7 %multiply_convert_fusion = (bf16[256,3072]{1,0:T(8,128)(2,1)S(1)}, f32[256,3072]{1,0:T(8,128)S(1)}, f32[256,3072]{1,0:T(8,128)S(1)}) fusion(bf16[768,768]{1,0:T(8,128)(2,1)S(1)} %bitcast.269, bf16[768,768]{1,0:T(8,128)(2,1)S(1)} %bitcast.271, bf16[768,768]{1,0:T(8,128)(2,1)S(1)} %bitcast.273, bf16[768,768]{1,0:T(8,128)(2,1)S(1)} %bitcast.267, ...), kind=kOutput, calls=%fused_computation.20 | convolution fusion | flops 1278738432 | bytes 13374464 | tf_op jit(solution)/shard_map/dot_general | solution.py:39
  243.6 3.1 collective-permute-done.28.g2
  253.7 4.4 collective-permute-done.30.gtail
  258.8 21.3 %shard_map.307 = (bf16[256,256]{1,0:T(8,128)(2,1)}, bf16[256,256]{1,0:T(8,128)(2,1)}, bf16[256,256]{1,0:T(8,128)(2,1)}, bf16[256,256]{1,0:T(8,128)(2,1)}, bf16[2...) custom-call(s32[8]{0:T(128)} %stack.60.scal, ...), custom_call_target="tpu_custom_call" | custom-call | flops 17179869184 | bytes 4194304 | tf_op jit(solution)/shard_map/pallas_call | solution.py:331
  285.7 12.7 %collective-permute-start.31 = (bf16[2,2,2,24,3072]{4,3,1,2,0:T(8,128)(2,1)S(1)}, bf16[2,2,2,24,3072]{4,3,1,2,0:T(8,128)(2,1)S(1)}, u32[]{:S(2)}, u32[]{:S(2)}) collective-permute-start(bf16[2,2,2,24,3072]{4,3,1,2,0:T(8,128)(2,1)S(1)} %dynamic-slice_bitcast_fusion.1), channel_id=1, source_target_pairs={{0,8},{1,9},{2,10},{3,11},{4,12},{5,13},{6,14},{7,15},{8,0},{9,1},... | collective-permute-start | bytes 3538952 | tf_op jit(solution)/shard_map/ppermute | solution.py:539
  306.9 18.0 %collective-permute-done.31 = bf16[2,2,2,24,3072]{4,3,1,2,0:T(8,128)(2,1)S(1)} collective-permute-done((bf16[2,2,2,24,3072]{4,3,1,2,0:T(8,128)(2,1)S(1)}, bf16[2,2,2,24,3072]{4,3,1,2,0:T(8,128)(2,1)S(1)}, u32[]{:S(2)}, u32[]{:S(2)}) %collective-permute-start.31) | collective-permute-done | bytes 1179680 | tf_op jit(solution)/shard_map/ppermute | solution.py:539
  339.7 10.0 %collective-permute-done.38 = bf16[2,2,96,768]{3,2,0,1:T(8,128)(2,1)S(1)} collective-permute-done((bf16[2,2,96,768]{3,2,0,1:T(8,128)(2,1)S(1)}, bf16[2,2,96,768]{3,2,0,1:T(8,128)(2,1)S(1)}, u32[]{:S(2)}, u32[]{:S(2)}) %collective-permute-start.38) | collective-permute-done | bytes 589856 | tf_op jit(solution)/shard_map/ppermute | solution.py:539
  366.6 7.7 %collective-permute-done.43.g3 = bf16[256,256]{1,0:T(8,128)(2,1)S(1)} collective-permute-done((bf16[256,256]{1,0:T(8,128)(2,1)S(1)}, bf16[256,256]{1,0:T(8,128)(2,1)S(1)}, u32[]{:S(2)}, u32[]{:S(2)}) %collective-permute-start.43) | collective-permute-done | bytes 131104 | tf_op jit(solution)/shard_map/ppermute | solution.py:386
  381.0 3.5 collective-permute-start.48
  384.5 11.6 %collective-permute-done.44.gtail = bf16[256,256]{1,0:T(8,128)(2,1)S(1)} collective-permute-done((bf16[256,256]{1,0:T(8,128)(2,1)S(1)}, bf16[256,256]{1,0:T(8,128)(2,1)S(1)}, u32[]{:S(2)}, u32[]{:S(2)}) %collective-permute-start.44) | collective-permute-done | bytes 131104 | tf_op jit(solution)/shard_map/ppermute | solution.py:391
  396.8 14.9 %shard_map.308 = bf16[1280,640]{1,0:T(8,128)(2,1)} custom-call(s32[8]{0:T(128)} %stack.60.scal, bf16[1280,640]{1,0:T(8,128)(2,1)} %convolution_convert_fusion.2.rows, bf16[256,256]{1,0:T(8,128)(2,1)} %get-tuple-element.145.g0, bf16[256,256]{1,0:T(8,128)(2,1)} %copy-done.64, bf16[256,256]{1,0:T(8,128)(2,1)} %copy-done.66, bf16[256,256]{1,0:T(8,128)(2,1)} %copy-done.65, ...), custom_call_target="tpu_custom_call" | custom-call | flops 8589934592 | bytes 4194304 | tf_op jit(solution)/shard_map/pallas_call | solution.py:331
  411.7 4.8 fusion.135
  416.6 3.8 fusion.7
  444.5 3.8 collective-permute-done.51
  455.0 4.1 collective-permute-done.70
  461.7 4.2 collective-permute-done.58
  466.0 3.4 collective-permute-start.59
  469.6 6.3 %collective-permute-done.59 = bf16[2,2,24,640]{3,2,1,0:T(8,128)(2,1)S(1)} collective-permute-done((bf16[2,2,24,640]{3,2,1,0:T(8,128)(2,1)S(1)}, bf16[2,2,24,640]{3,2,1,0:T(8,128)(2,1)S(1)}, u32[]{:S(2)}, u32[]{:S(2)}) %collective-permute-start.59) | collective-permute-done | bytes 122912 | tf_op jit(solution)/shard_map/ppermute | solution.py:539
  491.1 7.9 %collective-permute-done.53 = bf16[256,768]{1,0:T(8,128)(2,1)S(1)} collective-permute-done((bf16[256,768]{1,0:T(8,128)(2,1)S(1)}, bf16[256,768]{1,0:T(8,128)(2,1)S(1)}, u32[]{:S(2)}, u32[]{:S(2)}) %collective-permute-start.53) | collective-permute-done | bytes 393248 | tf_op jit(solution)/shard_map/ppermute | solution.py:386
  (542 shorter events, 233.5 us)
Async XLA Ops:
  7.2 119.6 %all-gather.3.cloned.1.call-start = ((), (), s32[]{:S(2)}) async-start(), calls=%async_computation | async-start | bytes 6488064 | tf_op jit(solution)/shard_map/all_gather | solution.py:515
  11.5 197.3 %all-gather.5.cloned.1.call-start = ((), (), s32[]{:S(2)}) async-start(), calls=%async_computation.1 | async-start | bytes 9732096 | tf_op jit(solution)/shard_map/all_gather | solution.py:515
  26.4 17.0 %collective-permute-start.1 = (bf16[256,768]{1,0:T(8,128)(2,1)S(1)}, bf16[256,768]{1,0:T(8,128)(2,1)S(1)}, u32[]{:S(2)}, u32[]{:S(2)}) collective-permute-start(bf16[256,768]{1,0:T(8,128)(2,1)S(1)} %copy-done), channel_id=1, source_target_pairs={{0,2},{1,3},{2,0},{3,1},{4,6},{5,7},{6,4},{7,5},{8,10},{9,11},{10,... | collective-permute-start | bytes 1179656 | tf_op jit(solution)/shard_map/ppermute | solution.py:386
  32.8 61.1 %collective-permute-start = (bf16[375,768]{1,0:T(8,128)(2,1)}, bf16[375,768]{1,0:T(8,128)(2,1)S(1)}, u32[]{:S(2)}, u32[]{:S(2)}) collective-permute-start(bf16[375,768]{1,0:T(8,128)(2,1)} %param.19), channel_id=1, source_target_pairs={{0,1},{1,0},{2,3},{3,2},{4,5},{5,4},{6,7},{7,6},{8,9},{9,8},{10,11... | collective-permute-start | bytes 1728008 | tf_op jit(solution)/shard_map/ppermute | solution.py:386
  46.6 24.8 %collective-permute-start.2 = (bf16[375,768]{1,0:T(8,128)(2,1)}, bf16[375,768]{1,0:T(8,128)(2,1)}, u32[]{:S(2)}, u32[]{:S(2)}) collective-permute-start(bf16[375,768]{1,0:T(8,128)(2,1)} %param.19), channel_id=1, source_target_pairs={{0,2},{1,3},{2,0},{3,1},{4,6},{5,7},{6,4},{7,5},{8,10},{9,11},{10,... | collective-permute-start | bytes 1728008 | tf_op jit(solution)/shard_map/ppermute | solution.py:386
  56.5 19.2 %collective-permute-start.12 = (bf16[16,24,640]{2,1,0:T(8,128)(2,1)}, bf16[16,24,640]{2,1,0:T(8,128)(2,1)}, u32[]{:S(2)}, u32[]{:S(2)}) collective-permute-start(bf16[16,24,640]{2,1,0:T(8,128)(2,1)} %pad_maximum_fusion.12), channel_id=1, source_target_pairs={{0,16},{1,17},{2,18},{3,19},{4,20},{5,21},{6,22},{7,23},{8,24},{9,... | collective-permute-start | bytes 1474568 | tf_op jit(solution)/shard_map/ppermute | solution.py:575
  61.1 28.0 %collective-permute-start.5 = (bf16[256,768]{1,0:T(8,128)(2,1)}, bf16[256,768]{1,0:T(8,128)(2,1)S(1)}, u32[]{:S(2)}, u32[]{:S(2)}) collective-permute-start(bf16[256,768]{1,0:T(8,128)(2,1)} %get-tuple-element.203), channel_id=1, source_target_pairs={{4,0},{6,2},{12,8},{14,10},{20,16},{22,18},{28,24},{30,26}} | collective-permute-start | bytes 1179656 | tf_op jit(solution)/shard_map/ppermute | solution.py:412
  71.4 22.6 %collective-permute-start.3 = (bf16[375,768]{1,0:T(8,128)(2,1)}, bf16[375,768]{1,0:T(8,128)(2,1)}, u32[]{:S(2)}, u32[]{:S(2)}) collective-permute-start(bf16[375,768]{1,0:T(8,128)(2,1)} %collective-permute-done.2), channel_id=1, source_target_pairs={{0,1},{1,0},{2,3},{3,2},{4,5},{5,4},{6,7},{7,6},{8,9},{9,8},{10,11... | collective-permute-start | bytes 1728008 | tf_op jit(solution)/shard_map/ppermute | solution.py:386
  149.1 21.2 %collective-permute-start.20 = (bf16[256,256]{1,0:T(8,128)(2,1)S(1)}, bf16[256,256]{1,0:T(8,128)(2,1)S(1)}, u32[]{:S(2)}, u32[]{:S(2)}) collective-permute-start(bf16[256,256]{1,0:T(8,128)(2,1)S(1)} %get-tuple-element.160), channel_id=1, source_target_pairs={{4,0},{5,1},{6,2},{7,3},{12,8},{13,9},{14,10},{15,11},{20,16},{21,... | collective-permute-start | bytes 393224 | tf_op jit(solution)/shard_map/ppermute | solution.py:391
  280.2 24.3 %collective-permute-start.54 = (bf16[375,384]{1,0:T(8,128)(2,1)}, bf16[375,384]{1,0:T(8,128)(2,1)S(1)}, u32[]{:S(2)}, u32[]{:S(2)}) collective-permute-start(bf16[375,384]{1,0:T(8,128)(2,1)} %get-tuple-element.107), channel_id=1, source_target_pairs={{0,1},{1,0},{2,3},{3,2},{4,5},{5,4},{6,7},{7,6},{8,9},{9,8},{10,11... | collective-permute-start | bytes 864008 | tf_op jit(solution)/shard_map/ppermute | solution.py:386
  281.9 22.6 %collective-permute-start.55 = (bf16[375,384]{1,0:T(8,128)(2,1)}, bf16[375,384]{1,0:T(8,128)(2,1)S(1)}, u32[]{:S(2)}, u32[]{:S(2)}) collective-permute-start(bf16[375,384]{1,0:T(8,128)(2,1)} %get-tuple-element.108), channel_id=1, source_target_pairs={{0,2},{1,3},{2,0},{3,1},{4,6},{5,7},{6,4},{7,5},{8,10},{9,11},{10,... | collective-permute-start | bytes 864008 | tf_op jit(solution)/shard_map/ppermute | solution.py:386
  283.9 20.6 %collective-permute-start.56 = (bf16[375,384]{1,0:T(8,128)(2,1)S(1)}, bf16[375,384]{1,0:T(8,128)(2,1)S(1)}, u32[]{:S(2)}, u32[]{:S(2)}) collective-permute-start(bf16[375,384]{1,0:T(8,128)(2,1)S(1)} %copy-done.44), channel_id=1, source_target_pairs={{0,3},{1,2},{2,1},{3,0},{4,7},{5,6},{6,5},{7,4},{8,11},{9,10},{10,... | collective-permute-start | bytes 864008 | tf_op jit(solution)/shard_map/ppermute | solution.py:386
  285.7 39.3 %collective-permute-start.31 = (bf16[2,2,2,24,3072]{4,3,1,2,0:T(8,128)(2,1)S(1)}, bf16[2,2,2,24,3072]{4,3,1,2,0:T(8,128)(2,1)S(1)}, u32[]{:S(2)}, u32[]{:S(2)}) collective-permute-start(bf16[2,2,2,24,3072]{4,3,1,2,0:T(8,128)(2,1)S(1)} %dynamic-slice_bitcast_fusion.1), channel_id=1, source_target_pairs={{0,8},{1,9},{2,10},{3,11},{4,12},{5,13},{6,14},{7,15},{8,0},{9,1},... | collective-permute-start | bytes 3538952 | tf_op jit(solution)/shard_map/ppermute | solution.py:539
  298.4 28.0 %collective-permute-start.32 = (bf16[2,2,2,96,768]{4,3,1,2,0:T(8,128)(2,1)S(1)}, bf16[2,2,2,96,768]{4,3,1,2,0:T(8,128)(2,1)S(1)}, u32[]{:S(2)}, u32[]{:S(2)}) collective-permute-start(bf16[2,2,2,96,768]{4,3,1,2,0:T(8,128)(2,1)S(1)} %copy-done.32), channel_id=1, source_target_pairs={{0,16},{1,17},{2,18},{3,19},{4,20},{5,21},{6,22},{7,23},{8,24},{9,... | collective-permute-start | bytes 3538952 | tf_op jit(solution)/shard_map/ppermute | solution.py:539
  334.3 15.4 %collective-permute-start.38 = (bf16[2,2,96,768]{3,2,0,1:T(8,128)(2,1)S(1)}, bf16[2,2,96,768]{3,2,0,1:T(8,128)(2,1)S(1)}, u32[]{:S(2)}, u32[]{:S(2)}) collective-permute-start(bf16[2,2,96,768]{3,2,0,1:T(8,128)(2,1)S(1)} %dynamic-slice_bitcast_fusion.2), channel_id=1, source_target_pairs={{0,8},{1,9},{2,10},{3,11},{4,12},{5,13},{6,14},{7,15},{8,0},{9,1},... | collective-permute-start | bytes 1769480 | tf_op jit(solution)/shard_map/ppermute | solution.py:539
  335.0 15.1 %collective-permute-start.37 = (bf16[2,2,24,3072]{3,2,0,1:T(8,128)(2,1)S(1)}, bf16[2,2,24,3072]{3,2,0,1:T(8,128)(2,1)S(1)}, u32[]{:S(2)}, u32[]{:S(2)}) collective-permute-start(bf16[2,2,24,3072]{3,2,0,1:T(8,128)(2,1)S(1)} %dynamic-slice_bitcast_fusion.3), channel_id=1, source_target_pairs={{0,16},{1,17},{2,18},{3,19},{4,20},{5,21},{6,22},{7,23},{8,24},{9,... | collective-permute-start | bytes 1769480 | tf_op jit(solution)/shard_map/ppermute | solution.py:539
  357.2 22.3 %collective-permute-start.40 = (bf16[2,96,768]{2,1,0:T(8,128)(2,1)S(1)}, bf16[2,96,768]{2,1,0:T(8,128)(2,1)S(1)}, u32[]{:S(2)}, u32[]{:S(2)}) collective-permute-start(bf16[2,96,768]{2,1,0:T(8,128)(2,1)S(1)} %dynamic-slice_bitcast_fusion.6), channel_id=1, source_target_pairs={{0,2},{1,3},{2,0},{3,1},{4,6},{5,7},{6,4},{7,5},{8,10},{9,11},{10,... | collective-permute-start | bytes 884744 | tf_op jit(solution)/shard_map/ppermute | solution.py:539
  358.8 19.0 %collective-permute-start.39 = (bf16[2,24,3072]{2,1,0:T(8,128)(2,1)S(1)}, bf16[2,24,3072]{2,1,0:T(8,128)(2,1)S(1)}, u32[]{:S(2)}, u32[]{:S(2)}) collective-permute-start(bf16[2,24,3072]{2,1,0:T(8,128)(2,1)S(1)} %dynamic-slice_bitcast_fusion.7), channel_id=1, source_target_pairs={{0,2},{1,3},{2,0},{3,1},{4,6},{5,7},{6,4},{7,5},{8,10},{9,11},{10,... | collective-permute-start | bytes 884744 | tf_op jit(solution)/shard_map/ppermute | solution.py:539
  359.4 14.9 %collective-permute-start.43 = (bf16[256,256]{1,0:T(8,128)(2,1)S(1)}, bf16[256,256]{1,0:T(8,128)(2,1)S(1)}, u32[]{:S(2)}, u32[]{:S(2)}) collective-permute-start(bf16[256,256]{1,0:T(8,128)(2,1)S(1)} %get-tuple-element.206), channel_id=1, source_target_pairs={{0,3},{1,2},{2,1},{3,0},{4,7},{5,6},{6,5},{7,4},{8,11},{9,10},{10,... | collective-permute-start | bytes 393224 | tf_op jit(solution)/shard_map/ppermute | solution.py:386
  361.1 16.0 %collective-permute-start.42 = (bf16[256,256]{1,0:T(8,128)(2,1)S(1)}, bf16[256,256]{1,0:T(8,128)(2,1)S(1)}, u32[]{:S(2)}, u32[]{:S(2)}) collective-permute-start(bf16[256,256]{1,0:T(8,128)(2,1)S(1)} %get-tuple-element.207), channel_id=1, source_target_pairs={{0,2},{1,3},{2,0},{3,1},{4,6},{5,7},{6,4},{7,5},{8,10},{9,11},{10,... | collective-permute-start | bytes 393224 | tf_op jit(solution)/shard_map/ppermute | solution.py:386
  364.9 46.7 %collective-permute-start.47 = (bf16[2,2,2,2,24,384]{5,4,3,2,1,0:T(8,128)(2,1)}, bf16[2,2,2,2,24,384]{5,4,3,2,1,0:T(8,128)(2,1)S(1)}, u32[]{:S(2)}, u32[]{:S(2)}) collective-permute-start(bf16[2,2,2,2,24,384]{5,4,3,2,1,0:T(8,128)(2,1)} %dynamic-slice_bitcast_fusion.8), channel_id=1, source_target_pairs={{0,16},{1,17},{2,18},{3,19},{4,20},{5,21},{6,22},{7,23},{8,24},{9,... | collective-permute-start | bytes 884744 | tf_op jit(solution)/shard_map/ppermute | solution.py:539
  374.3 37.3 %collective-permute-start.45 = (bf16[2,2,2,2,24,1280]{5,4,2,3,0,1:T(8,128)(2,1)}, bf16[2,2,2,2,24,1280]{5,4,2,3,0,1:T(8,128)(2,1)}, u32[]{:S(2)}, u32[]{:S(2)}) collective-permute-start(bf16[2,2,2,2,24,1280]{5,4,2,3,0,1:T(8,128)(2,1)} %bitcast.243), channel_id=1, source_target_pairs={{0,1},{1,0},{2,3},{3,2},{4,5},{5,4},{6,7},{7,6},{8,9},{9,8},{10,11... | collective-permute-start | bytes 2949128 | tf_op jit(solution)/shard_map/ppermute | solution.py:539
  377.1 34.6 %collective-permute-start.46 = (bf16[2,2,2,2,24,1280]{5,4,2,3,1,0:T(8,128)(2,1)}, bf16[2,2,2,2,24,1280]{5,4,2,3,1,0:T(8,128)(2,1)}, u32[]{:S(2)}, u32[]{:S(2)}) collective-permute-start(bf16[2,2,2,2,24,1280]{5,4,2,3,1,0:T(8,128)(2,1)} %bitcast.242), channel_id=1, source_target_pairs={{0,1},{1,0},{2,3},{3,2},{4,5},{5,4},{6,7},{7,6},{8,9},{9,8},{10,11... | collective-permute-start | bytes 2949128 | tf_op jit(solution)/shard_map/ppermute | solution.py:539
  377.8 18.3 %collective-permute-start.44 = (bf16[256,256]{1,0:T(8,128)(2,1)S(1)}, bf16[256,256]{1,0:T(8,128)(2,1)S(1)}, u32[]{:S(2)}, u32[]{:S(2)}) collective-permute-start(bf16[256,256]{1,0:T(8,128)(2,1)S(1)} %get-tuple-element.144), channel_id=1, source_target_pairs={{4,0},{5,1},{6,2},{7,3},{12,8},{13,9},{14,10},{15,11},{20,16},{21,... | collective-permute-start | bytes 393224 | tf_op jit(solution)/shard_map/ppermute | solution.py:391
  381.0 30.7 %collective-permute-start.48 = (bf16[24,3072]{1,0:T(8,128)(2,1)S(1)}, bf16[24,3072]{1,0:T(8,128)(2,1)}, u32[]{:S(2)}, u32[]{:S(2)}) collective-permute-start(bf16[24,3072]{1,0:T(8,128)(2,1)S(1)} %dynamic-slice_bitcast_fusion.14), channel_id=1, source_target_pairs={{0,4},{1,5},{2,6},{3,7},{4,0},{5,1},{6,2},{7,3},{8,12},{9,13},{10,... | collective-permute-start | bytes 442376 | tf_op jit(solution)/shard_map/ppermute | solution.py:539
  396.1 15.6 %collective-permute-start.49 = (bf16[96,768]{1,0:T(8,128)(2,1)}, bf16[96,768]{1,0:T(8,128)(2,1)}, u32[]{:S(2)}, u32[]{:S(2)}) collective-permute-start(bf16[96,768]{1,0:T(8,128)(2,1)} %dynamic-slice_bitcast_fusion.13), channel_id=1, source_target_pairs={{0,4},{1,5},{2,6},{3,7},{4,0},{5,1},{6,2},{7,3},{8,12},{9,13},{10,... | collective-permute-start | bytes 442376 | tf_op jit(solution)/shard_map/ppermute | solution.py:539
  421.1 16.7 %collective-permute-start.60 = (bf16[2,2,2,24,384]{4,3,2,1,0:T(8,128)(2,1)}, bf16[2,2,2,24,384]{4,3,2,1,0:T(8,128)(2,1)}, u32[]{:S(2)}, u32[]{:S(2)}) collective-permute-start(bf16[2,2,2,24,384]{4,3,2,1,0:T(8,128)(2,1)} %dynamic-slice_bitcast_fusion.12), channel_id=1, source_target_pairs={{0,8},{1,9},{2,10},{3,11},{4,12},{5,13},{6,14},{7,15},{8,0},{9,1},... | collective-permute-start | bytes 442376 | tf_op jit(solution)/shard_map/ppermute | solution.py:539
  427.3 22.1 %collective-permute-start.69 = (bf16[2,2,2,24,1280]{4,3,1,2,0:T(8,128)(2,1)}, bf16[2,2,2,24,1280]{4,3,1,2,0:T(8,128)(2,1)}, u32[]{:S(2)}, u32[]{:S(2)}) collective-permute-start(bf16[2,2,2,24,1280]{4,3,1,2,0:T(8,128)(2,1)} %dynamic-slice_bitcast_fusion.4), channel_id=1, source_target_pairs={{0,16},{1,17},{2,18},{3,19},{4,20},{5,21},{6,22},{7,23},{8,24},{9,... | collective-permute-start | bytes 1474568 | tf_op jit(solution)/shard_map/ppermute | solution.py:539
  429.0 22.4 %collective-permute-start.65 = (bf16[2,2,2,24,1280]{4,3,1,2,0:T(8,128)(2,1)}, bf16[2,2,2,24,1280]{4,3,1,2,0:T(8,128)(2,1)}, u32[]{:S(2)}, u32[]{:S(2)}) collective-permute-start(bf16[2,2,2,24,1280]{4,3,1,2,0:T(8,128)(2,1)} %dynamic-slice_bitcast_fusion.5), channel_id=1, source_target_pairs={{0,8},{1,9},{2,10},{3,11},{4,12},{5,13},{6,14},{7,15},{8,0},{9,1},... | collective-permute-start | bytes 1474568 | tf_op jit(solution)/shard_map/ppermute | solution.py:539
  432.8 20.2 %collective-permute-start.57 = (bf16[2,2,2,2,24,640]{5,4,3,2,1,0:T(8,128)(2,1)S(1)}, bf16[2,2,2,2,24,640]{5,4,3,2,1,0:T(8,128)(2,1)S(1)}, u32[]{:S(2)}, u32[]{:S(2)}) collective-permute-start(bf16[2,2,2,2,24,640]{5,4,3,2,1,0:T(8,128)(2,1)S(1)} %fusion.62), channel_id=1, source_target_pairs={{0,8},{1,9},{2,10},{3,11},{4,12},{5,13},{6,14},{7,15},{8,0},{9,1},... | collective-permute-start | bytes 1474568 | tf_op jit(solution)/shard_map/ppermute | solution.py:539
  449.4 36.0 %collective-permute-start.52 = (bf16[512,768]{1,0:T(8,128)(2,1)}, bf16[512,768]{1,0:T(8,128)(2,1)}, u32[]{:S(2)}, u32[]{:S(2)}) collective-permute-start(bf16[512,768]{1,0:T(8,128)(2,1)} %pad_maximum_fusion.8), channel_id=1, source_target_pairs={{0,1},{1,0},{2,3},{3,2},{4,5},{5,4},{6,7},{7,6},{8,9},{9,8},{10,11... | collective-permute-start | bytes 2359304 | tf_op jit(solution)/shard_map/ppermute | solution.py:386
  469.5 15.5 %collective-permute-start.72 = (bf16[24,1280]{1,0:T(8,128)(2,1)S(1)}, bf16[24,1280]{1,0:T(8,128)(2,1)S(1)}, u32[]{:S(2)}, u32[]{:S(2)}) collective-permute-start(bf16[24,1280]{1,0:T(8,128)(2,1)S(1)} %dynamic-slice_bitcast_fusion.19), channel_id=1, source_target_pairs={{0,4},{1,5},{2,6},{3,7},{4,0},{5,1},{6,2},{7,3},{8,12},{9,13},{10,... | collective-permute-start | bytes 184328 | tf_op jit(solution)/shard_map/ppermute | solution.py:539
  (134 other events, 962.3 us)
Sparse Core Ops, SparseCore 0:
  11.6 81.5 all-gather.2
  96.8 85.8 all-gather.4

commit v4 on v3

--- a/solution.py
+++ b/solution.py
@@ -252,19 +252,19 @@
     vt[1] = turned[HD:128]
     vt[2] = whole[:, 256:384].astype(F32).T.astype(BF)[HD:128]
 
-    def one_head(head, carry):
-        for i in range(MEM + 1):
-            a, b = i * ROWS, (i + 1) * ROWS
-            scores = product_right(ka[head], qa[head, a:b, :])
-            top = jnp.max(scores, axis=0, keepdims=True)
-            scores = jnp.exp(scores - top)
-            total = jnp.sum(scores, axis=0, keepdims=True)
-            mixed = product(vt[head], (scores * (1.0 / total)).astype(BF))
-            ot[pl.ds(pl.multiple_of(head * HD, HD), HD), a:b] = mixed
-            lse[head, 0:1, a:b] = top + jnp.log(total)
+    def one_block(step, carry):
+        head = step // (MEM + 1)
+        here = pl.ds(pl.multiple_of((step % (MEM + 1)) * ROWS, ROWS), ROWS)
+        scores = product_right(ka[head], qa[head, here, :])
+        top = jnp.max(scores, axis=0, keepdims=True)
+        scores = jnp.exp(scores - top)
+        total = jnp.sum(scores, axis=0, keepdims=True)
+        mixed = product(vt[head], (scores * (1.0 / total)).astype(BF))
+        ot[pl.ds(pl.multiple_of(head * HD, HD), HD), here] = mixed
+        lse[head, 0:1, here] = top + jnp.log(total)
         return carry
 
-    lax.fori_loop(0, HEADS, one_head, 0)
+    lax.fori_loop(0, HEADS * (MEM + 1), one_block, 0)
     forward_finish(scal, ot, out, (o0, o1, o2, o3), otail)
 
 
@@ -291,22 +291,22 @@
     dv[...] = jnp.zeros_like(dv)
     dqt[HEADS * HD :, :] = jnp.zeros((HD, WIDE), F32)
 
-    def one_head(head, carry):
+    def one_block(step, carry):
+        head = step // (MEM + 1)
         side = jnp.where(head == 2, 1, 0)
-        for i in range(MEM + 1):
-            a, b = i * ROWS, (i + 1) * ROWS
-            grad = dm[head, a:b, :]
-            scores = product_right(ka[head], qa[head, a:b, :])
-            probs = jnp.exp(scores - lse[head, 0:1, a:b])
-            slopes = product_right(vm[head], grad)
-            slopes = (probs * (slopes - delta[head, 0:1, a:b])).astype(BF)
-            dv[side] += product(probs.astype(BF), grad)
-            dk[side] += product(slopes, qm[head, a:b, :])
-            change = product(kt[head], slopes)
-            dqt[pl.ds(pl.multiple_of(head * HD, HD), HD), a:b] = change * 0.125
+        here = pl.ds(pl.multiple_of((step % (MEM + 1)) * ROWS, ROWS), ROWS)
+        grad = dm[head, here, :]
+        scores = product_right(ka[head], qa[head, here, :])
+        probs = jnp.exp(scores - lse[head, 0:1, here])
+        slopes = product_right(vm[head], grad)
+        slopes = (probs * (slopes - delta[head, 0:1, here])).astype(BF)
+        dv[side] += product(probs.astype(BF), grad)
+        dk[side] += product(slopes, qm[head, here, :])
+        change = product(kt[head], slopes)
+        dqt[pl.ds(pl.multiple_of(head * HD, HD), HD), here] = change * 0.125
         return carry
 
-    lax.fori_loop(0, HEADS, one_head, 0)
+    lax.fori_loop(0, HEADS * (MEM + 1), one_block, 0)
     for i in range(MEM + 1):
         a, b = i * ROWS, (i + 1) * ROWS
         out[a:b, :] = dqt[:, a:b].T.astype(BF)
@@ -396,11 +396,9 @@
     return lax.ppermute(value, LINE, [(s, s + MEM) for s in range(count - MEM)])
 
 
-def spread(member, rows, width):
-    return [
-        swap(lax.dynamic_slice_in_dim(rows, (member ^ j) * width, width, axis=1), j)
-        for j in range(MEM)
-    ]
+def spread(member, rows):
+    parts = [jnp.pad(rows[:, 192 * m : 192 * m + 192], ((0, 0), (0, 64))) for m in range(MEM)]
+    return [swap(lax.select_n(member, *[parts[m ^ j] for m in range(MEM)]), j) for j in range(MEM)]
 
 
 def with_tail(member, pieces):
@@ -413,7 +411,7 @@
         lax.select_n(member, *pieces), LINE, [(s, s - MEM) for s in range(MEM, count, 2)]
     )
     odd = lax.ppermute(even, LINE, [(s, s + 1) for s in range(0, count, 2)])
-    return jnp.where(member % 2 == 0, even, odd)
+    return (jnp.where(member % 2 == 0, even, odd), even)
 
 
 def total_rows(member, partial):
@@ -431,9 +429,9 @@
     return pieces[0] + other[:ROWS] + swap(far, 2).astype(F32)
 
 
-def join(member, pieces):
+def join(member, pieces, width):
     return jnp.concatenate(
-        [lax.select_n(member, *[pieces[s ^ m] for m in range(MEM)]) for s in range(MEM)], axis=1
+        [lax.select_n(member, *[pieces[s ^ m][:, :width] for m in range(MEM)]) for s in range(MEM)], axis=1
     )
 
 
@@ -443,72 +441,69 @@
     for j in range(MEM):
         piece = pieces[j].astype(F32) + jnp.where(member == j, late.astype(F32), 0.0)
         whole.append(swap(piece.astype(BF), j))
-    return join(member, whole)
-
-
-def self_columns(query, key, value, gains):
-    parts = []
+    return join(member, whole, 192)
+
+
+def pack_kernel(query, key, value, gains, so, co, cq, ck, cv, up, down, own, second, third):
+    rows = query.shape[0]
     for m in range(MEM):
         a = 192 * m
-        for matrix in (query, key, value):
-            parts.append(matrix[:, a : a + 128])
-        parts += [query[:, a + 128 : a + 192], key[:, a + 128 : a + 192], value[:, a + 128 : a + 192]]
-        parts += [gains, jnp.zeros((query.shape[0], 60), query.dtype)]
-    return jnp.concatenate(parts, axis=1)
-
-
-def self_columns_back(matrix):
-    parts = [[], [], []]
-    for m in range(MEM):
-        a = 640 * m
-        for n in range(3):
-            parts[n] += [matrix[:, a + 128 * n : a + 128 * n + 128], matrix[:, a + 384 + 64 * n : a + 448 + 64 * n]]
-    return [jnp.concatenate(part, axis=1) for part in parts]
-
-
-def query_columns(matrix):
-    zero = jnp.zeros((matrix.shape[0], 64), matrix.dtype)
-    parts = []
-    for m in range(MEM):
-        parts += [matrix[:, 192 * m : 192 * m + 192], zero]
-    return jnp.concatenate(parts, axis=1)
-
-
-def query_columns_back(matrix):
-    return jnp.concatenate([matrix[:, 256 * m : 256 * m + 192] for m in range(MEM)], axis=1)
-
-
-def frame_columns(key, value):
-    parts = []
+        for n, matrix in enumerate((query, key, value)):
+            own[m, :, 128 * n : 128 * n + 128] = matrix[:, a : a + 128]
+        own[m, :, 384:512] = jnp.concatenate([query[:, a + 128 : a + 192], key[:, a + 128 : a + 192]], axis=1)
+        own[m, :, 512:640] = jnp.concatenate([value[:, a + 128 : a + 192], gains[:, 0:64]], axis=1)
+        b = 3 * D + 384 * m
+        second[:, b : b + 128] = ck[:, a : a + 128]
+        second[:, b + 128 : b + 256] = cv[:, a : a + 128]
+        second[:, b + 256 : b + 384] = jnp.concatenate([ck[:, a + 128 : a + 192], cv[:, a + 128 : a + 192]], axis=1)
+    for n, matrix in enumerate((so, co, cq)):
+        second[:, D * n : D * n + D] = matrix[...]
+    for c in range(FF // D):
+        third[c * rows : (c + 1) * rows, :] = up[:, c * D : (c + 1) * D]
+    third[4 * rows :, :] = down[...]
+
+
+def pack(*args):
+    rows = args[0].shape[0]
+    full = pl.BlockSpec(memory_space=pltpu.VMEM)
+    return pl.pallas_call(
+        pack_kernel,
+        out_shape=[shape(MEM, rows, 640), shape(rows, 3 * D + 1536), shape(8 * rows, D)],
+        in_specs=[full] * len(args),
+        out_specs=[full] * 3,
+    )(*args)
+
+
+def unpack_kernel(scal, p0, p1, p2, p3, query, key, value, ck, cv, gains, sets):
+    for j, piece in enumerate((p0, p1, p2, p3)):
+        sets[scal[j]] = piece[...].astype(F32)
+    total = jnp.zeros_like(gains)
     for m in range(MEM):
         a = 192 * m
-        parts += [key[:, a : a + 128], value[:, a : a + 128], key[:, a + 128 : a + 192], value[:, a + 128 : a + 192]]
-    return jnp.concatenate(parts, axis=1)
-
-
-def frame_columns_back(matrix):
-    key, value = ([], [])
-    for m in range(MEM):
-        a = 384 * m
-        key += [matrix[:, a : a + 128], matrix[:, a + 256 : a + 320]]
-        value += [matrix[:, a + 128 : a + 256], matrix[:, a + 320 : a + 384]]
-    return [jnp.concatenate(key, axis=1), jnp.concatenate(value, axis=1)]
-
-
-def head_rows(matrix):
-    zero = jnp.zeros((64, matrix.shape[1]), matrix.dtype)
-    parts = []
-    for m in range(MEM):
-        parts += [matrix[192 * m : 192 * m + 192], zero]
-    return jnp.concatenate(parts, axis=0)
-
-
-def head_rows_back(matrix):
-    return jnp.concatenate([matrix[256 * m : 256 * m + 192] for m in range(MEM)], axis=0)
-
-
-def column_blocks(matrix):
-    return [matrix[:, c * D : (c + 1) * D] for c in range(FF // D)]
+        for n, out in enumerate((query, key, value)):
+            out[:, a : a + 128] = sets[m, :, 128 * n : 128 * n + 128]
+        last = sets[m, :, 512:640]
+        query[:, a + 128 : a + 192] = sets[m, :, 384:448]
+        key[:, a + 128 : a + 192] = sets[m, :, 448:512]
+        value[:, a + 128 : a + 192] = last[:, 0:64]
+        total = total + last
+        ck[:, a : a + 128] = sets[m, :, 640:768]
+        cv[:, a : a + 128] = sets[m, :, 768:896]
+        ck[:, a + 128 : a + 192] = sets[m, :, 896:960]
+        cv[:, a + 128 : a + 192] = sets[m, :, 960:1024]
+    gains[...] = total
+
+
+def unpack(scal, pieces):
+    rows = pieces[0].shape[0]
+    full = pl.BlockSpec(memory_space=pltpu.VMEM)
+    return pl.pallas_call(
+        unpack_kernel,
+        out_shape=[shape(rows, D, dtype=F32)] * 5 + [shape(rows, 128, dtype=F32)],
+        in_specs=[pl.BlockSpec(memory_space=pltpu.SMEM)] + [full] * MEM,
+        out_specs=[full] * 6,
+        scratch_shapes=[vmem(MEM, rows, 1024, dtype=F32)],
+    )(scal, *pieces)
 
 
 def gather(matrix):
@@ -568,21 +563,18 @@
 def gather_own(member, shard, width):
     devices = lax.axis_size("fsdp") * lax.axis_size("grp") * MEM
     here = lax.axis_index(ALL)
-    pieces = spread(member, shard, width)
+    pieces = [swap(lax.dynamic_index_in_dim(shard, member ^ j, keepdims=False), j) for j in range(MEM)]
     value = jnp.stack([lax.select_n(member, *[pieces[s ^ m] for m in range(MEM)]) for s in range(MEM)])
     for bit in range(2, devices.bit_length() - 1):
         mine = ((here >> bit) & 1) == 0
         came = lax.ppermute(value, ALL, [(s, s ^ (1 << bit)) for s in range(devices)])
         value = jnp.concatenate([jnp.where(mine, value, came), jnp.where(mine, came, value)])
-    return value.reshape(devices * shard.shape[0], width)
+    return value.reshape(devices * shard.shape[1], width)
 
 
 def own_sets(member, value):
     value = value.reshape(MEM, *value.shape[2:])
-    pieces = [
-        swap(lax.dynamic_index_in_dim(value, member ^ j, keepdims=False), j) for j in range(MEM)
-    ]
-    return [lax.select_n(member, *[pieces[s ^ m] for m in range(MEM)]).astype(F32) for s in range(MEM)]
+    return [swap(lax.dynamic_index_in_dim(value, member ^ j, keepdims=False), j) for j in range(MEM)]
 
 
 def moments(states):
@@ -613,24 +605,27 @@
     ]).astype(jnp.int32)
 
     gains = jnp.stack([gain_self, gain_cross, gain_feed, gain_final], axis=1)
-    w_own = gather_own(member, self_columns(self_query, self_key, self_value, gains), 640)
+    gains = jnp.pad(gains, ((0, 0), (0, 124)))
+    own_part, second, third = pack(
+        self_query, self_key, self_value, gains, self_output, cross_output,
+        cross_query, cross_key, cross_value, feed_up, feed_down,
+    )
+    w_own = gather_own(member, own_part, 640)
     two = swap(tokens, 2)
     other = swap(jnp.concatenate([tokens, two], axis=0), 1)
     near_tokens = [tokens, other[:ROWS], two, other[ROWS:]]
-    near_tokens = jnp.concatenate([*near_tokens, token_tail(member, near_tokens)], axis=0)
-    held_frames, two = lax.optimization_barrier((frames, two))
+    tail, even = token_tail(member, near_tokens)
+    near_tokens = jnp.concatenate([*near_tokens, tail], axis=0)
+    held_frames, even = lax.optimization_barrier((frames, even))
     two = swap(held_frames, 2)
-    near_frames = [frames, swap(frames, 1), two, swap(two, 1)]
-    scal, near_frames = lax.optimization_barrier((scal, near_frames))
-    second = gather(jnp.concatenate(
-        [self_output, cross_output, query_columns(cross_query), frame_columns(cross_key, cross_value)], axis=1))
-    third = gather(jnp.concatenate([*column_blocks(feed_up), feed_down], axis=0))
+    near_frames = [swap(held_frames, 1), two]
+    second, third = (gather(second), gather(third))
     third = third.reshape(devices, 2 * FF // devices, D)
     part = D // devices
 
     gain_rows = w_own[:, 512:].T[64:68].astype(F32)
-    w_so, w_co = (head_rows(second[:, :D]), head_rows(second[:, D : 2 * D]))
-    w_cq, w_kv = (second[:, 1536:2560], second[:, 2560:])
+    w_so, w_co = (second[:, :D], second[:, D : 2 * D])
+    w_cq, w_kv = (second[:, 2 * D : 3 * D], second[:, 3 * D :])
     w_up = jnp.concatenate([third[:, c * part : (c + 1) * part].reshape(D, D) for c in range(4)], axis=1)
     w_down = third[:, 4 * part :].reshape(FF, D)
 
@@ -639,6 +634,8 @@
     normed_self = (unit * gain_rows[0]).astype(BF)
     self_rows = product(normed_self, w_own).astype(BF)
     mixed, self_kept = self_forward(scal, self_rows)
+    mixed, near_frames = lax.optimization_barrier((mixed, near_frames))
+    near_frames = [frames, *near_frames, swap(near_frames[1], 1)]
     own_kv = lax.dynamic_slice_in_dim(w_kv, member * 384, 384, axis=1)
     frame_rows = [product(piece, own_kv).astype(BF) for piece in near_frames]
     self_heads = collect(member, mixed)
@@ -646,7 +643,7 @@
     normed_cross, back_cross = jax.vjp(normalize, first_sum, gain_rows[1])
     normed_cross = normed_cross.astype(BF)
     cross_queries = product(normed_cross, w_cq).astype(BF)
-    cross_pieces = with_tail(member, spread(member, cross_queries, 256))
+    cross_pieces = with_tail(member, spread(member, cross_queries))
     mixed, cross_kept = cross_forward(scal, cross_pieces, frame_rows)
     cross_heads = collect(member, mixed)
     second_sum = first_sum + product(cross_heads, w_co)
@@ -664,79 +661,68 @@
     grad_inner = grad_inner.astype(BF)
     grad_up = product_left(normed_feed, grad_inner).astype(BF)
     grad_down = product_left(hidden, grad_feed_out).astype(BF)
-    feed = [Halving(grad_up, False), Halving(grad_down, True)]
-    for chain in feed:
-        chain.send()
+    down = Halving(grad_down, False)
+    down.send()
+    sums_up = lax.psum_scatter(grad_up, ALL, scatter_dimension=0, tiled=True)
     grad_second_part, grad_gain_feed = back_feed(product_right(grad_inner, w_up))
     grad_second = grad_third + grad_second_part
 
     grad_cross_out = grad_second.astype(BF)
     grad_cross_heads = product_right(grad_cross_out, w_co).astype(BF)
-    grad_pieces = with_tail(member, spread(member, grad_cross_heads, 256))
-    for chain in feed:
-        chain.add()
-    held = tie(scal, feed, "away")
-    for chain in feed:
-        chain.send()
+    grad_pieces = with_tail(member, spread(member, grad_cross_heads))
+    down.add()
+    held = tie(scal, [down], "away")
+    down.send()
     query_pieces, frame_grads = cross_backward(held, cross_pieces, frame_rows, grad_pieces, cross_kept)
-    query_pieces = tie(query_pieces, feed, "came")
-    for chain in feed:
-        chain.on()
+    query_pieces, frame_grads = tie((query_pieces, frame_grads), [down], "came")
+    down.on()
     grad_cross_queries = collect(member, query_pieces)
-    grad_cross_queries = tie(grad_cross_queries, feed, "came")
-    for chain in feed:
-        chain.on()
     grad_cq = product_left(normed_cross, grad_cross_queries).astype(BF)
     grad_first_part, grad_gain_cross = back_cross(product_right(grad_cross_queries, w_cq))
     grad_first = grad_second + grad_first_part
 
     grad_self_out = grad_first.astype(BF)
     grad_self_heads = product_right(grad_self_out, w_so).astype(BF)
-    grad_pieces = with_tail(member, spread(member, grad_self_heads, 256))
-    grad_co = head_rows_back(product_left(cross_heads, grad_cross_out)).astype(BF)
-    grad_so = head_rows_back(product_left(self_heads, grad_self_out)).astype(BF)
-    grad_kv = sum(product_left(near_frames[j], frame_grads[j]) for j in range(MEM)).astype(BF)
-    rest = [
-        Halving(jnp.concatenate([grad_so, grad_cq[:, :512]], axis=1), False),
-        Halving(jnp.concatenate([grad_co, grad_cq[:, 512:]], axis=1), True),
-        Halving(grad_kv, True, True),
-    ]
-    held = tie(scal, rest, "away")
-    for chain in rest:
-        chain.send()
-    for chain in feed:
-        chain.add()
-    held = tie(held, feed, "away")
-    for chain in feed:
-        chain.send()
+    grad_pieces = with_tail(member, spread(member, grad_self_heads))
+    grad_co = product_left(cross_heads, grad_cross_out).astype(BF)
+    grad_so = product_left(self_heads, grad_self_out).astype(BF)
+    grad_kv = sum(product_left(near_frames[j], frame_grads[j]) for j in range(MEM))
+    rest = [part.reshape(devices, D // devices, D) for part in (grad_so, grad_co, grad_cq)]
+    rest = Halving(jnp.concatenate(rest, axis=1).reshape(3 * D, D), True)
+    rest.send()
+    down.add()
+    rest.add()
+    held = tie(scal, [down, rest], "away")
+    down.send()
+    rest.send()
     grad_rows = self_backward(held, self_rows, grad_pieces, self_kept)
-    grad_rows = tie(grad_rows, [*rest, *feed], "came")
-    for chain in rest:
-        chain.on()
+    grad_rows = tie(grad_rows, [down, rest], "came")
+    rest.on()
+    down.on()
     grad_normed = product_right(grad_rows, w_own)
     grad_gain_self = jnp.sum(grad_normed * unit, axis=0)
     grad_gains = jnp.stack([grad_gain_self, grad_gain_cross, grad_gain_feed, grad_gain_final])
     grad_gains = jnp.pad(grad_gains, ((64, 60), (0, 0))).T
     grad_qkv = product_left(normed_self, grad_rows)
     grad_qkv = jnp.concatenate([grad_qkv[:, :512], grad_qkv[:, 512:] + grad_gains], axis=1).astype(BF)
-    own = Halving(grad_qkv, False, True)
+    own = Halving(jnp.concatenate([grad_qkv, grad_kv.astype(BF)], axis=1), False, True)
     own.send()
     total = total_rows(member, grad_normed)
     _, back_self = jax.vjp(normalize, states, gain_rows[0])
     tokens_gradient = grad_first + back_self(total)[0]
-    frame_grad = join(member, [swap(frame_grads[j], j) for j in range(MEM)])
+    frame_grad = join(member, [swap(frame_grads[j], j) for j in range(MEM)], 384)
     frames_gradient = product_right(frame_grad, w_kv)
 
-    sums_up, sums_down = [chain.finish() for chain in feed]
+    sums_down = down.finish()
     for _ in range(8):
-        for chain in (*rest, own):
-            chain.on()
-    sums_out, sums_mix, kv = [chain.finish() for chain in rest]
-    sets = own_sets(member, jnp.concatenate([own.finish(), kv], axis=-1))
-    gains_out = sum(part[:, 576:580] for part in sets).T
-    query, key, value = self_columns_back(jnp.concatenate([part[:, :640] for part in sets], axis=1))
-    cross_k, cross_v = frame_columns_back(jnp.concatenate([part[:, 640:] for part in sets], axis=1))
-    grad_cq = jnp.concatenate([sums_out[:, D:], sums_mix[:, D:]], axis=1)
+        rest.on()
+        own.on()
+    sums_rest = rest.finish()
+    last, sums_up = lax.optimization_barrier((own.finish(), sums_up))
+    sets = own_sets(member, last)
+    sums_up = sums_up.astype(F32)
+    query, key, value, cross_k, cross_v, gains_out = unpack(scal, sets)
+    gains_out = gains_out.T[64:68]
     return (
         result.astype(BF),
         tokens_gradient,
@@ -748,11 +734,11 @@
         query,
         key,
         value,
-        sums_out[:, :D],
-        query_columns_back(grad_cq),
+        sums_rest[:part],
+        sums_rest[2 * part :],
         cross_k,
         cross_v,
-        sums_mix[:, :D],
+        sums_rest[part : 2 * part],
         sums_up,
         sums_down,
     )

time: 518 us -> 445 us (0.86)
  waiting for transfers between devices: 170 us -> 142 us
  local copies, waits for them, and re-layouts: 63.9 us -> 37 us
  starting transfers between devices: 92.7 us -> 78.1 us
  Pallas kernels: 68.4 us -> 75 us
    ppermute x26 -> x13, waiting for transfers between devices: 47.5 us -> 22.2 us  [send(): lax.ppermute(self.away, ALL, [(s, s ^ 1 << self.bit) for s in range(self....]
    ppermute x26 -> x13, starting transfers between devices: 40 us -> 17.6 us  [send(): lax.ppermute(self.away, ALL, [(s, s ^ 1 << self.bit) for s in range(self....]
    ppermute x35, waiting for transfers between devices: 43.6 us -> 60.2 us  [swap(): return lax.ppermute(value, LINE, [(s, s ^ mask) for s in range(count)])]
    unnamed x200 -> x166, local copies, waits for them, and re-layouts: 23.5 us -> 8.75 us
    ppermute x3, waiting for transfers between devices: 33.7 us -> 20.7 us  [to_previous(): return lax.ppermute(value, LINE, [(s, s - MEM) for s in range(MEM, count)])]
    ppermute x1, waiting for transfers between devices: 12.1 us -> 5.62 us  [token_tail(): lax.ppermute(lax.select_n(member, *pieces), LINE, [(s, s - MEM) for s in...]
    ppermute x4, waiting for transfers between devices: 13.9 us -> 7.98 us  [to_next(): return lax.ppermute(value, LINE, [(s, s + MEM) for s in range(count - MEM)])]
    slice x24 -> x5, local copies, waits for them, and re-layouts: 9.21 us -> 4 us  [the longest x1 1.93 us: shards(): w_cq, w_kv = (second[:, 2 * D:3 * D], second[:, 3 * D:])]
  transfers between devices with their start and end apart: 75 -> 63, of which waited for: 37 -> 30; matrix products, arithmetic and copies ran while one was open for 20% -> 20% of each run, Pallas kernels for 9% -> 17%
where the time goes in v4:
time: 445 us; the launch traced here: 437 us
  waiting for transfers between devices  142 us (32%)
  starting transfers between devices  78.1 us (18%)
  Pallas kernels  75 us (17%)
  matrix products  48.5 us (11%)
  other arithmetic  40.5 us (9%)
  local copies, waits for them, and re-layouts  37 us (8%)
  between operations  15.8 us (4%)
    pallas_call x4, Pallas kernels, call(): pl.pallas_call(kernel, out_shape=outs, in_specs=[pl.BlockSpec(memory_spac...  71.2 us
    ppermute x35, waiting for transfers between devices, swap(): return lax.ppermute(value, LINE, [(s, s ^ mask) for s in range(count)])  60.2 us
    ppermute x35, starting transfers between devices, swap(): return lax.ppermute(value, LINE, [(s, s ^ mask) for s in range(count)])  35.2 us
    ppermute x3, waiting for transfers between devices, gather_own(): came = lax.ppermute(value, ALL, [(s, s ^ 1 << bit) for s in range(devices)])  24.1 us
    dot_general x10, matrix products, product(): return jnp.dot(left, right, preferred_element_type=F32)  22.8 us
    ppermute x13, waiting for transfers between devices, send(): lax.ppermute(self.away, ALL, [(s, s ^ 1 << self.bit) for s in range(self....  22.2 us
    ppermute x3, waiting for transfers between devices, to_previous(): return lax.ppermute(value, LINE, [(s, s - MEM) for s in range(MEM, count)])  20.7 us
    ppermute x13, starting transfers between devices, send(): lax.ppermute(self.away, ALL, [(s, s ^ 1 << self.bit) for s in range(self....  17.6 us
  transfers between devices with their start and end apart: 63, of which 30 were waited for; matrix products, arithmetic and copies ran while one was open for 20% of the time, Pallas kernels for 17%

profile of v4, /device:TPU:0, one launch (start us, length us, event | category | flops | bytes accessed | tf_op | source)
XLA Modules:
  0.0 437.2 jit_solution(5326137906964657467)
XLA Ops:
  23.1 9.1 %collective-permute-done.7 = bf16[4,24,640]{2,1,0:T(8,128)(2,1)S(1)} collective-permute-done((bf16[4,24,640]{2,1,0:T(8,128)(2,1)S(1)}, bf16[4,24,640]{2,1,0:T(8,128)(2,1)S(1)}, u32[]{:S(2)}, u32[]{:S(2)}) %collective-permute-start.7) | collective-permute-done | bytes 122912 | tf_op jit(solution)/shard_map/ppermute | solution.py:570
  45.5 11.8 %collective-permute-done.9 = bf16[16,24,640]{2,1,0:T(8,128)(2,1)S(1)} collective-permute-done((bf16[16,24,640]{2,1,0:T(8,128)(2,1)S(1)}, bf16[16,24,640]{2,1,0:T(8,128)(2,1)S(1)}, u32[]{:S(2)}, u32[]{:S(2)}) %collective-permute-start.9) | collective-permute-done | bytes 491552 | tf_op jit(solution)/shard_map/ppermute | solution.py:570
  57.6 5.6 %collective-permute-done.2 = bf16[256,768]{1,0:T(8,128)(2,1)S(1)} collective-permute-done((bf16[256,768]{1,0:T(8,128)(2,1)S(1)}, bf16[256,768]{1,0:T(8,128)(2,1)S(1)}, u32[]{:S(2)}, u32[]{:S(2)}) %collective-permute-start.2) | collective-permute-done | bytes 393248 | tf_op jit(solution)/shard_map/ppermute | solution.py:410
  70.8 11.3 %shard_map.306 = (bf16[256,256]{1,0:T(8,128)(2,1)}, bf16[256,256]{1,0:T(8,128)(2,1)}, bf16[256,256]{1,0:T(8,128)(2,1)}, bf16[256,256]{1,0:T(8,128)(2,1)}, bf16[2...) custom-call(s32[8]{0:T(128)} %stack.62.scal, bf16[1280,640]{1,0:T(8,128)(2,1)} %convolution_convert_fusion.2.rows), custom_call_target="tpu_custom_call" | custom-call | flops 3221225472 | bytes 4194304 | tf_op jit(solution)/shard_map/pallas_call | solution.py:331
  82.0 9.3 %collective-permute-done.11 = bf16[375,768]{1,0:T(8,128)(2,1)S(1)} collective-permute-done((bf16[375,768]{1,0:T(8,128)(2,1)S(1)}, bf16[375,768]{1,0:T(8,128)(2,1)S(1)}, u32[]{:S(2)}, u32[]{:S(2)}) %collective-permute-start.11) | collective-permute-done | bytes 576032 | tf_op jit(solution)/shard_map/ppermute | solution.py:386
  100.8 4.1 collective-permute-done.14
  105.0 3.9 collective-permute-done.15
  122.8 4.8 %collective-permute-done.17.q2 = bf16[256,256]{1,0:T(8,128)(2,1)S(1)} collective-permute-done((bf16[256,256]{1,0:T(8,128)(2,1)S(1)}, bf16[256,256]{1,0:T(8,128)(2,1)S(1)}, u32[]{:S(2)}, u32[]{:S(2)}) %collective-permute-start.17) | collective-permute-done | bytes 131104 | tf_op jit(solution)/shard_map/ppermute | solution.py:386
  127.6 4.7 %collective-permute-done.18.q3 = bf16[256,256]{1,0:T(8,128)(2,1)S(1)} collective-permute-done((bf16[256,256]{1,0:T(8,128)(2,1)S(1)}, bf16[256,256]{1,0:T(8,128)(2,1)S(1)}, u32[]{:S(2)}, u32[]{:S(2)}) %collective-permute-start.18) | collective-permute-done | bytes 131104 | tf_op jit(solution)/shard_map/ppermute | solution.py:386
  135.6 12.8 %collective-permute-done.19.qtail = bf16[256,256]{1,0:T(8,128)(2,1)S(1)} collective-permute-done((bf16[256,256]{1,0:T(8,128)(2,1)S(1)}, bf16[256,256]{1,0:T(8,128)(2,1)S(1)}, u32[]{:S(2)}, u32[]{:S(2)}) %collective-permute-start.19) | collective-permute-done | bytes 131104 | tf_op jit(solution)/shard_map/ppermute | solution.py:391
  149.1 21.5 %shard_map.307 = (bf16[256,256]{1,0:T(8,128)(2,1)}, bf16[256,256]{1,0:T(8,128)(2,1)}, bf16[256,256]{1,0:T(8,128)(2,1)}, bf16[256,256]{1,0:T(8,128)(2,1)}, bf16[2...) custom-call(s32[8]{0:T(128)} %stack.62.scal, bf16[256,256]{1,0:T(8,128)(2,1)} %get-tuple-element.171.q0, ...), custom_call_target="tpu_custom_call" | custom-call | flops 6442450944 | bytes 4194304 | tf_op jit(solution)/shard_map/pallas_call | solution.py:331
  172.6 5.5 %collective-permute-done.21 = bf16[256,256]{1,0:T(8,128)(2,1)S(1)} collective-permute-done((bf16[256,256]{1,0:T(8,128)(2,1)}, bf16[256,256]{1,0:T(8,128)(2,1)S(1)}, u32[]{:S(2)}, u32[]{:S(2)}) %collective-permute-start.21) | collective-permute-done | bytes 131104 | tf_op jit(solution)/shard_map/ppermute | solution.py:396
  179.3 5.8 %collective-permute-start.23 = (bf16[256,256]{1,0:T(8,128)(2,1)S(1)}, bf16[256,256]{1,0:T(8,128)(2,1)S(1)}, u32[]{:S(2)}, u32[]{:S(2)}) collective-permute-start(bf16[256,256]{1,0:T(8,128)(2,1)S(1)} %get-tuple-element.241), channel_id=1, source_target_pairs={{0,2},{1,3},{2,0},{3,1},{4,6},{5,7},{6,4},{7,5},{8,10},{9,11},{10,... | collective-permute-start | bytes 393224 | tf_op jit(solution)/shard_map/ppermute | solution.py:386
  185.7 3.7 collective-permute-done.23
  200.5 7.7 %multiply_convert_fusion = (bf16[256,3072]{1,0:T(8,128)(2,1)S(1)}, f32[256,3072]{1,0:T(8,128)S(1)}, f32[256,3072]{1,0:T(8,128)S(1)}) fusion(bf16[768,768]{1,0:T(8,128)(2,1)S(1)} %bitcast.206, bf16[768,768]{1,0:T(8,128)(2,1)S(1)} %bitcast.208, bf16[768,768]{1,0:T(8,128)(2,1)S(1)} %bitcast.210, bf16[768,768]{1,0:T(8,128)(2,1)S(1)} %bitcast.204, ...), kind=kOutput, calls=%fused_computation.21 | convolution fusion | flops 1278738432 | bytes 13374464 | tf_op jit(solution)/shard_map/dot_general | solution.py:39
  226.7 3.8 convolution_convert_fusion
  244.3 4.1 collective-permute-done.29.gtail
  249.0 23.6 %shard_map.308 = (bf16[256,256]{1,0:T(8,128)(2,1)}, bf16[256,256]{1,0:T(8,128)(2,1)}, bf16[256,256]{1,0:T(8,128)(2,1)}, bf16[256,256]{1,0:T(8,128)(2,1)}, bf16[2...) custom-call(s32[8]{0:T(128)} %stack.62.scal, ...), custom_call_target="tpu_custom_call" | custom-call | flops 17179869184 | bytes 4194304 | tf_op jit(solution)/shard_map/pallas_call | solution.py:331
  274.3 5.3 %collective-permute-start.31 = (bf16[256,256]{1,0:T(8,128)(2,1)}, bf16[256,256]{1,0:T(8,128)(2,1)S(1)}, u32[]{:S(2)}, u32[]{:S(2)}) collective-permute-start(bf16[256,256]{1,0:T(8,128)(2,1)} %get-tuple-element.112), channel_id=1, source_target_pairs={{0,4},{1,5},{2,6},{3,7},{8,12},{9,13},{10,14},{11,15},{16,20},{17,... | collective-permute-start | bytes 393224 | tf_op jit(solution)/shard_map/ppermute | solution.py:396
  284.1 6.1 %collective-permute-start.33 = (bf16[256,256]{1,0:T(8,128)(2,1)S(1)}, bf16[256,256]{1,0:T(8,128)(2,1)S(1)}, u32[]{:S(2)}, u32[]{:S(2)}) collective-permute-start(bf16[256,256]{1,0:T(8,128)(2,1)S(1)} %get-tuple-element.238), channel_id=1, source_target_pairs={{0,2},{1,3},{2,0},{3,1},{4,6},{5,7},{6,4},{7,5},{8,10},{9,11},{10,... | collective-permute-start | bytes 393224 | tf_op jit(solution)/shard_map/ppermute | solution.py:386
  292.6 10.3 %collective-permute-done.33 = bf16[256,256]{1,0:T(8,128)(2,1)S(1)} collective-permute-done((bf16[256,256]{1,0:T(8,128)(2,1)S(1)}, bf16[256,256]{1,0:T(8,128)(2,1)S(1)}, u32[]{:S(2)}, u32[]{:S(2)}) %collective-permute-start.33) | collective-permute-done | bytes 131104 | tf_op jit(solution)/shard_map/ppermute | solution.py:386
  302.9 3.7 collective-permute-done.34
  317.1 7.1 %collective-permute-done.38.g2 = bf16[256,256]{1,0:T(8,128)(2,1)S(1)} collective-permute-done((bf16[256,256]{1,0:T(8,128)(2,1)S(1)}, bf16[256,256]{1,0:T(8,128)(2,1)S(1)}, u32[]{:S(2)}, u32[]{:S(2)}) %collective-permute-start.38) | collective-permute-done | bytes 131104 | tf_op jit(solution)/shard_map/ppermute | solution.py:386
  324.2 3.6 collective-permute-done.39.g3
  336.6 3.8 collective-permute-done.40.gtail
  341.1 14.9 %shard_map.309 = bf16[1280,640]{1,0:T(8,128)(2,1)} custom-call(s32[8]{0:T(128)} %stack.62.scal, bf16[1280,640]{1,0:T(8,128)(2,1)} %convolution_convert_fusion.2.rows, bf16[256,256]{1,0:T(8,128)(2,1)} %get-tuple-element.155.g0, bf16[256,256]{1,0:T(8,128)(2,1)} %copy-done.49, bf16[256,256]{1,0:T(8,128)(2,1)} %copy-done.50, bf16[256,256]{1,0:T(8,128)(2,1)} %copy-done.51, ...), custom_call_target="tpu_custom_call" | custom-call | flops 8589934592 | bytes 4194304 | tf_op jit(solution)/shard_map/pallas_call | solution.py:331
  357.0 3.3 collective-permute-start.59
  378.7 4.2 collective-permute-start.57
  383.2 5.3 %collective-permute-done.57 = bf16[2,72,768]{2,1,0:T(8,128)(2,1)S(1)} collective-permute-done((bf16[2,72,768]{2,1,0:T(8,128)(2,1)S(1)}, bf16[2,72,768]{2,1,0:T(8,128)(2,1)S(1)}, u32[]{:S(2)}, u32[]{:S(2)}) %collective-permute-start.57) | collective-permute-done | bytes 221216 | tf_op jit(solution)/shard_map/ppermute | solution.py:534
  388.6 3.5 collective-permute-start.58
  397.9 6.7 %collective-permute-done.51 = bf16[2,2,2,24,1024]{4,3,2,1,0:T(8,128)(2,1)S(1)} collective-permute-done((bf16[2,2,2,24,1024]{4,3,2,1,0:T(8,128)(2,1)S(1)}, bf16[2,2,2,24,1024]{4,3,2,1,0:T(8,128)(2,1)S(1)}, u32[]{:S(2)}, u32[]{:S(2)}) %collective-permute-start.51) | collective-permute-done | bytes 393248 | tf_op jit(solution)/shard_map/ppermute | solution.py:534
  408.0 7.2 %collective-permute-done.52 = bf16[2,2,24,1024]{3,2,1,0:T(8,128)(2,1)S(1)} collective-permute-done((bf16[2,2,24,1024]{3,2,1,0:T(8,128)(2,1)S(1)}, bf16[2,2,24,1024]{3,2,1,0:T(8,128)(2,1)S(1)}, u32[]{:S(2)}, u32[]{:S(2)}) %collective-permute-start.52) | collective-permute-done | bytes 196640 | tf_op jit(solution)/shard_map/ppermute | solution.py:534
  (425 shorter events, 183.5 us)
Async XLA Ops:
  7.2 102.8 %all-gather.3.cloned.1.call-start = ((), (), s32[]{:S(2)}) async-start(), calls=%async_computation.1 | async-start | bytes 6082560 | tf_op jit(solution)/shard_map/all_gather | solution.py:510
  10.8 184.3 %all-gather.5.cloned.1.call-start = ((), (), s32[]{:S(2)}) async-start(), calls=%async_computation.2 | async-start | bytes 9732096 | tf_op jit(solution)/shard_map/all_gather | solution.py:510
  11.6 404.4 %reduce-scatter.2.cloned.1.call-start = ((), (), s32[]{:S(2)}) async-start(), calls=%async_computation.3 | async-start | bytes 4866048 | tf_op jit(solution)/shard_map/reduce_scatter | solution.py:666
  15.7 16.9 %collective-permute-start = (bf16[256,768]{1,0:T(8,128)(2,1)}, bf16[256,768]{1,0:T(8,128)(2,1)S(1)}, u32[]{:S(2)}, u32[]{:S(2)}) collective-permute-start(bf16[256,768]{1,0:T(8,128)(2,1)} %param.18), channel_id=1, source_target_pairs={{0,2},{1,3},{2,0},{3,1},{4,6},{5,7},{6,4},{7,5},{8,10},{9,11},{10,... | collective-permute-start | bytes 1179656 | tf_op jit(solution)/shard_map/ppermute | solution.py:386
  19.7 12.4 %collective-permute-start.7 = (bf16[4,24,640]{2,1,0:T(8,128)(2,1)S(1)}, bf16[4,24,640]{2,1,0:T(8,128)(2,1)S(1)}, u32[]{:S(2)}, u32[]{:S(2)}) collective-permute-start(bf16[4,24,640]{2,1,0:T(8,128)(2,1)S(1)} %pad_maximum_fusion.14), channel_id=1, source_target_pairs={{0,4},{1,5},{2,6},{3,7},{4,0},{5,1},{6,2},{7,3},{8,12},{9,13},{10,... | collective-permute-start | bytes 368648 | tf_op jit(solution)/shard_map/ppermute | solution.py:570
  42.3 15.0 %collective-permute-start.9 = (bf16[16,24,640]{2,1,0:T(8,128)(2,1)S(1)}, bf16[16,24,640]{2,1,0:T(8,128)(2,1)S(1)}, u32[]{:S(2)}, u32[]{:S(2)}) collective-permute-start(bf16[16,24,640]{2,1,0:T(8,128)(2,1)S(1)} %pad_maximum_fusion.9), channel_id=1, source_target_pairs={{0,16},{1,17},{2,18},{3,19},{4,20},{5,21},{6,22},{7,23},{8,24},{9,... | collective-permute-start | bytes 1474568 | tf_op jit(solution)/shard_map/ppermute | solution.py:570
  44.1 19.1 %collective-permute-start.2 = (bf16[256,768]{1,0:T(8,128)(2,1)S(1)}, bf16[256,768]{1,0:T(8,128)(2,1)S(1)}, u32[]{:S(2)}, u32[]{:S(2)}) collective-permute-start(bf16[256,768]{1,0:T(8,128)(2,1)S(1)} %get-tuple-element.200), channel_id=1, source_target_pairs={{4,0},{6,2},{12,8},{14,10},{20,16},{22,18},{28,24},{30,26}} | collective-permute-start | bytes 1179656 | tf_op jit(solution)/shard_map/ppermute | solution.py:410
  65.5 25.8 %collective-permute-start.11 = (bf16[375,768]{1,0:T(8,128)(2,1)S(1)}, bf16[375,768]{1,0:T(8,128)(2,1)S(1)}, u32[]{:S(2)}, u32[]{:S(2)}) collective-permute-start(bf16[375,768]{1,0:T(8,128)(2,1)S(1)} %copy-done.17), channel_id=1, source_target_pairs={{0,2},{1,3},{2,0},{3,1},{4,6},{5,7},{6,4},{7,5},{8,10},{9,11},{10,... | collective-permute-start | bytes 1728008 | tf_op jit(solution)/shard_map/ppermute | solution.py:386
  65.6 25.7 %collective-permute-start.10 = (bf16[375,768]{1,0:T(8,128)(2,1)S(1)}, bf16[375,768]{1,0:T(8,128)(2,1)S(1)}, u32[]{:S(2)}, u32[]{:S(2)}) collective-permute-start(bf16[375,768]{1,0:T(8,128)(2,1)S(1)} %copy-done.17), channel_id=1, source_target_pairs={{0,1},{1,0},{2,3},{3,2},{4,5},{5,4},{6,7},{7,6},{8,9},{9,8},{10,11... | collective-permute-start | bytes 1728008 | tf_op jit(solution)/shard_map/ppermute | solution.py:386
  100.6 33.8 %collective-permute-start.20 = (bf16[375,768]{1,0:T(8,128)(2,1)S(1)}, bf16[375,768]{1,0:T(8,128)(2,1)S(1)}, u32[]{:S(2)}, u32[]{:S(2)}) collective-permute-start(bf16[375,768]{1,0:T(8,128)(2,1)S(1)} %collective-permute-done.11), channel_id=1, source_target_pairs={{0,1},{1,0},{2,3},{3,2},{4,5},{5,4},{6,7},{7,6},{8,9},{9,8},{10,11... | collective-permute-start | bytes 1728008 | tf_op jit(solution)/shard_map/ppermute | solution.py:386
  121.6 10.8 %collective-permute-start.18 = (bf16[256,256]{1,0:T(8,128)(2,1)S(1)}, bf16[256,256]{1,0:T(8,128)(2,1)S(1)}, u32[]{:S(2)}, u32[]{:S(2)}) collective-permute-start(bf16[256,256]{1,0:T(8,128)(2,1)S(1)} %get-tuple-element.199), channel_id=1, source_target_pairs={{0,3},{1,2},{2,1},{3,0},{4,7},{5,6},{6,5},{7,4},{8,11},{9,10},{10,... | collective-permute-start | bytes 393224 | tf_op jit(solution)/shard_map/ppermute | solution.py:386
  133.1 15.3 %collective-permute-start.19 = (bf16[256,256]{1,0:T(8,128)(2,1)S(1)}, bf16[256,256]{1,0:T(8,128)(2,1)S(1)}, u32[]{:S(2)}, u32[]{:S(2)}) collective-permute-start(bf16[256,256]{1,0:T(8,128)(2,1)S(1)} %get-tuple-element.170), channel_id=1, source_target_pairs={{4,0},{5,1},{6,2},{7,3},{12,8},{13,9},{14,10},{15,11},{20,16},{21,... | collective-permute-start | bytes 393224 | tf_op jit(solution)/shard_map/ppermute | solution.py:391
  221.3 16.8 %collective-permute-start.25 = (bf16[2,2,2,2,96,768]{5,4,2,3,0,1:T(8,128)(2,1)}, bf16[2,2,2,2,96,768]{5,4,2,3,0,1:T(8,128)(2,1)}, u32[]{:S(2)}, u32[]{:S(2)}) collective-permute-start(bf16[2,2,2,2,96,768]{5,4,2,3,0,1:T(8,128)(2,1)} %bitcast.185), channel_id=1, source_target_pairs={{0,1},{1,0},{2,3},{3,2},{4,5},{5,4},{6,7},{7,6},{8,9},{9,8},{10,11... | collective-permute-start | bytes 7077896 | tf_op jit(solution)/shard_map/ppermute | solution.py:534
  236.6 11.7 %collective-permute-start.29 = (bf16[256,256]{1,0:T(8,128)(2,1)S(1)}, bf16[256,256]{1,0:T(8,128)(2,1)S(1)}, u32[]{:S(2)}, u32[]{:S(2)}) collective-permute-start(bf16[256,256]{1,0:T(8,128)(2,1)S(1)} %get-tuple-element.160), channel_id=1, source_target_pairs={{4,0},{5,1},{6,2},{7,3},{12,8},{13,9},{14,10},{15,11},{20,16},{21,... | collective-permute-start | bytes 393224 | tf_op jit(solution)/shard_map/ppermute | solution.py:391
  243.7 28.9 %collective-permute-start.30 = (bf16[2,2,2,96,768]{4,3,1,2,0:T(8,128)(2,1)}, bf16[2,2,2,96,768]{4,3,1,2,0:T(8,128)(2,1)}, u32[]{:S(2)}, u32[]{:S(2)}) collective-permute-start(bf16[2,2,2,96,768]{4,3,1,2,0:T(8,128)(2,1)} %dynamic-slice_bitcast_fusion), channel_id=1, source_target_pairs={{0,8},{1,9},{2,10},{3,11},{4,12},{5,13},{6,14},{7,15},{8,0},{9,1},... | collective-permute-start | bytes 3538952 | tf_op jit(solution)/shard_map/ppermute | solution.py:534
  272.7 41.8 %collective-permute-start.47 = (bf16[375,384]{1,0:T(8,128)(2,1)}, bf16[375,384]{1,0:T(8,128)(2,1)S(1)}, u32[]{:S(2)}, u32[]{:S(2)}) collective-permute-start(bf16[375,384]{1,0:T(8,128)(2,1)} %get-tuple-element.124), channel_id=1, source_target_pairs={{0,1},{1,0},{2,3},{3,2},{4,5},{5,4},{6,7},{7,6},{8,9},{9,8},{10,11... | collective-permute-start | bytes 864008 | tf_op jit(solution)/shard_map/ppermute | solution.py:386
  279.6 35.8 %collective-permute-start.48 = (bf16[375,384]{1,0:T(8,128)(2,1)}, bf16[375,384]{1,0:T(8,128)(2,1)S(1)}, u32[]{:S(2)}, u32[]{:S(2)}) collective-permute-start(bf16[375,384]{1,0:T(8,128)(2,1)} %get-tuple-element.125), channel_id=1, source_target_pairs={{0,2},{1,3},{2,0},{3,1},{4,6},{5,7},{6,4},{7,5},{8,10},{9,11},{10,... | collective-permute-start | bytes 864008 | tf_op jit(solution)/shard_map/ppermute | solution.py:386
  284.1 18.8 %collective-permute-start.33 = (bf16[256,256]{1,0:T(8,128)(2,1)S(1)}, bf16[256,256]{1,0:T(8,128)(2,1)S(1)}, u32[]{:S(2)}, u32[]{:S(2)}) collective-permute-start(bf16[256,256]{1,0:T(8,128)(2,1)S(1)} %get-tuple-element.238), channel_id=1, source_target_pairs={{0,2},{1,3},{2,0},{3,1},{4,6},{5,7},{6,4},{7,5},{8,10},{9,11},{10,... | collective-permute-start | bytes 393224 | tf_op jit(solution)/shard_map/ppermute | solution.py:386
  290.1 16.4 %collective-permute-start.34 = (bf16[256,256]{1,0:T(8,128)(2,1)S(1)}, bf16[256,256]{1,0:T(8,128)(2,1)S(1)}, u32[]{:S(2)}, u32[]{:S(2)}) collective-permute-start(bf16[256,256]{1,0:T(8,128)(2,1)S(1)} %get-tuple-element.239), channel_id=1, source_target_pairs={{0,3},{1,2},{2,1},{3,0},{4,7},{5,6},{6,5},{7,4},{8,11},{9,10},{10,... | collective-permute-start | bytes 393224 | tf_op jit(solution)/shard_map/ppermute | solution.py:386
  290.8 25.9 %collective-permute-start.49 = (bf16[375,384]{1,0:T(8,128)(2,1)S(1)}, bf16[375,384]{1,0:T(8,128)(2,1)S(1)}, u32[]{:S(2)}, u32[]{:S(2)}) collective-permute-start(bf16[375,384]{1,0:T(8,128)(2,1)S(1)} %copy-done.44), channel_id=1, source_target_pairs={{0,3},{1,2},{2,1},{3,0},{4,7},{5,6},{6,5},{7,4},{8,11},{9,10},{10,... | collective-permute-start | bytes 864008 | tf_op jit(solution)/shard_map/ppermute | solution.py:386
  302.9 27.4 %collective-permute-start.35 = (bf16[2,2,96,768]{3,2,0,1:T(8,128)(2,1)S(1)}, bf16[2,2,96,768]{3,2,0,1:T(8,128)(2,1)S(1)}, u32[]{:S(2)}, u32[]{:S(2)}) collective-permute-start(bf16[2,2,96,768]{3,2,0,1:T(8,128)(2,1)S(1)} %dynamic-slice_bitcast_fusion.3), channel_id=1, source_target_pairs={{0,16},{1,17},{2,18},{3,19},{4,20},{5,21},{6,22},{7,23},{8,24},{9,... | collective-permute-start | bytes 1769480 | tf_op jit(solution)/shard_map/ppermute | solution.py:534
  310.7 20.4 %collective-permute-start.36 = (bf16[2,2,2,2,72,768]{5,4,2,3,1,0:T(8,128)(2,1)S(1)}, bf16[2,2,2,2,72,768]{5,4,2,3,1,0:T(8,128)(2,1)S(1)}, u32[]{:S(2)}, u32[]{:S(2)}) collective-permute-start(bf16[2,2,2,2,72,768]{5,4,2,3,1,0:T(8,128)(2,1)S(1)} %bitcast.200), channel_id=1, source_target_pairs={{0,1},{1,0},{2,3},{3,2},{4,5},{5,4},{6,7},{7,6},{8,9},{9,8},{10,11... | collective-permute-start | bytes 5308424 | tf_op jit(solution)/shard_map/ppermute | solution.py:534
  316.7 11.1 %collective-permute-start.39 = (bf16[256,256]{1,0:T(8,128)(2,1)S(1)}, bf16[256,256]{1,0:T(8,128)(2,1)S(1)}, u32[]{:S(2)}, u32[]{:S(2)}) collective-permute-start(bf16[256,256]{1,0:T(8,128)(2,1)S(1)} %get-tuple-element.193), channel_id=1, source_target_pairs={{0,3},{1,2},{2,1},{3,0},{4,7},{5,6},{6,5},{7,4},{8,11},{9,10},{10,... | collective-permute-start | bytes 393224 | tf_op jit(solution)/shard_map/ppermute | solution.py:386
  328.6 11.9 %collective-permute-start.40 = (bf16[256,256]{1,0:T(8,128)(2,1)S(1)}, bf16[256,256]{1,0:T(8,128)(2,1)S(1)}, u32[]{:S(2)}, u32[]{:S(2)}) collective-permute-start(bf16[256,256]{1,0:T(8,128)(2,1)S(1)} %get-tuple-element.154), channel_id=1, source_target_pairs={{4,0},{5,1},{6,2},{7,3},{12,8},{13,9},{14,10},{15,11},{20,16},{21,... | collective-permute-start | bytes 393224 | tf_op jit(solution)/shard_map/ppermute | solution.py:391
  332.7 23.6 %collective-permute-start.42 = (bf16[2,2,2,72,768]{4,3,1,2,0:T(8,128)(2,1)}, bf16[2,2,2,72,768]{4,3,1,2,0:T(8,128)(2,1)}, u32[]{:S(2)}, u32[]{:S(2)}) collective-permute-start(bf16[2,2,2,72,768]{4,3,1,2,0:T(8,128)(2,1)} %dynamic-slice_bitcast_fusion.1), channel_id=1, source_target_pairs={{0,16},{1,17},{2,18},{3,19},{4,20},{5,21},{6,22},{7,23},{8,24},{9,... | collective-permute-start | bytes 2654216 | tf_op jit(solution)/shard_map/ppermute | solution.py:534
  334.8 21.2 %collective-permute-start.41 = (bf16[2,96,768]{2,1,0:T(8,128)(2,1)}, bf16[2,96,768]{2,1,0:T(8,128)(2,1)S(1)}, u32[]{:S(2)}, u32[]{:S(2)}) collective-permute-start(bf16[2,96,768]{2,1,0:T(8,128)(2,1)} %dynamic-slice_bitcast_fusion.6), channel_id=1, source_target_pairs={{0,2},{1,3},{2,0},{3,1},{4,6},{5,7},{6,4},{7,5},{8,10},{9,11},{10,... | collective-permute-start | bytes 884744 | tf_op jit(solution)/shard_map/ppermute | solution.py:534
  357.0 37.6 %collective-permute-start.59 = (bf16[96,768]{1,0:T(8,128)(2,1)}, bf16[96,768]{1,0:T(8,128)(2,1)}, u32[]{:S(2)}, u32[]{:S(2)}) collective-permute-start(bf16[96,768]{1,0:T(8,128)(2,1)} %dynamic-slice_bitcast_fusion.9), channel_id=1, source_target_pairs={{0,4},{1,5},{2,6},{3,7},{4,0},{5,1},{6,2},{7,3},{8,12},{9,13},{10,... | collective-permute-start | bytes 442376 | tf_op jit(solution)/shard_map/ppermute | solution.py:534
  362.8 14.6 %collective-permute-start.56 = (bf16[2,2,72,768]{3,2,0,1:T(8,128)(2,1)}, bf16[2,2,72,768]{3,2,0,1:T(8,128)(2,1)}, u32[]{:S(2)}, u32[]{:S(2)}) collective-permute-start(bf16[2,2,72,768]{3,2,0,1:T(8,128)(2,1)} %dynamic-slice_bitcast_fusion.4), channel_id=1, source_target_pairs={{0,8},{1,9},{2,10},{3,11},{4,12},{5,13},{6,14},{7,15},{8,0},{9,1},... | collective-permute-start | bytes 1327112 | tf_op jit(solution)/shard_map/ppermute | solution.py:534
  374.3 19.6 %collective-permute-start.50 = (bf16[2,2,2,2,24,1024]{5,4,3,2,1,0:T(8,128)(2,1)S(1)}, bf16[2,2,2,2,24,1024]{5,4,3,2,1,0:T(8,128)(2,1)S(1)}, u32[]{:S(2)}, u32[]{:S(2)}) collective-permute-start(bf16[2,2,2,2,24,1024]{5,4,3,2,1,0:T(8,128)(2,1)S(1)} %dynamic-slice_bitcast_fusion.2), channel_id=1, source_target_pairs={{0,8},{1,9},{2,10},{3,11},{4,12},{5,13},{6,14},{7,15},{8,0},{9,1},... | collective-permute-start | bytes 2359304 | tf_op jit(solution)/shard_map/ppermute | solution.py:534
  383.1 21.8 %collective-permute-start.45 = (bf16[512,768]{1,0:T(8,128)(2,1)S(1)}, bf16[512,768]{1,0:T(8,128)(2,1)S(1)}, u32[]{:S(2)}, u32[]{:S(2)}) collective-permute-start(bf16[512,768]{1,0:T(8,128)(2,1)S(1)} %pad_maximum_fusion.8), channel_id=1, source_target_pairs={{0,1},{1,0},{2,3},{3,2},{4,5},{5,4},{6,7},{7,6},{8,9},{9,8},{10,11... | collective-permute-start | bytes 2359304 | tf_op jit(solution)/shard_map/ppermute | solution.py:386
  404.8 10.4 %collective-permute-start.52 = (bf16[2,2,24,1024]{3,2,1,0:T(8,128)(2,1)S(1)}, bf16[2,2,24,1024]{3,2,1,0:T(8,128)(2,1)S(1)}, u32[]{:S(2)}, u32[]{:S(2)}) collective-permute-start(bf16[2,2,24,1024]{3,2,1,0:T(8,128)(2,1)S(1)} %dynamic-slice_bitcast_fusion.8), channel_id=1, source_target_pairs={{0,4},{1,5},{2,6},{3,7},{4,0},{5,1},{6,2},{7,3},{8,12},{9,13},{10,... | collective-permute-start | bytes 589832 | tf_op jit(solution)/shard_map/ppermute | solution.py:534
  405.9 21.3 %collective-permute-start.46 = (bf16[256,768]{1,0:T(8,128)(2,1)}, bf16[256,768]{1,0:T(8,128)(2,1)}, u32[]{:S(2)}, u32[]{:S(2)}) collective-permute-start(bf16[256,768]{1,0:T(8,128)(2,1)} %fusion.51), channel_id=1, source_target_pairs={{0,2},{1,3},{2,0},{3,1},{4,6},{5,7},{6,4},{7,5},{8,10},{9,11},{10,... | collective-permute-start | bytes 1179656 | tf_op jit(solution)/shard_map/ppermute | solution.py:386
  (112 other events, 1041.3 us)
Sparse Core Ops, SparseCore 0:
  11.6 79.4 all-gather.2
  94.7 86.8 all-gather.4
  234.9 116.1 reduce-scatter.1
